TPU v7x, 128 devices: a whole 4x4x4 slice. The times are simulated.
128 devices in a mesh: group: 8 (over y, core), tile: 16 (over x, z).
Axes of the slice: x: 4, y: 4, z: 4, core: 2. Of those that a mesh axis runs over, the one named last changes fastest.
Arguments:
- embeddings: bfloat16 [49152, 768], P(('group', 'tile')), may hold values from -15 to 15
- clusters: int32 [49152], P(('group', 'tile')), may hold values from 0 to 31, as said below
- cluster_owner: int32 [32], replicated, may hold values from 0 to 7, as said below
Outputs:
- neighbours: bfloat16 [49152, 768], P(('group', 'tile'))
- log_mass: float32 [49152], P(('group', 'tile'))
Inputs may be any that keep to these rules, and one draw needn't show every extreme that they name: Among the 384 rows of one device at most 72 belong to clusters of any one group; in every draw one group has exactly 72 rows on every device. `cluster_owner`: each group owns exactly 4 clusters.
All inputs are finite; a program needn't handle non-finite values.
Results may differ from a plain program's by a relative error of at most 0.034.
Values may be sent and summed in bfloat16 or wider, within the bound.
No kernel may reach another device: no remote copies, remote signals or barrier semaphores. Data moves between devices by JAX's collectives and lax.ppermute only.
A program may use at most 128 MiB of HBM per device.

v0:
```python
import math

import jax
import jax.numpy as jnp
from jax import lax
from jax.sharding import PartitionSpec as P

score_scale = 3.0
penalty = 2.0


def block_scores(queries, query_ids, key_rows, key_ids):
    feature_width = queries.shape[1]
    products = lax.dot_general(
        queries, key_rows, (((1,), (1,)), ((), ())), preferred_element_type=jnp.float32
    )
    differs = (query_ids[:, None] != key_ids[None, :]).astype(jnp.float32)
    return products * (score_scale / math.sqrt(feature_width)) - penalty * differs


def partial_terms(scores, usable, key_rows):
    row_peak = jnp.max(jnp.where(usable, scores, 0.0), axis=1)
    weights = jnp.exp(jnp.where(usable, scores - row_peak[:, None], -jnp.inf))
    row_total = jnp.sum(weights, axis=1)
    weighted = jnp.dot(weights.astype(jnp.bfloat16), key_rows, preferred_element_type=jnp.float32)
    return (row_peak, row_total, weighted)


def combine_terms(former, second):
    row_peak = jnp.maximum(former[0], second[0])
    factor_one = jnp.exp(former[0] - row_peak)
    factor_two = jnp.exp(second[0] - row_peak)
    row_total = former[1] * factor_one + second[1] * factor_two
    weighted = second[2] * factor_two[:, None]
    return (row_peak, row_total, weighted)


def per_device(embeddings, clusters, cluster_owner):
    row_count = embeddings.shape[0]
    feature_width = embeddings.shape[1]
    groups_total = lax.axis_size("group")
    capacity = 3 * row_count // (2 * groups_total)
    slot_count = groups_total * capacity
    cluster_total = cluster_owner.shape[0]
    table_hit = clusters[:, None] == jnp.arange(cluster_total, dtype=jnp.int32)[None, :]
    group_of = jnp.sum(jnp.where(table_hit, cluster_owner[None, :], 0), axis=1)
    same_group = group_of[:, None] == group_of[None, :]
    row_index = jnp.arange(row_count, dtype=jnp.int32)
    earlier = row_index[None, :] < row_index[:, None]
    rank_in = jnp.sum(same_group & earlier, axis=1)
    slot_of = group_of * capacity + rank_in
    slot_index = jnp.arange(slot_count, dtype=jnp.int32)
    placing = slot_index[:, None] == slot_of[None, :]
    outgoing = jnp.dot(
        placing.astype(jnp.bfloat16), embeddings, preferred_element_type=jnp.float32
    ).astype(jnp.bfloat16)
    outgoing_ids = jnp.sum(jnp.where(placing, clusters[None, :] + 1, 0), axis=1) - 1
    arrived, arrived_ids = (
        lax.all_to_all(
            outgoing.reshape(groups_total, capacity, feature_width),
            "group",
            split_axis=0,
            concat_axis=0,
            tiled=True,
        ),
        lax.all_to_all(
            outgoing_ids.reshape(groups_total, capacity),
            "group",
            split_axis=0,
            concat_axis=0,
            tiled=True,
        ),
    )
    queries = arrived.reshape(slot_count, feature_width)
    query_ids = arrived_ids.reshape(slot_count)
    start_state = (
        jnp.zeros((slot_count,), jnp.float32),
        jnp.ones((slot_count,), jnp.float32),
        jnp.zeros((slot_count, feature_width), jnp.float32),
    )
    tile_pos = lax.axis_index("tile")
    query_pos = tile_pos * slot_count + jnp.arange(slot_count, dtype=jnp.int32)
    key_rows = lax.all_gather(queries, "tile", axis=0, tiled=True)
    key_ids = lax.all_gather(query_ids, "tile", axis=0, tiled=True)
    key_pos = jnp.arange(key_rows.shape[0], dtype=jnp.int32)
    scores = block_scores(queries, query_ids, key_rows, key_ids)
    usable = (key_ids[None, :] >= 0) & (key_pos[None, :] != query_pos[:, None])
    partials = combine_terms(start_state, partial_terms(scores, usable, key_rows))
    row_peak, row_total, weighted = partials
    lse_slots = row_peak + jnp.log(row_total)
    neighbour_slots = (weighted / row_total[:, None]).astype(jnp.bfloat16)
    back_rows, back_lse = (
        lax.all_to_all(
            neighbour_slots.reshape(groups_total, capacity, feature_width),
            "group",
            split_axis=0,
            concat_axis=0,
            tiled=True,
        ),
        lax.all_to_all(
            lse_slots.reshape(groups_total, capacity).astype(jnp.bfloat16),
            "group",
            split_axis=0,
            concat_axis=0,
            tiled=True,
        ).astype(jnp.float32),
    )
    flat_rows = back_rows.reshape(slot_count, feature_width)
    neighbours = jnp.take(flat_rows, slot_of, axis=0)
    log_mass = jnp.take(back_lse.reshape(slot_count), slot_of, axis=0).astype(jnp.float32)
    return (neighbours, log_mass)


def solution(mesh):
    placed = (P(("group", "tile"), None), P(("group", "tile")), P())
    return jax.shard_map(
        per_device,
        mesh=mesh,
        in_specs=placed,
        out_specs=(P(("group", "tile"), None), P(("group", "tile"))),
        check_vma=False,
    )
```

profile of v0, /device:TPU:1, one launch (start us, length us, event | category | flops | bytes accessed | tf_op | source)
XLA Modules:
  0.0 218.7 jit_solution(13662327656676615391)
XLA Ops:
  7.2 0.0 all-gather.2.cloned.1.call-start
  7.2 0.8 select_reduce_fusion.2
  8.1 0.2 convert_reduce_fusion
  8.3 0.7 multiply_add_fusion
  9.0 0.6 convolution_convert_fusion
  9.6 19.4 %all_to_all.22 = bf16[8,72,768]{2,1,0:T(8,128)(2,1)} all-to-all(bf16[8,72,768]{2,1,0:T(8,128)(2,1)S(1)} %bitcast.12), channel_id=1, replica_groups=mesh['group'=8,'tile'=16] {'group'}, dimensions={0} | all-to-all | bytes 1769472 | tf_op jit(solution)/shard_map/all_to_all | solution.py:59
  29.0 0.0 all-gather.2.cloned.1.call-update
  29.0 0.2 select_reduce_fusion.1
  29.2 0.7 sub.55
  29.9 4.0 %all-to-all-start = ((s32[8,1,72]{2,1,0:T(1,128)}), s32[8,1,72]{2,1,0:T(1,128)S(1)}, u32[]{:S(2)}, u32[]{:S(2)}) async-start(s32[8,1,72]{2,1,0:T(1,128)} %sub.55), calls=%async_computation | async-start | bytes 8192 | tf_op jit(solution)/shard_map/all_to_all | solution.py:66
  33.9 1.2 dynamic-slice
  35.8 2.6 %all-to-all-done = s32[8,1,72]{2,1,0:T(1,128)S(1)} async-done(((s32[8,1,72]{2,1,0:T(1,128)}), s32[8,1,72]{2,1,0:T(1,128)S(1)}, u32[]{:S(2)}, u32[]{:S(2)}) %all-to-all-start) | async-done | bytes 2336 | tf_op jit(solution)/shard_map/all_to_all | solution.py:66
  38.4 0.5 broadcast.121
  38.9 0.7 reduce.9
  39.6 0.1 reshape.184
  39.7 0.3 dynamic-update-slice
  40.0 63.1 %all-reduce = s32[9216]{0:T(1024)S(1)} all-reduce(s32[9216]{0:T(1024)S(1)} %dynamic-update-slice), channel_id=1, replica_groups=mesh['group'=8,'tile'=16] {'tile'}, use_global_device_ids=true, to_apply=%add | all-reduce | flops 9216 | bytes 73728
  103.1 25.9 %all-gather.2.cloned.1.call-done = bf16[9216,768]{1,0:T(8,128)(2,1)} async-done(((bf16[576,768]{1,0:T(8,128)(2,1)}), bf16[9216,768]{1,0:T(8,128)(2,1)}) %all-gather.2.cloned.1.call-update) | async-done | bytes 14155792 | tf_op jit(solution)/shard_map/all_gather | solution.py:83
  128.9 18.6 %select_reduce_fusion = (f32[576]{0:T(1024)S(1)}, f32[576,9216]{1,0:T(8,128)}) fusion(s32[9216]{0:T(1024)S(1)} %all-reduce, s32[576]{0:T(1024)S(1)} %iota_add_fusion, s32[576]{0:T(1024)S(1)} %reshape.184, pred[9216]{0:T(1024)(128)(4,1)S(1)} %broadcast_compare_fusion, bf16[576,768]{1,0:T(8,128)(2,1)} %bitcast.11, ...), kind=kOutput, calls=%fused_computation.3 | convolution fusion | flops 8196193792 | bytes 36327168 | tf_op jit(solution)/shard_map/dot_general | solution.py:14
  147.6 13.3 %fusion.17 = f32[576]{0:T(1024)S(1)} fusion(f32[576]{0:T(1024)S(1)} %get-tuple-element.6, s32[9216]{0:T(1024)S(1)} %all-reduce, s32[576]{0:T(1024)S(1)} %reshape.184, f32[576,9216]{1,0:T(8,128)} %get-tuple-element.7, s32[576]{0:T(1024)S(1)} %iota_add_fusion, pred[9216]{0:T(1024)(128)(4,1)S(1)} %broadcast_compare_fusion), kind=kLoop, calls=%fused_computation.46 | loop fusion | flops 47775168 | bytes 21288960 | tf_op jit(solution)/shard_map/reduce_sum | solution.py:24
  160.9 0.1 reduce_sum.42
  160.9 0.1 reduce_max.12
  161.0 0.6 copy.5
  161.6 5.0 %all-to-all-start.3 = ((bf16[8,1,72]{2,1,0:T(2,128)(2,1)}), bf16[8,1,72]{2,1,0:T(2,128)(2,1)S(1)}, u32[]{:S(2)}, u32[]{:S(2)}) async-start(bf16[8,1,72]{2,1,0:T(2,128)(2,1)} %copy.5), calls=%async_computation.3 | async-start | bytes 8192 | tf_op jit(solution)/shard_map/all_to_all | solution.py:100
  166.6 24.0 %divide_convert_fusion = bf16[576,768]{1,0:T(8,128)(2,1)} fusion(bf16[9216,768]{1,0:T(8,128)(2,1)} %all-gather.2.cloned.1.call-done, f32[576]{0:T(1024)S(1)} %get-tuple-element.5, f32[576]{0:T(1024)S(1)} %get-tuple-element.4, f32[576,9216]{1,0:T(8,128)} %get-tuple-element.7, f32[576]{0:T(1024)S(1)} %get-tuple-element.6, s32[9216]{0:T(1024)S(1)} %all-reduce, ...), kind=kOutput, calls=%fused_computation.9 | convolution fusion | flops 8202829824 | bytes 36331776 | tf_op jit(solution)/shard_map/dot_general | solution.py:25
  190.6 4.8 %all-to-all-start.2 = ((bf16[8,72,768]{2,1,0:T(8,128)(2,1)}), bf16[8,72,768]{2,1,0:T(8,128)(2,1)S(1)}, u32[]{:S(2)}, u32[]{:S(2)}) async-start(bf16[8,72,768]{2,1,0:T(8,128)(2,1)} %bitcast.3), calls=%async_computation.2 | async-start | bytes 1769472 | tf_op jit(solution)/shard_map/all_to_all | solution.py:93
  195.5 0.1 reshape.167
  195.5 1.9 gather_fusion.1
  197.4 0.6 broadcast_select_fusion.1
  198.0 10.7 %all-to-all-done.2 = bf16[8,72,768]{2,1,0:T(8,128)(2,1)S(1)} async-done(((bf16[8,72,768]{2,1,0:T(8,128)(2,1)}), bf16[8,72,768]{2,1,0:T(8,128)(2,1)S(1)}, u32[]{:S(2)}, u32[]{:S(2)}) %all-to-all-start.2) | async-done | bytes 884768 | tf_op jit(solution)/shard_map/all_to_all | solution.py:93
  208.8 2.2 gather_fusion
  210.9 0.9 broadcast_select_fusion
  (12 shorter events, 0.1 us)
Async XLA Ops:
  7.2 1.8 copy-start
  7.2 121.8 %all-gather.2.cloned.1.call-start = ((), (), s32[]{:S(2)}) async-start(), calls=%async_computation.4 | async-start | bytes 15040512 | tf_op jit(solution)/shard_map/all_gather | solution.py:83
  29.9 8.6 %all-to-all-start = ((s32[8,1,72]{2,1,0:T(1,128)}), s32[8,1,72]{2,1,0:T(1,128)S(1)}, u32[]{:S(2)}, u32[]{:S(2)}) async-start(s32[8,1,72]{2,1,0:T(1,128)} %sub.55), calls=%async_computation | async-start | bytes 8192 | tf_op jit(solution)/shard_map/all_to_all | solution.py:66
  161.6 29.0 %all-to-all-start.3 = ((bf16[8,1,72]{2,1,0:T(2,128)(2,1)}), bf16[8,1,72]{2,1,0:T(2,128)(2,1)S(1)}, u32[]{:S(2)}, u32[]{:S(2)}) async-start(bf16[8,1,72]{2,1,0:T(2,128)(2,1)} %copy.5), calls=%async_computation.3 | async-start | bytes 8192 | tf_op jit(solution)/shard_map/all_to_all | solution.py:100
  190.6 18.1 %all-to-all-start.2 = ((bf16[8,72,768]{2,1,0:T(8,128)(2,1)}), bf16[8,72,768]{2,1,0:T(8,128)(2,1)S(1)}, u32[]{:S(2)}, u32[]{:S(2)}) async-start(bf16[8,72,768]{2,1,0:T(8,128)(2,1)} %bitcast.3), calls=%async_computation.2 | async-start | bytes 1769472 | tf_op jit(solution)/shard_map/all_to_all | solution.py:93
Sparse Core Ops, SparseCore 0:
  29.1 99.7 all-gather.1
where the time goes:
time: 219 us
  blocking collectives  82.4 us (38%)
  matrix products  43.2 us (20%)
  waiting for transfers between devices  39.3 us (18%)
  other arithmetic  17.5 us (8%)
  between operations  14.8 us (7%)
  starting transfers between devices  13.8 us (6%)
  local copies, waits for them, and re-layouts  7.68 us (4%)
    unnamed x1, blocking collectives  63.1 us
    all_gather x1, waiting for transfers between devices, per_device(): key_rows = lax.all_gather(queries, 'tile', axis=0, tiled=True)  25.9 us
    dot_general x1, matrix products, partial_terms(): jnp.dot(weights.astype(jnp.bfloat16), key_rows, preferred_element_type=jn...  24 us
    all_to_all x1, blocking collectives, per_device(): lax.all_to_all(outgoing.reshape(groups_total, capacity, feature_width), '...  19.4 us
    dot_general x1, matrix products, block_scores(): lax.dot_general(queries, key_rows, (((1,), (1,)), ((), ())), preferred_el...  18.6 us
    reduce_sum x1, other arithmetic, partial_terms(): row_total = jnp.sum(weights, axis=1)  13.3 us
    all_to_all x1, waiting for transfers between devices, per_device(): lax.all_to_all(neighbour_slots.reshape(groups_total, capacity, feature_wi...  10.7 us
    all_to_all x1, starting transfers between devices, per_device(): lax.all_to_all(lse_slots.reshape(groups_total, capacity).astype(jnp.bfloa...  4.97 us
  transfers between devices with their start and end apart: 4, of which 3 were waited for; matrix products, arithmetic and copies ran while one was open for 14% of the time, Pallas kernels for 0%

commit v1 on v0

v1 whole, which is shorter than its diff:
```python
import functools
import math

import jax
import jax.numpy as jnp
from jax import lax
from jax.experimental import pallas as pl
from jax.experimental.pallas import tpu as pltpu
from jax.sharding import PartitionSpec as P

score_scale = 3.0
penalty = 2.0
log2e = math.log2(math.e)
ln2 = math.log(2.0)
masked = -1e30
axes = ("group", "tile")
part_rows = 24
parts = 3
packet_rows = 80
block_keys = 192
block_rows = 208
f32 = jnp.float32
bf16 = jnp.bfloat16


def vmem_specs(count):
    return [pl.BlockSpec(memory_space=pltpu.VMEM) for _ in range(count)]


params = pltpu.CompilerParams(vmem_limit_bytes=48 * 1024 * 1024)


def row_facts(clusters_ref, owner_ref, me):
    cluster = clusters_ref[...]
    rows = cluster.shape[1]
    group = jnp.zeros_like(cluster)
    for number in range(owner_ref.shape[0]):
        group = jnp.where(cluster == number, owner_ref[number], group)
    member = lax.broadcasted_iota(jnp.int32, (8, rows), 0) == group
    upper = lax.broadcasted_iota(jnp.int32, (rows, rows), 0) < lax.broadcasted_iota(
        jnp.int32, (rows, rows), 1
    )
    counts = jnp.dot(
        member.astype(f32).astype(bf16), upper.astype(f32).astype(bf16), preferred_element_type=f32
    )
    rank = jnp.sum(jnp.where(member, counts, 0.0), axis=0, keepdims=True).astype(jnp.int32)
    part = (rank >= part_rows).astype(jnp.int32) + (rank >= 2 * part_rows).astype(jnp.int32)
    lane = me * part_rows + rank - part * part_rows
    return cluster, group, rank, part, lane


def hits(count, target):
    shape = (count, target.shape[1])
    return lax.broadcasted_iota(jnp.int32, shape, 0) == target


def ones_at(count, target):
    return hits(count, target).astype(f32).astype(bf16)


def place_kernel(me_ref, owner_ref, clusters_ref, rows_ref, out_ref):
    cluster, group, rank, part, lane = row_facts(clusters_ref, owner_ref, me_ref[0])
    width = rows_ref.shape[1]
    total = out_ref.shape[0]
    placed = jnp.dot(
        ones_at(total, group * packet_rows + rank), rows_ref[...], preferred_element_type=f32
    )
    labels = jnp.where(hits(64, group * 8 + part), (cluster + 1).astype(f32), 0.0).astype(bf16)
    ids = lax.dot_general(
        labels, ones_at(width, lane), (((1,), (1,)), ((), ())), preferred_element_type=f32
    ).astype(bf16)
    source = lax.broadcasted_iota(jnp.int32, (1, 64), 1)
    placed_ids = jnp.dot(
        ones_at(total, (source // 8) * packet_rows + 72 + source % 8), ids, preferred_element_type=f32
    )
    out_ref[...] = (placed + placed_ids).astype(bf16)


def pack_kernel(in_ref, q_ref, *part_refs):
    packets = [in_ref[s].astype(f32) for s in range(8)]
    for p in range(parts):
        rows = [packets[s][p * part_rows : (p + 1) * part_rows] for s in range(8)]
        ids = packets[0][72:80]
        for s in range(1, 8):
            ids = ids + packets[s][72:80]
        at = lax.broadcasted_iota(jnp.int32, ids.shape, 0)
        row = jnp.sum(jnp.where(at == p, ids, 0.0), axis=0, keepdims=True)
        tail = jnp.where(at == 0, row, 0.0)
        block = jnp.concatenate(rows + [tail, jnp.zeros_like(tail)], axis=0).astype(bf16)
        part_refs[p][...] = block
        q_ref[p * block_rows : (p + 1) * block_rows, :] = block


def column_of(row):
    count = block_keys
    wide = row.shape[1]
    eye = lax.broadcasted_iota(jnp.int32, (count, wide), 0) == lax.broadcasted_iota(
        jnp.int32, (count, wide), 1
    )
    return jnp.sum(jnp.where(eye, row, 0.0), axis=1, keepdims=True)


def row_of(column, wide):
    count = column.shape[0]
    eye = lax.broadcasted_iota(jnp.int32, (count, wide), 0) == lax.broadcasted_iota(
        jnp.int32, (count, wide), 1
    )
    return jnp.sum(jnp.where(eye, column, 0.0), axis=0, keepdims=True)


def high_low(value):
    high = value.astype(bf16).astype(f32)
    return high, value - high


def flash_kernel(blocks, chunk, first, own, finish, *refs):
    refs = list(refs)
    q_ref = refs.pop(0)
    key_refs = [refs.pop(0) for _ in blocks]
    if not first:
        m_in, l_in, acc_in = refs.pop(0), refs.pop(0), refs.pop(0)
    if finish:
        out_ref = refs.pop(0)
    else:
        m_out, l_out, acc_out = refs.pop(0), refs.pop(0), refs.pop(0)
    keys = refs.pop(0)
    width = q_ref.shape[1]
    scale = score_scale / math.sqrt(width) * log2e
    id_rows = []
    number = 0
    for ref, count in zip(key_refs, blocks):
        for b in range(count):
            keys[number * block_keys : (number + 1) * block_keys, :] = ref[
                b * block_rows : b * block_rows + block_keys, :
            ]
            ids = ref[b * block_rows + block_keys : (b + 1) * block_rows, 0:256].astype(f32)
            id_rows.append(ids[0:8])
            number += 1
    pieces = []
    for b in range(0, number, 2):
        even = id_rows[b]
        odd = pltpu.roll(id_rows[b + 1], 64, 1)
        pieces += [even[:, 0:128], even[:, 128:256] + odd[:, 0:128], odd[:, 128:256]]
    key_id = jnp.concatenate(pieces, axis=1)[0:1]
    other = jnp.where(key_id == 0.0, masked, -penalty * log2e)
    total_keys = number * block_keys
    for p in range(parts):
        q = q_ref[p * block_rows : p * block_rows + block_keys, :]
        q_ids = q_ref[p * block_rows + block_keys : (p + 1) * block_rows, 0:256].astype(f32)
        q_id = column_of(q_ids[0:1])
        at = slice(p * block_keys, (p + 1) * block_keys)
        if first:
            peak = jnp.zeros((block_keys, 1), f32)
            mass = jnp.full((block_keys, 1), 1.0 if own else 0.0, f32)
            acc = None
        else:
            peak, mass, acc = m_in[at, :], l_in[at, :], acc_in[at, :]
        for start in range(0, total_keys, chunk):
            span = slice(start, start + chunk)
            scores = lax.dot_general(
                q, keys[span, :], (((1,), (1,)), ((), ())), preferred_element_type=f32
            )
            scores = scores * scale + jnp.where(key_id[:, span] == q_id, 0.0, other[:, span])
            if first and own and start <= p * block_keys < start + chunk:
                row = lax.broadcasted_iota(jnp.int32, scores.shape, 0) + (p * block_keys - start)
                scores = jnp.where(row == lax.broadcasted_iota(jnp.int32, scores.shape, 1), masked, scores)
            new_peak = jnp.maximum(peak, jnp.max(scores, axis=1, keepdims=True))
            weights = jnp.exp2(scores - new_peak)
            fade = jnp.exp2(peak - new_peak)
            mass = mass * fade + jnp.sum(weights, axis=1, keepdims=True)
            mixed = jnp.dot(weights.astype(bf16), keys[span, :], preferred_element_type=f32)
            acc = mixed if acc is None else acc * fade + mixed
            peak = new_peak
        if finish:
            safe = jnp.where(mass > 0.0, mass, 1.0)
            out_ref[at, :] = (acc / safe).astype(bf16)
            level = jnp.where(mass > 0.0, peak + jnp.log2(safe), masked)
            high, low = high_low(level)
            pair = [row_of(high, width), row_of(low, width)]
            here = lax.broadcasted_iota(jnp.int32, (16, width), 0)
            tail = jnp.where(here == 2 * p, pair[0], 0.0) + jnp.where(here == 2 * p + 1, pair[1], 0.0)
            tails = tail if p == 0 else tails + tail
        else:
            m_out[at, :], l_out[at, :], acc_out[at, :] = peak, mass, acc
    if finish:
        rows = parts * block_keys
        out_ref[rows : rows + 16, :] = tails.astype(bf16)


def flash(q, key_arrays, state, own, finish):
    width = q.shape[1]
    blocks = [a.shape[0] // block_rows for a in key_arrays]
    total = sum(blocks) * block_keys
    rows = parts * block_keys
    first = state is None
    if finish:
        outs = [jax.ShapeDtypeStruct((rows + 16, width), bf16)]
    else:
        outs = [
            jax.ShapeDtypeStruct((rows, 1), f32),
            jax.ShapeDtypeStruct((rows, 1), f32),
            jax.ShapeDtypeStruct((rows, width), f32),
        ]
    args = [q, *key_arrays] + ([] if first else list(state))
    out = pl.pallas_call(
        functools.partial(flash_kernel, blocks, 1152, first, own, finish),
        out_shape=outs,
        in_specs=vmem_specs(len(args)),
        out_specs=vmem_specs(len(outs)),
        scratch_shapes=[pltpu.VMEM((total, width), bf16)],
        compiler_params=params,
        cost_estimate=pl.CostEstimate(
            flops=4 * rows * total * width,
            transcendentals=rows * total,
            bytes_accessed=2 * total * width + 6 * rows * width,
        ),
        name="flash",
    )(*args)
    return out[0] if finish else tuple(out)


def combine_kernel(m_ref, l_ref, acc_ref, other_ref, out_ref):
    width = acc_ref.shape[1]
    rows = parts * block_keys
    tails = other_ref[rows : rows + 16, :].astype(f32)
    mixes, levels = [], []
    here = lax.broadcasted_iota(jnp.int32, (8, width), 0)
    for p in range(parts):
        at = slice(p * block_keys, (p + 1) * block_keys)
        level = column_of(
            tails[2 * p : 2 * p + 1, 0:256] + tails[2 * p + 1 : 2 * p + 2, 0:256]
        )
        peak = jnp.maximum(m_ref[at, :], level)
        mine = jnp.exp2(m_ref[at, :] - peak)
        theirs = jnp.exp2(level - peak)
        total = l_ref[at, :] * mine + theirs
        mixes.append(
            (acc_ref[at, :] * mine + other_ref[at, :].astype(f32) * theirs) / total
        )
        high, low = high_low((peak + jnp.log2(total)) * ln2)
        tail = jnp.where(here == p, row_of(high, width), 0.0) + jnp.where(
            here == 3 + p, row_of(low, width), 0.0
        )
        levels = tail if p == 0 else levels + tail
    for s in range(8):
        pieces = [m[s * part_rows : (s + 1) * part_rows] for m in mixes] + [levels]
        out_ref[s] = jnp.concatenate(pieces, axis=0).astype(bf16)


def final_kernel(me_ref, owner_ref, clusters_ref, back_ref, rows_ref, mass_ref):
    _, group, rank, part, lane = row_facts(clusters_ref, owner_ref, me_ref[0])
    total = back_ref.shape[0]
    rows_ref[...] = lax.dot_general(
        ones_at(total, group * packet_rows + rank),
        back_ref[...],
        (((0,), (0,)), ((), ())),
        preferred_element_type=f32,
    ).astype(bf16)
    levels = jnp.concatenate(
        [
            back_ref[g * packet_rows + 64 : (g + 1) * packet_rows, 0:256].astype(f32)[8:16]
            for g in range(8)
        ],
        axis=0,
    ).astype(bf16)
    found = jnp.dot(levels, ones_at(256, lane), preferred_element_type=f32)
    chosen = hits(64, group * 8 + part) | hits(64, group * 8 + 3 + part)
    mass_ref[...] = jnp.sum(jnp.where(chosen, found, 0.0), axis=0, keepdims=True)


def links(mesh):
    side = 4

    def number(y, c, x, z):
        return ((y * 2 + c) * side + x) * side + z

    places = [
        (y, c, x, z) for y in range(side) for c in range(2) for x in range(side) for z in range(side)
    ]

    def pairs(move):
        return [(number(*at), number(*move(*at))) for at in places]

    dims = [
        pairs(lambda y, c, x, z: (y, c, x ^ 3, z)),
        pairs(lambda y, c, x, z: (y, c, x, z ^ 1)),
        pairs(lambda y, c, x, z: (y, c, x, z ^ 3)),
    ]
    swap = pairs(lambda y, c, x, z: (y, c ^ 1, x, z))
    groups = []
    for c in range(2):
        for half in range(2):
            for z in range(side):
                groups.append(
                    [
                        number(y, c, 2 * half + (kind ^ half), z)
                        for y in range(side)
                        for kind in range(2)
                    ]
                )
    return dims, swap, groups


def per_device(dims, swap, groups, embeddings, clusters, cluster_owner):
    rows, width = embeddings.shape
    send = lambda a, pairs: lax.ppermute(a, axes, pairs)
    group_axis, tile = lax.axis_index("group"), lax.axis_index("tile")
    x = tile // 4
    kind = ((x + 1) // 2) % 2
    me = ((group_axis // 2) * 2 + kind).astype(jnp.int32).reshape(1)
    cluster_row = clusters.reshape(1, rows)
    smem = pl.BlockSpec(memory_space=pltpu.SMEM)
    packets = pl.pallas_call(
        place_kernel,
        out_shape=jax.ShapeDtypeStruct((8 * packet_rows, width), bf16),
        in_specs=[smem, smem] + vmem_specs(2),
        out_specs=vmem_specs(1)[0],
        compiler_params=params,
        name="place",
    )(me, cluster_owner, cluster_row, embeddings)
    arrived = lax.all_to_all(
        packets.reshape(8, packet_rows, width), axes, 0, 0, axis_index_groups=groups, tiled=True
    )
    q_own, *pieces = pl.pallas_call(
        pack_kernel,
        out_shape=[jax.ShapeDtypeStruct((parts * block_rows, width), bf16)]
        + [jax.ShapeDtypeStruct((block_rows, width), bf16)] * parts,
        in_specs=vmem_specs(1),
        out_specs=vmem_specs(1 + parts),
        compiler_params=params,
        name="pack",
    )(arrived)
    near = [send(pieces[p], dims[p]) for p in range(parts)]
    q_other = send(q_own, swap)
    two = [jnp.concatenate([pieces[p], near[p]], axis=0) for p in range(parts)]
    second = [send(two[p], dims[(p + 1) % 3]) for p in range(parts)]
    third = [send(two[p], dims[(p + 2) % 3]) for p in range(parts)]
    last = [send(second[p], dims[(p + 2) % 3]) for p in range(parts)]
    begin = [q_own] + near + second
    other = flash(q_other, begin, None, False, False)
    mine = flash(q_own, begin, None, True, False)
    other = flash(q_other, third, other, False, False)
    mine = flash(q_own, third, mine, True, False)
    partial = flash(q_other, last, other, False, True)
    mine = flash(q_own, last, mine, True, False)
    theirs = send(partial, swap)
    answers = pl.pallas_call(
        combine_kernel,
        out_shape=jax.ShapeDtypeStruct((8, packet_rows, width), bf16),
        in_specs=vmem_specs(4),
        out_specs=vmem_specs(1)[0],
        compiler_params=params,
        name="combine",
    )(*mine, theirs)
    back = lax.all_to_all(answers, axes, 0, 0, axis_index_groups=groups, tiled=True)
    neighbours, log_mass = pl.pallas_call(
        final_kernel,
        out_shape=[
            jax.ShapeDtypeStruct((rows, width), bf16),
            jax.ShapeDtypeStruct((1, rows), f32),
        ],
        in_specs=[smem, smem] + vmem_specs(2),
        out_specs=vmem_specs(2),
        compiler_params=params,
        name="final",
    )(me, cluster_owner, cluster_row, back.reshape(8 * packet_rows, width))
    return neighbours, log_mass.reshape(rows)


def solution(mesh):
    placed = (P(axes, None), P(axes), P())
    dims, swap, groups = links(mesh)
    return jax.shard_map(
        functools.partial(per_device, dims, swap, groups),
        mesh=mesh,
        in_specs=placed,
        out_specs=(P(axes, None), P(axes)),
        check_vma=False,
    )
```

time: 219 us -> 137 us (0.63)
  blocking collectives: 82.4 us -> 37.2 us
  Pallas kernels: 0 us -> 43.7 us
  matrix products: 43.2 us -> 0 us
  waiting for transfers between devices: 39.3 us -> 20.9 us
  other arithmetic: 17.5 us -> 0.6 us
  starting transfers between devices: 13.8 us -> 28.1 us
  between operations: 14.8 us -> 0.86 us
  local copies, waits for them, and re-layouts: 7.68 us -> 4.99 us
    unnamed x1 -> x0, blocking collectives: 63.1 us -> none
    pallas_call x0 -> x10, Pallas kernels: none -> 43.7 us  [the longest x6 38.5 us: flash(): pl.pallas_call(functools.partial(flash_kernel, blocks, 1152, first, own,...]
    dot_general x3 -> x0, matrix products: 43.2 us -> none  [the longest x1 24 us: partial_terms(): jnp.dot(weights.astype(jnp.bfloat16), key_rows, preferred_element_type=jn...]
    ppermute x0 -> x14, starting transfers between devices: none -> 28.1 us  [per_device(): send = lambda a, pairs: lax.ppermute(a, axes, pairs)]
    all_gather x1 -> x0, waiting for transfers between devices: 25.9 us -> none  [per_device(): key_rows = lax.all_gather(queries, 'tile', axis=0, tiled=True)]
    ppermute x0 -> x14, waiting for transfers between devices: none -> 20.9 us  [per_device(): send = lambda a, pairs: lax.ppermute(a, axes, pairs)]
    all_to_all x1 -> x2, blocking collectives: 19.4 us -> 37.2 us  [the longest x1 19.6 us: per_device(): lax.all_to_all(packets.reshape(8, packet_rows, width), axes, 0, 0, axis_i...]
    reduce_sum x4 -> x0, other arithmetic: 14.5 us -> none  [the longest x1 13.3 us: partial_terms(): row_total = jnp.sum(weights, axis=1)]
  transfers between devices with their start and end apart: 4 -> 14, of which waited for: 3 -> 3; matrix products, arithmetic and copies ran while one was open for 14% -> 0% of each run, Pallas kernels for 0% -> 25%
where the time goes in v1:
time: 137 us; the launch traced here: 136 us
  Pallas kernels  43.7 us (32%)
  blocking collectives  37.2 us (27%)
  starting transfers between devices  28.1 us (21%)
  waiting for transfers between devices  20.9 us (15%)
  local copies, waits for them, and re-layouts  4.99 us (4%)
    pallas_call x6, Pallas kernels, flash(): pl.pallas_call(functools.partial(flash_kernel, blocks, 1152, first, own,...  38.5 us
    ppermute x14, starting transfers between devices, per_device(): send = lambda a, pairs: lax.ppermute(a, axes, pairs)  28.1 us
    ppermute x14, waiting for transfers between devices, per_device(): send = lambda a, pairs: lax.ppermute(a, axes, pairs)  20.9 us
    all_to_all x1, blocking collectives, per_device(): lax.all_to_all(packets.reshape(8, packet_rows, width), axes, 0, 0, axis_i...  19.6 us
    all_to_all x1, blocking collectives, per_device(): lax.all_to_all(answers, axes, 0, 0, axis_index_groups=groups, tiled=True)  17.5 us
    unnamed x13, local copies, waits for them, and re-layouts  4.24 us
  transfers between devices with their start and end apart: 14, of which 3 were waited for; matrix products, arithmetic and copies ran while one was open for 0% of the time, Pallas kernels for 25%

profile of v1, /device:TPU:1, one launch (start us, length us, event | category | flops | bytes accessed | tf_op | source)
XLA Modules:
  0.0 136.2 jit_solution(7695825021897486246)
XLA Ops:
  0.7 0.7 reshape.20.clusters_ref
  1.4 1.1 copy-done
  2.4 0.7 copy-done.1
  3.1 2.1 %place.1 = bf16[640,768]{1,0:T(8,128)(2,1)S(1)} custom-call(s32[1]{0:T(128)} %bitcast.me_ref, s32[32]{0:T(128)S(1)} %copy-done.1, s32[1,384]{1,0:T(1,128)S(1)} %reshape.20.clusters_ref, bf16[384,768]{1,0:T(8,128)(2,1)S(1)} %copy-done), custom_call_target="tpu_custom_call" | custom-call | tf_op jit(solution)/shard_map/place/pallas_call | solution.py:313
  5.2 19.6 %all_to_all.10.in_ref = bf16[8,80,768]{2,1,0:T(8,128)(2,1)S(1)} all-to-all(bf16[8,80,768]{2,1,0:T(8,128)(2,1)S(1)} %bitcast.4), channel_id=1, replica_groups={{0,4,32,36,64,68,96,100},{1,5,33,37,65,69,97,101},{2,6,34,38,66,70,98,1..., dimensions={0} | all-to-all | bytes 1966080 | tf_op jit(solution)/shard_map/all_to_all | solution.py:321
  24.8 0.1 pack.1
  24.9 3.8 %collective-permute-start.6 = (bf16[208,768]{1,0:T(8,128)(2,1)S(1)}, bf16[208,768]{1,0:T(8,128)(2,1)S(1)}, u32[]{:S(2)}, u32[]{:S(2)}) collective-permute-start(bf16[208,768]{1,0:T(8,128)(2,1)S(1)} %get-tuple-element.26), channel_id=1, source_target_pairs={{0,3},{1,2},{2,1},{3,0},{4,7},{5,6},{6,5},{7,4},{8,11},{9,10},{10,... | collective-permute-start | bytes 958472 | tf_op jit(solution)/shard_map/ppermute | solution.py:306
  28.7 1.8 %collective-permute-start = (bf16[208,768]{1,0:T(8,128)(2,1)S(1)}, bf16[208,768]{1,0:T(8,128)(2,1)S(1)}, u32[]{:S(2)}, u32[]{:S(2)}) collective-permute-start(bf16[208,768]{1,0:T(8,128)(2,1)S(1)} %get-tuple-element.24), channel_id=1, source_target_pairs={{0,12},{1,13},{2,14},{3,15},{4,8},{5,9},{6,10},{7,11},{8,4},{9,5},... | collective-permute-start | bytes 958472 | tf_op jit(solution)/shard_map/ppermute | solution.py:306
  30.6 2.7 %collective-permute-start.12 = (bf16[624,768]{1,0:T(8,128)(2,1)S(1)}, bf16[624,768]{1,0:T(8,128)(2,1)S(1)}, u32[]{:S(2)}, u32[]{:S(2)}) collective-permute-start(bf16[624,768]{1,0:T(8,128)(2,1)S(1)} %get-tuple-element.23.refs_0_.refs_1_), channel_id=1, source_target_pairs={{0,16},{1,17},{2,18},{3,19},{4,20},{5,21},{6,22},{7,23},{8,24},{9,... | collective-permute-start | bytes 2875400 | tf_op jit(solution)/shard_map/ppermute | solution.py:306
  33.3 1.1 collective-permute-done.6.refs_4_
  34.5 1.9 %collective-permute-start.7 = (bf16[416,768]{1,0:T(8,128)(2,1)S(1)}, bf16[416,768]{1,0:T(8,128)(2,1)S(1)}, u32[]{:S(2)}, u32[]{:S(2)}) collective-permute-start(bf16[416,768]{1,0:T(8,128)(2,1)S(1)} %constant_dynamic-update-slice_fusion.4), channel_id=1, source_target_pairs={{0,12},{1,13},{2,14},{3,15},{4,8},{5,9},{6,10},{7,11},{8,4},{9,5},... | collective-permute-start | bytes 1916936 | tf_op jit(solution)/shard_map/ppermute | solution.py:306
  36.4 2.5 %collective-permute-start.4 = (bf16[416,768]{1,0:T(8,128)(2,1)S(1)}, bf16[416,768]{1,0:T(8,128)(2,1)S(1)}, u32[]{:S(2)}, u32[]{:S(2)}) collective-permute-start(bf16[416,768]{1,0:T(8,128)(2,1)S(1)} %constant_dynamic-update-slice_fusion.2), channel_id=1, source_target_pairs={{0,3},{1,2},{2,1},{3,0},{4,7},{5,6},{6,5},{7,4},{8,11},{9,10},{10,... | collective-permute-start | bytes 1916936 | tf_op jit(solution)/shard_map/ppermute | solution.py:306
  39.0 1.5 %collective-permute-start.11 = (bf16[416,768]{1,0:T(8,128)(2,1)S(1)}, bf16[416,768]{1,0:T(8,128)(2,1)S(1)}, u32[]{:S(2)}, u32[]{:S(2)}) collective-permute-start(bf16[416,768]{1,0:T(8,128)(2,1)S(1)} %constant_dynamic-update-slice_fusion.4), channel_id=1, source_target_pairs={{0,1},{1,0},{2,3},{3,2},{4,5},{5,4},{6,7},{7,6},{8,9},{9,8},{10,11... | collective-permute-start | bytes 1916936 | tf_op jit(solution)/shard_map/ppermute | solution.py:306
  40.5 10.5 %collective-permute-done.7.refs_7_ = bf16[416,768]{1,0:T(8,128)(2,1)S(1)} collective-permute-done((bf16[416,768]{1,0:T(8,128)(2,1)S(1)}, bf16[416,768]{1,0:T(8,128)(2,1)S(1)}, u32[]{:S(2)}, u32[]{:S(2)}) %collective-permute-start.7) | collective-permute-done | bytes 639008 | tf_op jit(solution)/shard_map/ppermute | solution.py:306
  50.9 1.8 %collective-permute-start.10 = (bf16[416,768]{1,0:T(8,128)(2,1)S(1)}, bf16[416,768]{1,0:T(8,128)(2,1)S(1)}, u32[]{:S(2)}, u32[]{:S(2)}) collective-permute-start(bf16[416,768]{1,0:T(8,128)(2,1)S(1)} %constant_dynamic-update-slice_fusion.2), channel_id=1, source_target_pairs={{0,12},{1,13},{2,14},{3,15},{4,8},{5,9},{6,10},{7,11},{8,4},{9,5},... | collective-permute-start | bytes 1916936 | tf_op jit(solution)/shard_map/ppermute | solution.py:306
  52.8 1.0 collective-permute-start.8
  53.7 1.9 %collective-permute-start.5 = (bf16[416,768]{1,0:T(8,128)(2,1)S(1)}, bf16[416,768]{1,0:T(8,128)(2,1)S(1)}, u32[]{:S(2)}, u32[]{:S(2)}) collective-permute-start(bf16[416,768]{1,0:T(8,128)(2,1)S(1)} %collective-permute-done.4.refs_6_), channel_id=1, source_target_pairs={{0,12},{1,13},{2,14},{3,15},{4,8},{5,9},{6,10},{7,11},{8,4},{9,5},... | collective-permute-start | bytes 1916936 | tf_op jit(solution)/shard_map/ppermute | solution.py:306
  55.7 9.3 %collective-permute-done.11.refs_3_ = bf16[416,768]{1,0:T(8,128)(2,1)S(1)} collective-permute-done((bf16[416,768]{1,0:T(8,128)(2,1)S(1)}, bf16[416,768]{1,0:T(8,128)(2,1)S(1)}, u32[]{:S(2)}, u32[]{:S(2)}) %collective-permute-start.11) | collective-permute-done | bytes 639008 | tf_op jit(solution)/shard_map/ppermute | solution.py:306
  64.9 0.6 collective-permute-start.2
  65.5 8.7 %flash.9 = (f32[576,1]{1,0:T(8,128)S(1)}, f32[576,1]{1,0:T(8,128)S(1)}, f32[576,768]{1,0:T(8,128)}) custom-call(bf16[624,768]{1,0:T(8,128)(2,1)S(1)} %collective-permute-done.12.refs_0_, bf16[624,768]{1,0:T(8,128)(2,1)S(1)} %get-tuple-element.23.refs_0_.refs_1_, bf16[208,768]{1,0:T(8,128)(2,1)S(1)} %collective-permute-done.refs_2_, ...), custom_call_target="tpu_custom_call" | custom-call | flops 4076863488 | bytes 6193152 | tf_op jit(solution)/shard_map/flash/pallas_call | solution.py:205
  74.2 5.8 %flash.10 = (f32[576,1]{1,0:T(8,128)S(1)}, f32[576,1]{1,0:T(8,128)S(1)}, f32[576,768]{1,0:T(8,128)S(1)}) custom-call(bf16[624,768]{1,0:T(8,128)(2,1)S(1)} %collective-permute-done.12.refs_0_, bf16[416,768]{1,0:T(8,128)(2,1)S(1)} %collective-permute-done.9.refs_1_, bf16[416,768]{1,0:T(8,128)(2,1)S(1)} %collective-permute-done.10.refs_2_, ...), custom_call_target="tpu_custom_call" | custom-call | flops 2038431744 | bytes 4423680 | tf_op jit(solution)/shard_map/flash/pallas_call | solution.py:205
  80.0 4.7 %flash.11 = bf16[592,768]{1,0:T(8,128)(2,1)S(1)} custom-call(bf16[624,768]{1,0:T(8,128)(2,1)S(1)} %collective-permute-done.12.refs_0_, bf16[416,768]{1,0:T(8,128)(2,1)S(1)} %collective-permute-done.2.refs_1_, bf16[416,768]{1,0:T(8,128)(2,1)S(1)} %collective-permute-done.5.refs_2_, bf16[416,768]{1,0:T(8,128)(2,1)S(1)} %collective-permute-done.8.refs_3_, ...), custom_call_target="tpu_custom_call" | custom-call | flops 2038431744 | bytes 4423680 | tf_op jit(solution)/shard_map/flash/pallas_call | solution.py:205
  84.8 8.5 %collective-permute-start.13 = (bf16[592,768]{1,0:T(8,128)(2,1)S(1)}, bf16[592,768]{1,0:T(8,128)(2,1)S(1)}, u32[]{:S(2)}, u32[]{:S(2)}) collective-permute-start(bf16[592,768]{1,0:T(8,128)(2,1)S(1)} %flash.11), channel_id=1, source_target_pairs={{0,16},{1,17},{2,18},{3,19},{4,20},{5,21},{6,22},{7,23},{8,24},{9,... | collective-permute-start | bytes 2727944 | tf_op jit(solution)/shard_map/ppermute | solution.py:306
  93.3 7.5 %flash.6 = (f32[576,1]{1,0:T(8,128)S(1)}, f32[576,1]{1,0:T(8,128)S(1)}, f32[576,768]{1,0:T(8,128)S(1)}) custom-call(bf16[624,768]{1,0:T(8,128)(2,1)S(1)} %get-tuple-element.23.refs_0_.refs_1_, bf16[624,768]{1,0:T(8,128)(2,1)S(1)} %get-tuple-element.23.refs_0_.refs_1_, bf16[208,768]{1,0:T(8,128)(2,1)S(1)} %collective-permute-done.refs_2_, ...), custom_call_target="tpu_custom_call" | custom-call | flops 4076863488 | bytes 6193152 | tf_op jit(solution)/shard_map/flash/pallas_call | solution.py:205
  100.8 1.2 copy-done.4
  102.0 5.8 %flash.7 = (f32[576,1]{1,0:T(8,128)S(1)}, f32[576,1]{1,0:T(8,128)S(1)}, f32[576,768]{1,0:T(8,128)S(1)}) custom-call(bf16[624,768]{1,0:T(8,128)(2,1)S(1)} %get-tuple-element.23.refs_0_.refs_1_, bf16[416,768]{1,0:T(8,128)(2,1)S(1)} %collective-permute-done.9.refs_1_, bf16[416,768]{1,0:T(8,128)(2,1)S(1)} %collective-permute-done.10.refs_2_, ...), custom_call_target="tpu_custom_call" | custom-call | flops 2038431744 | bytes 4423680 | tf_op jit(solution)/shard_map/flash/pallas_call | solution.py:205
  107.9 1.2 copy-done.3
  109.1 5.9 %flash.8 = (f32[576,1]{1,0:T(8,128)S(1)}, f32[576,1]{1,0:T(8,128)S(1)}, f32[576,768]{1,0:T(8,128)S(1)}) custom-call(bf16[624,768]{1,0:T(8,128)(2,1)S(1)} %get-tuple-element.23.refs_0_.refs_1_, bf16[416,768]{1,0:T(8,128)(2,1)S(1)} %collective-permute-done.2.refs_1_, bf16[416,768]{1,0:T(8,128)(2,1)S(1)} %collective-permute-done.5.refs_2_, ...), custom_call_target="tpu_custom_call" | custom-call | flops 2038431744 | bytes 4423680 | tf_op jit(solution)/shard_map/flash/pallas_call | solution.py:205
  115.0 0.8 combine.1
  115.8 17.5 %all_to_all.11 = bf16[8,80,768]{2,1,0:T(8,128)(2,1)S(1)} all-to-all(bf16[8,80,768]{2,1,0:T(8,128)(2,1)S(1)} %combine.1), channel_id=1, replica_groups={{0,4,32,36,64,68,96,100},{1,5,33,37,65,69,97,101},{2,6,34,38,66,70,98,1..., dimensions={0} | all-to-all | bytes 1966080 | tf_op jit(solution)/shard_map/all_to_all | solution.py:355
  133.3 2.3 %final.1 = (bf16[384,768]{1,0:T(8,128)(2,1)}, f32[1,384]{1,0:T(1,128)S(1)}) custom-call(s32[1]{0:T(128)} %bitcast.me_ref, s32[32]{0:T(128)S(1)} %copy-done.2, s32[1,384]{1,0:T(1,128)S(1)} %reshape.20.clusters_ref, bf16[640,768]{1,0:T(8,128)(2,1)S(1)} %bitcast.3), custom_call_target="tpu_custom_call" | custom-call | tf_op jit(solution)/shard_map/final/pallas_call | solution.py:356
  135.6 0.6 reduce
  (26 shorter events, 0.3 us)
Async XLA Ops:
  1.4 1.1 copy-start
  2.4 0.7 copy-start.1
  24.9 9.5 %collective-permute-start.6 = (bf16[208,768]{1,0:T(8,128)(2,1)S(1)}, bf16[208,768]{1,0:T(8,128)(2,1)S(1)}, u32[]{:S(2)}, u32[]{:S(2)}) collective-permute-start(bf16[208,768]{1,0:T(8,128)(2,1)S(1)} %get-tuple-element.26), channel_id=1, source_target_pairs={{0,3},{1,2},{2,1},{3,0},{4,7},{5,6},{6,5},{7,4},{8,11},{9,10},{10,... | collective-permute-start | bytes 958472 | tf_op jit(solution)/shard_map/ppermute | solution.py:306
  28.7 7.6 %collective-permute-start.3 = (bf16[208,768]{1,0:T(8,128)(2,1)S(1)}, bf16[208,768]{1,0:T(8,128)(2,1)S(1)}, u32[]{:S(2)}, u32[]{:S(2)}) collective-permute-start(bf16[208,768]{1,0:T(8,128)(2,1)S(1)} %get-tuple-element.25), channel_id=1, source_target_pairs={{0,1},{1,0},{2,3},{3,2},{4,5},{5,4},{6,7},{7,6},{8,9},{9,8},{10,11... | collective-permute-start | bytes 958472 | tf_op jit(solution)/shard_map/ppermute | solution.py:306
  28.7 10.1 %collective-permute-start = (bf16[208,768]{1,0:T(8,128)(2,1)S(1)}, bf16[208,768]{1,0:T(8,128)(2,1)S(1)}, u32[]{:S(2)}, u32[]{:S(2)}) collective-permute-start(bf16[208,768]{1,0:T(8,128)(2,1)S(1)} %get-tuple-element.24), channel_id=1, source_target_pairs={{0,12},{1,13},{2,14},{3,15},{4,8},{5,9},{6,10},{7,11},{8,4},{9,5},... | collective-permute-start | bytes 958472 | tf_op jit(solution)/shard_map/ppermute | solution.py:306
  30.6 23.2 %collective-permute-start.12 = (bf16[624,768]{1,0:T(8,128)(2,1)S(1)}, bf16[624,768]{1,0:T(8,128)(2,1)S(1)}, u32[]{:S(2)}, u32[]{:S(2)}) collective-permute-start(bf16[624,768]{1,0:T(8,128)(2,1)S(1)} %get-tuple-element.23.refs_0_.refs_1_), channel_id=1, source_target_pairs={{0,16},{1,17},{2,18},{3,19},{4,20},{5,21},{6,22},{7,23},{8,24},{9,... | collective-permute-start | bytes 2875400 | tf_op jit(solution)/shard_map/ppermute | solution.py:306
  34.5 16.5 %collective-permute-start.7 = (bf16[416,768]{1,0:T(8,128)(2,1)S(1)}, bf16[416,768]{1,0:T(8,128)(2,1)S(1)}, u32[]{:S(2)}, u32[]{:S(2)}) collective-permute-start(bf16[416,768]{1,0:T(8,128)(2,1)S(1)} %constant_dynamic-update-slice_fusion.4), channel_id=1, source_target_pairs={{0,12},{1,13},{2,14},{3,15},{4,8},{5,9},{6,10},{7,11},{8,4},{9,5},... | collective-permute-start | bytes 1916936 | tf_op jit(solution)/shard_map/ppermute | solution.py:306
  36.4 16.4 %collective-permute-start.4 = (bf16[416,768]{1,0:T(8,128)(2,1)S(1)}, bf16[416,768]{1,0:T(8,128)(2,1)S(1)}, u32[]{:S(2)}, u32[]{:S(2)}) collective-permute-start(bf16[416,768]{1,0:T(8,128)(2,1)S(1)} %constant_dynamic-update-slice_fusion.2), channel_id=1, source_target_pairs={{0,3},{1,2},{2,1},{3,0},{4,7},{5,6},{6,5},{7,4},{8,11},{9,10},{10,... | collective-permute-start | bytes 1916936 | tf_op jit(solution)/shard_map/ppermute | solution.py:306
  38.9 13.8 %collective-permute-start.1 = (bf16[416,768]{1,0:T(8,128)(2,1)S(1)}, bf16[416,768]{1,0:T(8,128)(2,1)S(1)}, u32[]{:S(2)}, u32[]{:S(2)}) collective-permute-start(bf16[416,768]{1,0:T(8,128)(2,1)S(1)} %constant_dynamic-update-slice_fusion), channel_id=1, source_target_pairs={{0,1},{1,0},{2,3},{3,2},{4,5},{5,4},{6,7},{7,6},{8,9},{9,8},{10,11... | collective-permute-start | bytes 1916936 | tf_op jit(solution)/shard_map/ppermute | solution.py:306
  39.0 25.9 %collective-permute-start.11 = (bf16[416,768]{1,0:T(8,128)(2,1)S(1)}, bf16[416,768]{1,0:T(8,128)(2,1)S(1)}, u32[]{:S(2)}, u32[]{:S(2)}) collective-permute-start(bf16[416,768]{1,0:T(8,128)(2,1)S(1)} %constant_dynamic-update-slice_fusion.4), channel_id=1, source_target_pairs={{0,1},{1,0},{2,3},{3,2},{4,5},{5,4},{6,7},{7,6},{8,9},{9,8},{10,11... | collective-permute-start | bytes 1916936 | tf_op jit(solution)/shard_map/ppermute | solution.py:306
  50.9 23.2 %collective-permute-start.10 = (bf16[416,768]{1,0:T(8,128)(2,1)S(1)}, bf16[416,768]{1,0:T(8,128)(2,1)S(1)}, u32[]{:S(2)}, u32[]{:S(2)}) collective-permute-start(bf16[416,768]{1,0:T(8,128)(2,1)S(1)} %constant_dynamic-update-slice_fusion.2), channel_id=1, source_target_pairs={{0,12},{1,13},{2,14},{3,15},{4,8},{5,9},{6,10},{7,11},{8,4},{9,5},... | collective-permute-start | bytes 1916936 | tf_op jit(solution)/shard_map/ppermute | solution.py:306
  52.8 21.4 %collective-permute-start.9 = (bf16[416,768]{1,0:T(8,128)(2,1)S(1)}, bf16[416,768]{1,0:T(8,128)(2,1)S(1)}, u32[]{:S(2)}, u32[]{:S(2)}) collective-permute-start(bf16[416,768]{1,0:T(8,128)(2,1)S(1)} %constant_dynamic-update-slice_fusion), channel_id=1, source_target_pairs={{0,3},{1,2},{2,1},{3,0},{4,7},{5,6},{6,5},{7,4},{8,11},{9,10},{10,... | collective-permute-start | bytes 1916936 | tf_op jit(solution)/shard_map/ppermute | solution.py:306
  52.8 27.2 %collective-permute-start.8 = (bf16[416,768]{1,0:T(8,128)(2,1)S(1)}, bf16[416,768]{1,0:T(8,128)(2,1)S(1)}, u32[]{:S(2)}, u32[]{:S(2)}) collective-permute-start(bf16[416,768]{1,0:T(8,128)(2,1)S(1)} %collective-permute-done.7.refs_7_), channel_id=1, source_target_pairs={{0,1},{1,0},{2,3},{3,2},{4,5},{5,4},{6,7},{7,6},{8,9},{9,8},{10,11... | collective-permute-start | bytes 1916936 | tf_op jit(solution)/shard_map/ppermute | solution.py:306
  53.7 26.3 %collective-permute-start.5 = (bf16[416,768]{1,0:T(8,128)(2,1)S(1)}, bf16[416,768]{1,0:T(8,128)(2,1)S(1)}, u32[]{:S(2)}, u32[]{:S(2)}) collective-permute-start(bf16[416,768]{1,0:T(8,128)(2,1)S(1)} %collective-permute-done.4.refs_6_), channel_id=1, source_target_pairs={{0,12},{1,13},{2,14},{3,15},{4,8},{5,9},{6,10},{7,11},{8,4},{9,5},... | collective-permute-start | bytes 1916936 | tf_op jit(solution)/shard_map/ppermute | solution.py:306
  64.9 15.1 %collective-permute-start.2 = (bf16[416,768]{1,0:T(8,128)(2,1)S(1)}, bf16[416,768]{1,0:T(8,128)(2,1)S(1)}, u32[]{:S(2)}, u32[]{:S(2)}) collective-permute-start(bf16[416,768]{1,0:T(8,128)(2,1)S(1)} %collective-permute-done.1.refs_5_), channel_id=1, source_target_pairs={{0,3},{1,2},{2,1},{3,0},{4,7},{5,6},{6,5},{7,4},{8,11},{9,10},{10,... | collective-permute-start | bytes 1916936 | tf_op jit(solution)/shard_map/ppermute | solution.py:306
  84.8 30.2 %collective-permute-start.13 = (bf16[592,768]{1,0:T(8,128)(2,1)S(1)}, bf16[592,768]{1,0:T(8,128)(2,1)S(1)}, u32[]{:S(2)}, u32[]{:S(2)}) collective-permute-start(bf16[592,768]{1,0:T(8,128)(2,1)S(1)} %flash.11), channel_id=1, source_target_pairs={{0,16},{1,17},{2,18},{3,19},{4,20},{5,21},{6,22},{7,23},{8,24},{9,... | collective-permute-start | bytes 2727944 | tf_op jit(solution)/shard_map/ppermute | solution.py:306
  100.8 1.2 copy-start.4
  107.9 1.2 copy-start.3
  115.8 17.5 %copy-start.2 = (s32[32]{0:T(128)S(1)}, s32[32]{0:T(128)}, u32[]{:S(2)}) copy-start(s32[32]{0:T(128)} %owner_ref.3) | copy-start | bytes 388

commit v2 on v1

--- a/solution.py
+++ b/solution.py
@@ -19,6 +19,7 @@
 packet_rows = 80
 block_keys = 192
 block_rows = 208
+query_rows = 288
 f32 = jnp.float32
 bf16 = jnp.bfloat16
 
@@ -27,7 +28,7 @@
     return [pl.BlockSpec(memory_space=pltpu.VMEM) for _ in range(count)]
 
 
-params = pltpu.CompilerParams(vmem_limit_bytes=48 * 1024 * 1024)
+params = pltpu.CompilerParams(vmem_limit_bytes=32 * 1024 * 1024)
 
 
 def row_facts(clusters_ref, owner_ref, me):
@@ -76,7 +77,7 @@
     out_ref[...] = (placed + placed_ids).astype(bf16)
 
 
-def pack_kernel(in_ref, q_ref, *part_refs):
+def pack_kernel(in_ref, q_ref, big_ref, small_ref):
     packets = [in_ref[s].astype(f32) for s in range(8)]
     for p in range(parts):
         rows = [packets[s][p * part_rows : (p + 1) * part_rows] for s in range(8)]
@@ -87,8 +88,12 @@
         row = jnp.sum(jnp.where(at == p, ids, 0.0), axis=0, keepdims=True)
         tail = jnp.where(at == 0, row, 0.0)
         block = jnp.concatenate(rows + [tail, jnp.zeros_like(tail)], axis=0).astype(bf16)
-        part_refs[p][...] = block
-        q_ref[p * block_rows : (p + 1) * block_rows, :] = block
+        at = slice(p * block_rows, (p + 1) * block_rows)
+        q_ref[at, :] = block
+        if p < 2:
+            big_ref[at, :] = block
+        else:
+            small_ref[...] = block
 
 
 def column_of(row):
@@ -113,19 +118,7 @@
     return high, value - high
 
 
-def flash_kernel(blocks, chunk, first, own, finish, *refs):
-    refs = list(refs)
-    q_ref = refs.pop(0)
-    key_refs = [refs.pop(0) for _ in blocks]
-    if not first:
-        m_in, l_in, acc_in = refs.pop(0), refs.pop(0), refs.pop(0)
-    if finish:
-        out_ref = refs.pop(0)
-    else:
-        m_out, l_out, acc_out = refs.pop(0), refs.pop(0), refs.pop(0)
-    keys = refs.pop(0)
-    width = q_ref.shape[1]
-    scale = score_scale / math.sqrt(width) * log2e
+def gather_keys(key_refs, blocks, keys):
     id_rows = []
     number = 0
     for ref, count in zip(key_refs, blocks):
@@ -141,82 +134,109 @@
         even = id_rows[b]
         odd = pltpu.roll(id_rows[b + 1], 64, 1)
         pieces += [even[:, 0:128], even[:, 128:256] + odd[:, 0:128], odd[:, 128:256]]
-    key_id = jnp.concatenate(pieces, axis=1)[0:1]
+    return jnp.concatenate(pieces, axis=1)[0:1]
+
+
+def flash_kernel(blocks, first, owns, finish, *refs):
+    refs = list(refs)
+    count = len(owns)
+    q_refs = [refs.pop(0) for _ in range(count)]
+    key_refs = [refs.pop(0) for _ in blocks]
+    states = None if first else [[refs.pop(0) for _ in range(3)] for _ in range(count)]
+    outs = [[refs.pop(0)] if finish else [refs.pop(0) for _ in range(3)] for _ in range(count)]
+    keys, queries, labels = refs
+    width = q_refs[0].shape[1]
+    scale = score_scale / math.sqrt(width) * log2e
+    key_id = gather_keys(key_refs, blocks, keys)
     other = jnp.where(key_id == 0.0, masked, -penalty * log2e)
-    total_keys = number * block_keys
-    for p in range(parts):
-        q = q_ref[p * block_rows : p * block_rows + block_keys, :]
-        q_ids = q_ref[p * block_rows + block_keys : (p + 1) * block_rows, 0:256].astype(f32)
-        q_id = column_of(q_ids[0:1])
-        at = slice(p * block_keys, (p + 1) * block_keys)
-        if first:
-            peak = jnp.zeros((block_keys, 1), f32)
-            mass = jnp.full((block_keys, 1), 1.0 if own else 0.0, f32)
-            acc = None
-        else:
-            peak, mass, acc = m_in[at, :], l_in[at, :], acc_in[at, :]
-        for start in range(0, total_keys, chunk):
-            span = slice(start, start + chunk)
+    for n in range(count):
+        for p in range(parts):
+            at = slice(p * block_keys, (p + 1) * block_keys)
+            queries[n, at, :] = q_refs[n][p * block_rows : p * block_rows + block_keys, :]
+            ids = q_refs[n][p * block_rows + block_keys : (p + 1) * block_rows, 0:256]
+            labels[n, at, :] = column_of(ids.astype(f32)[0:1])
+    for n in range(count):
+        for start in range(0, parts * block_keys, query_rows):
+            at = slice(start, start + query_rows)
             scores = lax.dot_general(
-                q, keys[span, :], (((1,), (1,)), ((), ())), preferred_element_type=f32
+                queries[n, at, :], keys[...], (((1,), (1,)), ((), ())), preferred_element_type=f32
             )
-            scores = scores * scale + jnp.where(key_id[:, span] == q_id, 0.0, other[:, span])
-            if first and own and start <= p * block_keys < start + chunk:
-                row = lax.broadcasted_iota(jnp.int32, scores.shape, 0) + (p * block_keys - start)
-                scores = jnp.where(row == lax.broadcasted_iota(jnp.int32, scores.shape, 1), masked, scores)
-            new_peak = jnp.maximum(peak, jnp.max(scores, axis=1, keepdims=True))
-            weights = jnp.exp2(scores - new_peak)
-            fade = jnp.exp2(peak - new_peak)
-            mass = mass * fade + jnp.sum(weights, axis=1, keepdims=True)
-            mixed = jnp.dot(weights.astype(bf16), keys[span, :], preferred_element_type=f32)
-            acc = mixed if acc is None else acc * fade + mixed
-            peak = new_peak
-        if finish:
+            scores = scores * scale + jnp.where(key_id == labels[n, at, :], 0.0, other)
+            if first and owns[n]:
+                row = lax.broadcasted_iota(jnp.int32, scores.shape, 0) + start
+                scores = jnp.where(
+                    row == lax.broadcasted_iota(jnp.int32, scores.shape, 1), masked, scores
+                )
+            highest = jnp.max(scores, axis=1, keepdims=True)
+            if first:
+                peak = jnp.maximum(highest, 0.0)
+            else:
+                former = states[n][0][at, :]
+                peak = jnp.maximum(former, highest)
+                fade = jnp.exp2(former - peak)
+            weights = jnp.exp2(scores - peak)
+            mass = jnp.sum(weights, axis=1, keepdims=True)
+            acc = jnp.dot(weights.astype(bf16), keys[...], preferred_element_type=f32)
+            if not first:
+                mass = mass + states[n][1][at, :] * fade
+                acc = acc + states[n][2][at, :] * fade
+            elif owns[n]:
+                mass = mass + jnp.exp2(-peak)
+            if not finish:
+                outs[n][0][at, :], outs[n][1][at, :], outs[n][2][at, :] = peak, mass, acc
+                continue
             safe = jnp.where(mass > 0.0, mass, 1.0)
-            out_ref[at, :] = (acc / safe).astype(bf16)
-            level = jnp.where(mass > 0.0, peak + jnp.log2(safe), masked)
-            high, low = high_low(level)
-            pair = [row_of(high, width), row_of(low, width)]
-            here = lax.broadcasted_iota(jnp.int32, (16, width), 0)
-            tail = jnp.where(here == 2 * p, pair[0], 0.0) + jnp.where(here == 2 * p + 1, pair[1], 0.0)
-            tails = tail if p == 0 else tails + tail
-        else:
-            m_out[at, :], l_out[at, :], acc_out[at, :] = peak, mass, acc
+            outs[n][0][at, :] = (acc / safe).astype(bf16)
+            labels[n, at, :] = jnp.where(mass > 0.0, peak + jnp.log2(safe), masked)
     if finish:
         rows = parts * block_keys
-        out_ref[rows : rows + 16, :] = tails.astype(bf16)
-
-
-def flash(q, key_arrays, state, own, finish):
-    width = q.shape[1]
+        for n in range(count):
+            here = lax.broadcasted_iota(jnp.int32, (16, width), 0)
+            tails = jnp.zeros((16, width), f32)
+            for p in range(parts):
+                high, low = high_low(labels[n, p * block_keys : (p + 1) * block_keys, :])
+                tails = tails + jnp.where(here == 2 * p, row_of(high, width), 0.0)
+                tails = tails + jnp.where(here == 2 * p + 1, row_of(low, width), 0.0)
+            outs[n][0][rows : rows + 16, :] = tails.astype(bf16)
+
+
+def flash(qs, owns, key_arrays, states, finish):
+    width = qs[0].shape[1]
     blocks = [a.shape[0] // block_rows for a in key_arrays]
     total = sum(blocks) * block_keys
     rows = parts * block_keys
-    first = state is None
+    first = states is None
     if finish:
-        outs = [jax.ShapeDtypeStruct((rows + 16, width), bf16)]
+        each = [jax.ShapeDtypeStruct((rows + 16, width), bf16)]
     else:
-        outs = [
+        each = [
             jax.ShapeDtypeStruct((rows, 1), f32),
             jax.ShapeDtypeStruct((rows, 1), f32),
             jax.ShapeDtypeStruct((rows, width), f32),
         ]
-    args = [q, *key_arrays] + ([] if first else list(state))
+    count = len(qs)
+    args = [*qs, *key_arrays] + ([] if first else [a for state in states for a in state])
     out = pl.pallas_call(
-        functools.partial(flash_kernel, blocks, 1152, first, own, finish),
-        out_shape=outs,
+        functools.partial(flash_kernel, blocks, first, owns, finish),
+        out_shape=each * count,
         in_specs=vmem_specs(len(args)),
-        out_specs=vmem_specs(len(outs)),
-        scratch_shapes=[pltpu.VMEM((total, width), bf16)],
+        out_specs=vmem_specs(len(each) * count),
+        scratch_shapes=[
+            pltpu.VMEM((total, width), bf16),
+            pltpu.VMEM((count, rows, width), bf16),
+            pltpu.VMEM((count, rows, 1), f32),
+        ],
         compiler_params=params,
         cost_estimate=pl.CostEstimate(
-            flops=4 * rows * total * width,
-            transcendentals=rows * total,
-            bytes_accessed=2 * total * width + 6 * rows * width,
+            flops=8 * count * rows * total * width,
+            transcendentals=count * rows * total,
+            bytes_accessed=2 * total * width + 6 * count * rows * width,
         ),
         name="flash",
     )(*args)
-    return out[0] if finish else tuple(out)
+    if finish:
+        return out
+    return [tuple(out[3 * n : 3 * n + 3]) for n in range(count)]
 
 
 def combine_kernel(m_ref, l_ref, acc_ref, other_ref, out_ref):
@@ -321,28 +341,36 @@
     arrived = lax.all_to_all(
         packets.reshape(8, packet_rows, width), axes, 0, 0, axis_index_groups=groups, tiled=True
     )
-    q_own, *pieces = pl.pallas_call(
+    q_own, big, small = pl.pallas_call(
         pack_kernel,
-        out_shape=[jax.ShapeDtypeStruct((parts * block_rows, width), bf16)]
-        + [jax.ShapeDtypeStruct((block_rows, width), bf16)] * parts,
+        out_shape=[
+            jax.ShapeDtypeStruct((count * block_rows, width), bf16) for count in (parts, 2, 1)
+        ],
         in_specs=vmem_specs(1),
-        out_specs=vmem_specs(1 + parts),
+        out_specs=vmem_specs(3),
         compiler_params=params,
         name="pack",
     )(arrived)
-    near = [send(pieces[p], dims[p]) for p in range(parts)]
+    wide = [
+        [pair for pair in dims[s % 3] if pair[0] // 16 % 2 == 0]
+        + [pair for pair in dims[(s + 1) % 3] if pair[0] // 16 % 2 == 1]
+        for s in range(3)
+    ]
+    narrow = [dims[(s + 2) % 3] for s in range(3)]
+    big0, small0 = send(big, wide[0]), send(small, narrow[0])
     q_other = send(q_own, swap)
-    two = [jnp.concatenate([pieces[p], near[p]], axis=0) for p in range(parts)]
-    second = [send(two[p], dims[(p + 1) % 3]) for p in range(parts)]
-    third = [send(two[p], dims[(p + 2) % 3]) for p in range(parts)]
-    last = [send(second[p], dims[(p + 2) % 3]) for p in range(parts)]
-    begin = [q_own] + near + second
-    other = flash(q_other, begin, None, False, False)
-    mine = flash(q_own, begin, None, True, False)
-    other = flash(q_other, third, other, False, False)
-    mine = flash(q_own, third, mine, True, False)
-    partial = flash(q_other, last, other, False, True)
-    mine = flash(q_own, last, mine, True, False)
+    big0, small0 = lax.optimization_barrier((big0, small0))
+    big, small = jnp.concatenate([big, big0], axis=0), jnp.concatenate([small, small0], axis=0)
+    big1, small1 = send(big, wide[1]), send(small, narrow[1])
+    big2, small2 = send(big, wide[2]), send(small, narrow[2])
+    queries, owns = [q_other, q_own], [False, True]
+    states = flash(queries, owns, [q_own, big0, small0], None, False)
+    big1, small1, states[1] = lax.optimization_barrier((big1, small1, states[1]))
+    big3, small3 = send(big1, wide[2]), send(small1, narrow[2])
+    states = flash(queries, owns, [big1, small1], states, False)
+    states = flash(queries, owns, [big2, small2], states, False)
+    (partial,) = flash(queries[:1], owns[:1], [big3, small3], states[:1], True)
+    (mine,) = flash(queries[1:], owns[1:], [big3, small3], states[1:], False)
     theirs = send(partial, swap)
     answers = pl.pallas_call(
         combine_kernel,

time: 137 us -> 112 us (0.82)
  starting transfers between devices: 28.1 us -> 17.8 us
  Pallas kernels: 43.7 us -> 34.7 us
  local copies, waits for them, and re-layouts: 4.99 us -> 2.54 us
  waiting for transfers between devices: 20.9 us -> 18.9 us
    ppermute x14 -> x10, starting transfers between devices: 28.1 us -> 17.8 us  [per_device(): send = lambda a, pairs: lax.ppermute(a, axes, pairs)]
    pallas_call x7 -> x6, Pallas kernels: 38.6 us -> 29.6 us  [the longest x5 29.5 us: flash(): pl.pallas_call(functools.partial(flash_kernel, blocks, first, owns, finis...]
    unnamed x13 -> x8, local copies, waits for them, and re-layouts: 4.24 us -> 1.79 us
    ppermute x14 -> x10, waiting for transfers between devices: 20.9 us -> 18.9 us  [per_device(): send = lambda a, pairs: lax.ppermute(a, axes, pairs)]
  transfers between devices with their start and end apart: 14 -> 10, of which waited for: 3 -> 6; matrix products, arithmetic and copies ran while one was open for 0% -> 0% of each run, Pallas kernels for 25% -> 23%
where the time goes in v2:
time: 112 us
  blocking collectives  36.4 us (32%)
  Pallas kernels  34.7 us (31%)
  waiting for transfers between devices  18.9 us (17%)
  starting transfers between devices  17.8 us (16%)
  local copies, waits for them, and re-layouts  2.54 us (2%)
    pallas_call x5, Pallas kernels, flash(): pl.pallas_call(functools.partial(flash_kernel, blocks, first, owns, finis...  29.5 us
    all_to_all x1, blocking collectives, per_device(): lax.all_to_all(packets.reshape(8, packet_rows, width), axes, 0, 0, axis_i...  19.6 us
    ppermute x10, waiting for transfers between devices, per_device(): send = lambda a, pairs: lax.ppermute(a, axes, pairs)  18.9 us
    ppermute x10, starting transfers between devices, per_device(): send = lambda a, pairs: lax.ppermute(a, axes, pairs)  17.8 us
    all_to_all x1, blocking collectives, per_device(): lax.all_to_all(answers, axes, 0, 0, axis_index_groups=groups, tiled=True)  16.8 us
    pallas_call x1, Pallas kernels, per_device(): pl.pallas_call(final_kernel, out_shape=[jax.ShapeDtypeStruct((rows, width...  2.26 us
  transfers between devices with their start and end apart: 10, of which 6 were waited for; matrix products, arithmetic and copies ran while one was open for 0% of the time, Pallas kernels for 23%

profile of v2, /device:TPU:1, one launch (start us, length us, event | category | flops | bytes accessed | tf_op | source)
XLA Modules:
  0.0 111.7 jit_solution(16614876499307976884)
XLA Ops:
  0.7 0.7 reshape.20.clusters_ref
  1.4 1.1 copy-done
  2.4 0.7 copy-done.1
  3.1 2.1 %place.1 = bf16[640,768]{1,0:T(8,128)(2,1)S(1)} custom-call(s32[1]{0:T(128)} %bitcast.me_ref, s32[32]{0:T(128)S(1)} %copy-done.1, s32[1,384]{1,0:T(1,128)S(1)} %reshape.20.clusters_ref, bf16[384,768]{1,0:T(8,128)(2,1)S(1)} %copy-done), custom_call_target="tpu_custom_call" | custom-call | tf_op jit(solution)/shard_map/place/pallas_call | solution.py:333
  5.2 19.6 %all_to_all.10.in_ref = bf16[8,80,768]{2,1,0:T(8,128)(2,1)S(1)} all-to-all(bf16[8,80,768]{2,1,0:T(8,128)(2,1)S(1)} %bitcast.4), channel_id=1, replica_groups={{0,4,32,36,64,68,96,100},{1,5,33,37,65,69,97,101},{2,6,34,38,66,70,98,1..., dimensions={0} | all-to-all | bytes 1966080 | tf_op jit(solution)/shard_map/all_to_all | solution.py:341
  24.8 0.1 pack.1
  24.9 1.7 %collective-permute-start = (bf16[416,768]{1,0:T(8,128)(2,1)S(1)}, bf16[416,768]{1,0:T(8,128)(2,1)S(1)}, u32[]{:S(2)}, u32[]{:S(2)}) collective-permute-start(bf16[416,768]{1,0:T(8,128)(2,1)S(1)} %get-tuple-element.36), channel_id=1, source_target_pairs={{0,12},{1,13},{2,14},{3,15},{4,8},{5,9},{6,10},{7,11},{8,4},{9,5},... | collective-permute-start | bytes 1916936 | tf_op jit(solution)/shard_map/ppermute | solution.py:326
  26.6 2.2 %collective-permute-start.1 = (bf16[208,768]{1,0:T(8,128)(2,1)S(1)}, bf16[208,768]{1,0:T(8,128)(2,1)S(1)}, u32[]{:S(2)}, u32[]{:S(2)}) collective-permute-start(bf16[208,768]{1,0:T(8,128)(2,1)S(1)} %get-tuple-element.37), channel_id=1, source_target_pairs={{0,3},{1,2},{2,1},{3,0},{4,7},{5,6},{6,5},{7,4},{8,11},{9,10},{10,... | collective-permute-start | bytes 958472 | tf_op jit(solution)/shard_map/ppermute | solution.py:326
  28.9 4.4 %collective-permute-start.4 = (bf16[624,768]{1,0:T(8,128)(2,1)S(1)}, bf16[624,768]{1,0:T(8,128)(2,1)S(1)}, u32[]{:S(2)}, u32[]{:S(2)}) collective-permute-start(bf16[624,768]{1,0:T(8,128)(2,1)S(1)} %get-tuple-element.35.refs_1_.refs_2_.refs_0_), channel_id=1, source_target_pairs={{0,16},{1,17},{2,18},{3,19},{4,20},{5,21},{6,22},{7,23},{8,24},{9,... | collective-permute-start | bytes 2875400 | tf_op jit(solution)/shard_map/ppermute | solution.py:326
  33.3 0.6 collective-permute-done.1.refs_4_
  34.0 0.8 collective-permute-done.refs_3_
  34.8 3.7 %collective-permute-start.2 = (bf16[832,768]{1,0:T(8,128)(2,1)S(1)}, bf16[832,768]{1,0:T(8,128)(2,1)S(1)}, u32[]{:S(2)}, u32[]{:S(2)}) collective-permute-start(bf16[832,768]{1,0:T(8,128)(2,1)S(1)} %constant_dynamic-update-slice_fusion), channel_id=1, source_target_pairs={{0,1},{1,0},{2,3},{3,2},{4,5},{5,4},{6,7},{7,6},{8,9},{9,8},{10,11... | collective-permute-start | bytes 3833864 | tf_op jit(solution)/shard_map/ppermute | solution.py:326
  38.5 0.1 collective-permute-start.8
  38.6 1.9 %collective-permute-start.3 = (bf16[416,768]{1,0:T(8,128)(2,1)S(1)}, bf16[416,768]{1,0:T(8,128)(2,1)S(1)}, u32[]{:S(2)}, u32[]{:S(2)}) collective-permute-start(bf16[416,768]{1,0:T(8,128)(2,1)S(1)} %constant_dynamic-update-slice_fusion.2), channel_id=1, source_target_pairs={{0,12},{1,13},{2,14},{3,15},{4,8},{5,9},{6,10},{7,11},{8,4},{9,5},... | collective-permute-start | bytes 1916936 | tf_op jit(solution)/shard_map/ppermute | solution.py:326
  40.5 0.9 collective-permute-start.7
  41.3 0.0 collective-permute-done.4.refs_0_
  41.3 6.9 %flash.5 = (f32[576,1]{1,0:T(8,128)S(1)}, f32[576,1]{1,0:T(8,128)S(1)}, f32[576,768]{1,0:T(8,128)S(1)}, f32[576,1]{1,0:T(8,128)S(1)}, f32[576,1]{1,0:T(8,128)S(1)}, /*index=5*/f32[576,768]{1,0:T(8,128)S(1)}) custom-call(bf16[624,768]{1,0:T(8,128)(2,1)S(1)} %collective-permute-done.4.refs_0_, bf16[624,768]{1,0:T(8,128)(2,1)S(1)} %get-tuple-element.35.refs_1_.refs_2_.refs_0_, ...), custom_call_target="tpu_custom_call" | custom-call | flops 8153726976 | bytes 7077888 | tf_op jit(solution)/shard_map/flash/pallas_call | solution.py:219
  48.3 5.1 %collective-permute-done.3.refs_3_ = bf16[416,768]{1,0:T(8,128)(2,1)S(1)} collective-permute-done((bf16[416,768]{1,0:T(8,128)(2,1)S(1)}, bf16[416,768]{1,0:T(8,128)(2,1)S(1)}, u32[]{:S(2)}, u32[]{:S(2)}) %collective-permute-start.3) | collective-permute-done | bytes 639008 | tf_op jit(solution)/shard_map/ppermute | solution.py:326
  53.3 5.0 %collective-permute-done.2.refs_2_ = bf16[832,768]{1,0:T(8,128)(2,1)S(1)} collective-permute-done((bf16[832,768]{1,0:T(8,128)(2,1)S(1)}, bf16[832,768]{1,0:T(8,128)(2,1)S(1)}, u32[]{:S(2)}, u32[]{:S(2)}) %collective-permute-start.2) | collective-permute-done | bytes 1277984 | tf_op jit(solution)/shard_map/ppermute | solution.py:326
  58.3 2.8 %collective-permute-start.5 = (bf16[832,768]{1,0:T(8,128)(2,1)S(1)}, bf16[832,768]{1,0:T(8,128)(2,1)S(1)}, u32[]{:S(2)}, u32[]{:S(2)}) collective-permute-start(bf16[832,768]{1,0:T(8,128)(2,1)S(1)} %collective-permute-done.2.refs_2_), channel_id=1, source_target_pairs={{0,3},{1,2},{2,1},{3,0},{4,7},{5,6},{6,5},{7,4},{8,11},{9,10},{10,... | collective-permute-start | bytes 3833864 | tf_op jit(solution)/shard_map/ppermute | solution.py:326
  61.1 7.3 %flash.6 = (f32[576,1]{1,0:T(8,128)S(1)}, f32[576,1]{1,0:T(8,128)S(1)}, f32[576,768]{1,0:T(8,128)S(1)}, f32[576,1]{1,0:T(8,128)S(1)}, f32[576,1]{1,0:T(8,128)S(1)}, /*index=5*/f32[576,768]{1,0:T(8,128)S(1)}) custom-call(bf16[624,768]{1,0:T(8,128)(2,1)S(1)} %collective-permute-done.4.refs_0_, bf16[624,768]{1,0:T(8,128)(2,1)S(1)} %get-tuple-element.35.refs_1_.refs_2_.refs_0_, ...), custom_call_target="tpu_custom_call" | custom-call | flops 8153726976 | bytes 7077888 | tf_op jit(solution)/shard_map/flash/pallas_call | solution.py:219
  68.4 1.6 %collective-permute-done.7.refs_2_ = bf16[832,768]{1,0:T(8,128)(2,1)S(1)} collective-permute-done((bf16[832,768]{1,0:T(8,128)(2,1)S(1)}, bf16[832,768]{1,0:T(8,128)(2,1)S(1)}, u32[]{:S(2)}, u32[]{:S(2)}) %collective-permute-start.7) | collective-permute-done | bytes 1277984 | tf_op jit(solution)/shard_map/ppermute | solution.py:326
  70.0 7.5 %flash.7 = (f32[576,1]{1,0:T(8,128)S(1)}, f32[576,1]{1,0:T(8,128)S(1)}, f32[576,768]{1,0:T(8,128)S(1)}, f32[576,1]{1,0:T(8,128)S(1)}, f32[576,1]{1,0:T(8,128)S(1)}, /*index=5*/f32[576,768]{1,0:T(8,128)S(1)}) custom-call(bf16[624,768]{1,0:T(8,128)(2,1)S(1)} %collective-permute-done.4.refs_0_, bf16[624,768]{1,0:T(8,128)(2,1)S(1)} %get-tuple-element.35.refs_1_.refs_2_.refs_0_, ...), custom_call_target="tpu_custom_call" | custom-call | flops 8153726976 | bytes 7077888 | tf_op jit(solution)/shard_map/flash/pallas_call | solution.py:219
  77.4 5.9 %collective-permute-done.5.refs_1_ = bf16[832,768]{1,0:T(8,128)(2,1)S(1)} collective-permute-done((bf16[832,768]{1,0:T(8,128)(2,1)S(1)}, bf16[832,768]{1,0:T(8,128)(2,1)S(1)}, u32[]{:S(2)}, u32[]{:S(2)}) %collective-permute-start.5) | collective-permute-done | bytes 1277984 | tf_op jit(solution)/shard_map/ppermute | solution.py:326
  83.4 3.9 %flash.9 = bf16[592,768]{1,0:T(8,128)(2,1)S(1)} custom-call(bf16[624,768]{1,0:T(8,128)(2,1)S(1)} %collective-permute-done.4.refs_0_, bf16[832,768]{1,0:T(8,128)(2,1)S(1)} %collective-permute-done.5.refs_1_, bf16[416,768]{1,0:T(8,128)(2,1)S(1)} %collective-permute-done.6.refs_2_, f32[576,1]{1,0:T(8,128)S(1)} %get-tuple-element.63.refs_3_, ...), custom_call_target="tpu_custom_call" | custom-call | flops 4076863488 | bytes 4423680 | tf_op jit(solution)/shard_map/flash/pallas_call | solution.py:219
  87.3 0.1 collective-permute-start.9
  87.4 3.9 %flash.8 = (f32[576,1]{1,0:T(8,128)S(1)}, f32[576,1]{1,0:T(8,128)S(1)}, f32[576,768]{1,0:T(8,128)S(1)}) custom-call(bf16[624,768]{1,0:T(8,128)(2,1)S(1)} %get-tuple-element.35.refs_1_.refs_2_.refs_0_, bf16[832,768]{1,0:T(8,128)(2,1)S(1)} %collective-permute-done.5.refs_1_, bf16[416,768]{1,0:T(8,128)(2,1)S(1)} %collective-permute-done.6.refs_2_, ...), custom_call_target="tpu_custom_call" | custom-call | flops 4076863488 | bytes 4423680 | tf_op jit(solution)/shard_map/flash/pallas_call | solution.py:219
  91.3 0.8 combine.1
  92.1 0.0 copy-start.2
  92.1 16.8 %all_to_all.11 = bf16[8,80,768]{2,1,0:T(8,128)(2,1)S(1)} all-to-all(bf16[8,80,768]{2,1,0:T(8,128)(2,1)S(1)} %combine.1), channel_id=1, replica_groups={{0,4,32,36,64,68,96,100},{1,5,33,37,65,69,97,101},{2,6,34,38,66,70,98,1..., dimensions={0} | all-to-all | bytes 1966080 | tf_op jit(solution)/shard_map/all_to_all | solution.py:383
  108.8 2.3 %final.1 = (bf16[384,768]{1,0:T(8,128)(2,1)}, f32[1,384]{1,0:T(1,128)S(1)}) custom-call(s32[1]{0:T(128)} %bitcast.me_ref, s32[32]{0:T(128)S(1)} %copy-done.2, s32[1,384]{1,0:T(1,128)S(1)} %reshape.20.clusters_ref, bf16[640,768]{1,0:T(8,128)(2,1)S(1)} %bitcast.3), custom_call_target="tpu_custom_call" | custom-call | tf_op jit(solution)/shard_map/final/pallas_call | solution.py:384
  111.1 0.6 reduce
  (11 shorter events, 0.1 us)
Async XLA Ops:
  1.4 1.1 copy-start
  2.4 0.7 copy-start.1
  24.9 9.8 %collective-permute-start = (bf16[416,768]{1,0:T(8,128)(2,1)S(1)}, bf16[416,768]{1,0:T(8,128)(2,1)S(1)}, u32[]{:S(2)}, u32[]{:S(2)}) collective-permute-start(bf16[416,768]{1,0:T(8,128)(2,1)S(1)} %get-tuple-element.36), channel_id=1, source_target_pairs={{0,12},{1,13},{2,14},{3,15},{4,8},{5,9},{6,10},{7,11},{8,4},{9,5},... | collective-permute-start | bytes 1916936 | tf_op jit(solution)/shard_map/ppermute | solution.py:326
  26.6 7.3 %collective-permute-start.1 = (bf16[208,768]{1,0:T(8,128)(2,1)S(1)}, bf16[208,768]{1,0:T(8,128)(2,1)S(1)}, u32[]{:S(2)}, u32[]{:S(2)}) collective-permute-start(bf16[208,768]{1,0:T(8,128)(2,1)S(1)} %get-tuple-element.37), channel_id=1, source_target_pairs={{0,3},{1,2},{2,1},{3,0},{4,7},{5,6},{6,5},{7,4},{8,11},{9,10},{10,... | collective-permute-start | bytes 958472 | tf_op jit(solution)/shard_map/ppermute | solution.py:326
  28.9 12.5 %collective-permute-start.4 = (bf16[624,768]{1,0:T(8,128)(2,1)S(1)}, bf16[624,768]{1,0:T(8,128)(2,1)S(1)}, u32[]{:S(2)}, u32[]{:S(2)}) collective-permute-start(bf16[624,768]{1,0:T(8,128)(2,1)S(1)} %get-tuple-element.35.refs_1_.refs_2_.refs_0_), channel_id=1, source_target_pairs={{0,16},{1,17},{2,18},{3,19},{4,20},{5,21},{6,22},{7,23},{8,24},{9,... | collective-permute-start | bytes 2875400 | tf_op jit(solution)/shard_map/ppermute | solution.py:326
  34.8 23.6 %collective-permute-start.2 = (bf16[832,768]{1,0:T(8,128)(2,1)S(1)}, bf16[832,768]{1,0:T(8,128)(2,1)S(1)}, u32[]{:S(2)}, u32[]{:S(2)}) collective-permute-start(bf16[832,768]{1,0:T(8,128)(2,1)S(1)} %constant_dynamic-update-slice_fusion), channel_id=1, source_target_pairs={{0,1},{1,0},{2,3},{3,2},{4,5},{5,4},{6,7},{7,6},{8,9},{9,8},{10,11... | collective-permute-start | bytes 3833864 | tf_op jit(solution)/shard_map/ppermute | solution.py:326
  38.5 29.9 %collective-permute-start.8 = (bf16[416,768]{1,0:T(8,128)(2,1)S(1)}, bf16[416,768]{1,0:T(8,128)(2,1)S(1)}, u32[]{:S(2)}, u32[]{:S(2)}) collective-permute-start(bf16[416,768]{1,0:T(8,128)(2,1)S(1)} %constant_dynamic-update-slice_fusion.2), channel_id=1, source_target_pairs={{0,1},{1,0},{2,3},{3,2},{4,5},{5,4},{6,7},{7,6},{8,9},{9,8},{10,11... | collective-permute-start | bytes 1916936 | tf_op jit(solution)/shard_map/ppermute | solution.py:326
  38.6 14.8 %collective-permute-start.3 = (bf16[416,768]{1,0:T(8,128)(2,1)S(1)}, bf16[416,768]{1,0:T(8,128)(2,1)S(1)}, u32[]{:S(2)}, u32[]{:S(2)}) collective-permute-start(bf16[416,768]{1,0:T(8,128)(2,1)S(1)} %constant_dynamic-update-slice_fusion.2), channel_id=1, source_target_pairs={{0,12},{1,13},{2,14},{3,15},{4,8},{5,9},{6,10},{7,11},{8,4},{9,5},... | collective-permute-start | bytes 1916936 | tf_op jit(solution)/shard_map/ppermute | solution.py:326
  40.5 29.5 %collective-permute-start.7 = (bf16[832,768]{1,0:T(8,128)(2,1)S(1)}, bf16[832,768]{1,0:T(8,128)(2,1)S(1)}, u32[]{:S(2)}, u32[]{:S(2)}) collective-permute-start(bf16[832,768]{1,0:T(8,128)(2,1)S(1)} %constant_dynamic-update-slice_fusion), channel_id=1, source_target_pairs={{0,3},{1,2},{2,1},{3,0},{4,7},{5,6},{6,5},{7,4},{8,11},{9,10},{10,... | collective-permute-start | bytes 3833864 | tf_op jit(solution)/shard_map/ppermute | solution.py:326
  58.3 19.1 %collective-permute-start.6 = (bf16[416,768]{1,0:T(8,128)(2,1)S(1)}, bf16[416,768]{1,0:T(8,128)(2,1)S(1)}, u32[]{:S(2)}, u32[]{:S(2)}) collective-permute-start(bf16[416,768]{1,0:T(8,128)(2,1)S(1)} %collective-permute-done.3.refs_3_), channel_id=1, source_target_pairs={{0,1},{1,0},{2,3},{3,2},{4,5},{5,4},{6,7},{7,6},{8,9},{9,8},{10,11... | collective-permute-start | bytes 1916936 | tf_op jit(solution)/shard_map/ppermute | solution.py:326
  58.3 25.0 %collective-permute-start.5 = (bf16[832,768]{1,0:T(8,128)(2,1)S(1)}, bf16[832,768]{1,0:T(8,128)(2,1)S(1)}, u32[]{:S(2)}, u32[]{:S(2)}) collective-permute-start(bf16[832,768]{1,0:T(8,128)(2,1)S(1)} %collective-permute-done.2.refs_2_), channel_id=1, source_target_pairs={{0,3},{1,2},{2,1},{3,0},{4,7},{5,6},{6,5},{7,4},{8,11},{9,10},{10,... | collective-permute-start | bytes 3833864 | tf_op jit(solution)/shard_map/ppermute | solution.py:326
  87.3 4.0 %collective-permute-start.9 = (bf16[592,768]{1,0:T(8,128)(2,1)S(1)}, bf16[592,768]{1,0:T(8,128)(2,1)S(1)}, u32[]{:S(2)}, u32[]{:S(2)}) collective-permute-start(bf16[592,768]{1,0:T(8,128)(2,1)S(1)} %flash.9), channel_id=1, source_target_pairs={{0,16},{1,17},{2,18},{3,19},{4,20},{5,21},{6,22},{7,23},{8,24},{9,... | collective-permute-start | bytes 2727944 | tf_op jit(solution)/shard_map/ppermute | solution.py:326
  92.1 16.8 %copy-start.2 = (s32[32]{0:T(128)S(1)}, s32[32]{0:T(128)}, u32[]{:S(2)}) copy-start(s32[32]{0:T(128)} %owner_ref.3) | copy-start | bytes 388

commit v3 on v2

--- a/solution.py
+++ b/solution.py
@@ -14,8 +14,8 @@
 ln2 = math.log(2.0)
 masked = -1e30
 axes = ("group", "tile")
-part_rows = 24
 parts = 3
+filled = 72
 packet_rows = 80
 block_keys = 192
 block_rows = 208
@@ -31,8 +31,7 @@
 params = pltpu.CompilerParams(vmem_limit_bytes=32 * 1024 * 1024)
 
 
-def row_facts(clusters_ref, owner_ref, me):
-    cluster = clusters_ref[...]
+def row_facts(cluster, owner_ref, me):
     rows = cluster.shape[1]
     group = jnp.zeros_like(cluster)
     for number in range(owner_ref.shape[0]):
@@ -45,9 +44,11 @@
         member.astype(f32).astype(bf16), upper.astype(f32).astype(bf16), preferred_element_type=f32
     )
     rank = jnp.sum(jnp.where(member, counts, 0.0), axis=0, keepdims=True).astype(jnp.int32)
-    part = (rank >= part_rows).astype(jnp.int32) + (rank >= 2 * part_rows).astype(jnp.int32)
-    lane = me * part_rows + rank - part * part_rows
-    return cluster, group, rank, part, lane
+    change = group ^ me
+    packet = jnp.where(change == 3, 4, jnp.where(change == 4, 3, change))
+    slot = packet * filled + rank
+    part = (slot >= block_keys).astype(jnp.int32) + (slot >= 2 * block_keys).astype(jnp.int32)
+    return cluster, packet, rank, part, slot - part * block_keys
 
 
 def hits(count, target):
@@ -59,41 +60,65 @@
     return hits(count, target).astype(f32).astype(bf16)
 
 
-def place_kernel(me_ref, owner_ref, clusters_ref, rows_ref, out_ref):
-    cluster, group, rank, part, lane = row_facts(clusters_ref, owner_ref, me_ref[0])
+def place_kernel(me_ref, owner_ref, clusters_ref, rows_ref, *out_refs):
+    cluster, packet, rank, part, lane = row_facts(
+        clusters_ref[...].reshape(1, clusters_ref.shape[0]), owner_ref, me_ref[0]
+    )
     width = rows_ref.shape[1]
-    total = out_ref.shape[0]
+    total = 8 * packet_rows
     placed = jnp.dot(
-        ones_at(total, group * packet_rows + rank), rows_ref[...], preferred_element_type=f32
-    )
-    labels = jnp.where(hits(64, group * 8 + part), (cluster + 1).astype(f32), 0.0).astype(bf16)
+        ones_at(total, packet * packet_rows + rank), rows_ref[...], preferred_element_type=f32
+    )
+    labels = jnp.where(hits(64, packet * 8 + part), (cluster + 1).astype(f32), 0.0).astype(bf16)
     ids = lax.dot_general(
         labels, ones_at(width, lane), (((1,), (1,)), ((), ())), preferred_element_type=f32
     ).astype(bf16)
     source = lax.broadcasted_iota(jnp.int32, (1, 64), 1)
     placed_ids = jnp.dot(
-        ones_at(total, (source // 8) * packet_rows + 72 + source % 8), ids, preferred_element_type=f32
-    )
-    out_ref[...] = (placed + placed_ids).astype(bf16)
-
-
-def pack_kernel(in_ref, q_ref, big_ref, small_ref):
-    packets = [in_ref[s].astype(f32) for s in range(8)]
-    for p in range(parts):
-        rows = [packets[s][p * part_rows : (p + 1) * part_rows] for s in range(8)]
-        ids = packets[0][72:80]
-        for s in range(1, 8):
-            ids = ids + packets[s][72:80]
+        ones_at(total, (source // 8) * packet_rows + filled + source % 8),
+        ids,
+        preferred_element_type=f32,
+    )
+    both = (placed + placed_ids).astype(bf16)
+    for n in range(8):
+        out_refs[n][...] = both[n * packet_rows : (n + 1) * packet_rows]
+
+
+def spans(p):
+    found = []
+    for n in range(8):
+        low = max(p * block_keys, n * filled) - n * filled
+        high = min((p + 1) * block_keys, (n + 1) * filled) - n * filled
+        if low < high:
+            found.append((n, low, high))
+    return found
+
+
+def pack_kernel(blocks, names, *refs):
+    packets = {n: ref[...].astype(f32) for n, ref in zip(names, refs)}
+    out_ref = refs[-1]
+    for k, p in enumerate(blocks):
+        rows = [packets[n][low:high] for n, low, high in spans(p)]
+        ids = sum(packets[n][filled : filled + 8] for n, _, _ in spans(p))
         at = lax.broadcasted_iota(jnp.int32, ids.shape, 0)
         row = jnp.sum(jnp.where(at == p, ids, 0.0), axis=0, keepdims=True)
         tail = jnp.where(at == 0, row, 0.0)
-        block = jnp.concatenate(rows + [tail, jnp.zeros_like(tail)], axis=0).astype(bf16)
-        at = slice(p * block_rows, (p + 1) * block_rows)
-        q_ref[at, :] = block
-        if p < 2:
-            big_ref[at, :] = block
-        else:
-            small_ref[...] = block
+        out_ref[k * block_rows : (k + 1) * block_rows, :] = jnp.concatenate(
+            rows + [tail, jnp.zeros_like(tail)], axis=0
+        ).astype(bf16)
+
+
+def pack(blocks, packets):
+    names = sorted({n for p in blocks for n, _, _ in spans(p)})
+    width = packets[0].shape[1]
+    return pl.pallas_call(
+        functools.partial(pack_kernel, blocks, names),
+        out_shape=jax.ShapeDtypeStruct((len(blocks) * block_rows, width), bf16),
+        in_specs=vmem_specs(len(names)),
+        out_specs=vmem_specs(1)[0],
+        compiler_params=params,
+        name="pack",
+    )(*[packets[n] for n in names])
 
 
 def column_of(row):
@@ -140,20 +165,21 @@
 def flash_kernel(blocks, first, owns, finish, *refs):
     refs = list(refs)
     count = len(owns)
-    q_refs = [refs.pop(0) for _ in range(count)]
+    q_refs = [[refs.pop(0), refs.pop(0)] for _ in range(count)]
     key_refs = [refs.pop(0) for _ in blocks]
     states = None if first else [[refs.pop(0) for _ in range(3)] for _ in range(count)]
     outs = [[refs.pop(0)] if finish else [refs.pop(0) for _ in range(3)] for _ in range(count)]
     keys, queries, labels = refs
-    width = q_refs[0].shape[1]
+    width = q_refs[0][0].shape[1]
     scale = score_scale / math.sqrt(width) * log2e
     key_id = gather_keys(key_refs, blocks, keys)
     other = jnp.where(key_id == 0.0, masked, -penalty * log2e)
     for n in range(count):
         for p in range(parts):
             at = slice(p * block_keys, (p + 1) * block_keys)
-            queries[n, at, :] = q_refs[n][p * block_rows : p * block_rows + block_keys, :]
-            ids = q_refs[n][p * block_rows + block_keys : (p + 1) * block_rows, 0:256]
+            ref, first_row = q_refs[n][p // 2], (p % 2) * block_rows
+            queries[n, at, :] = ref[first_row : first_row + block_keys, :]
+            ids = ref[first_row + block_keys : first_row + block_rows, 0:256]
             labels[n, at, :] = column_of(ids.astype(f32)[0:1])
     for n in range(count):
         for start in range(0, parts * block_keys, query_rows):
@@ -201,7 +227,7 @@
 
 
 def flash(qs, owns, key_arrays, states, finish):
-    width = qs[0].shape[1]
+    width = qs[0][0].shape[1]
     blocks = [a.shape[0] // block_rows for a in key_arrays]
     total = sum(blocks) * block_keys
     rows = parts * block_keys
@@ -215,7 +241,7 @@
             jax.ShapeDtypeStruct((rows, width), f32),
         ]
     count = len(qs)
-    args = [*qs, *key_arrays] + ([] if first else [a for state in states for a in state])
+    args = [a for q in qs for a in q] + list(key_arrays) + ([] if first else [a for state in states for a in state])
     out = pl.pallas_call(
         functools.partial(flash_kernel, blocks, first, owns, finish),
         out_shape=each * count,
@@ -239,7 +265,7 @@
     return [tuple(out[3 * n : 3 * n + 3]) for n in range(count)]
 
 
-def combine_kernel(m_ref, l_ref, acc_ref, other_ref, out_ref):
+def combine_kernel(m_ref, l_ref, acc_ref, other_ref, *out_refs):
     width = acc_ref.shape[1]
     rows = parts * block_keys
     tails = other_ref[rows : rows + 16, :].astype(f32)
@@ -262,30 +288,37 @@
             here == 3 + p, row_of(low, width), 0.0
         )
         levels = tail if p == 0 else levels + tail
-    for s in range(8):
-        pieces = [m[s * part_rows : (s + 1) * part_rows] for m in mixes] + [levels]
-        out_ref[s] = jnp.concatenate(pieces, axis=0).astype(bf16)
-
-
-def final_kernel(me_ref, owner_ref, clusters_ref, back_ref, rows_ref, mass_ref):
-    _, group, rank, part, lane = row_facts(clusters_ref, owner_ref, me_ref[0])
-    total = back_ref.shape[0]
+    for n in range(8):
+        pieces = [
+            mixes[p][n * filled + low - p * block_keys : n * filled + high - p * block_keys]
+            for p in range(parts)
+            for other, low, high in spans(p)
+            if other == n
+        ]
+        out_refs[n][...] = jnp.concatenate(pieces + [levels], axis=0).astype(bf16)
+
+
+def final_kernel(me_ref, owner_ref, clusters_ref, *refs):
+    backs, (rows_ref, mass_ref, back) = refs[:8], refs[8:]
+    _, packet, rank, part, lane = row_facts(
+        clusters_ref[...].reshape(1, clusters_ref.shape[0]), owner_ref, me_ref[0]
+    )
+    for n in range(8):
+        back[n * packet_rows : (n + 1) * packet_rows, :] = backs[n][...]
     rows_ref[...] = lax.dot_general(
-        ones_at(total, group * packet_rows + rank),
-        back_ref[...],
+        ones_at(8 * packet_rows, packet * packet_rows + rank),
+        back[...],
         (((0,), (0,)), ((), ())),
         preferred_element_type=f32,
     ).astype(bf16)
     levels = jnp.concatenate(
-        [
-            back_ref[g * packet_rows + 64 : (g + 1) * packet_rows, 0:256].astype(f32)[8:16]
-            for g in range(8)
-        ],
-        axis=0,
+        [backs[n][64:packet_rows, 0:256].astype(f32)[8:16] for n in range(8)], axis=0
     ).astype(bf16)
     found = jnp.dot(levels, ones_at(256, lane), preferred_element_type=f32)
-    chosen = hits(64, group * 8 + part) | hits(64, group * 8 + 3 + part)
-    mass_ref[...] = jnp.sum(jnp.where(chosen, found, 0.0), axis=0, keepdims=True)
+    chosen = hits(64, packet * 8 + part) | hits(64, packet * 8 + 3 + part)
+    mass_ref[...] = jnp.sum(jnp.where(chosen, found, 0.0), axis=0, keepdims=True).reshape(
+        mass_ref.shape
+    )
 
 
 def links(mesh):
@@ -303,54 +336,36 @@
 
     dims = [
         pairs(lambda y, c, x, z: (y, c, x ^ 3, z)),
-        pairs(lambda y, c, x, z: (y, c, x, z ^ 1)),
+        pairs(lambda y, c, x, z: (y ^ 3, c, x, z)),
         pairs(lambda y, c, x, z: (y, c, x, z ^ 3)),
     ]
     swap = pairs(lambda y, c, x, z: (y, c ^ 1, x, z))
-    groups = []
-    for c in range(2):
-        for half in range(2):
-            for z in range(side):
-                groups.append(
-                    [
-                        number(y, c, 2 * half + (kind ^ half), z)
-                        for y in range(side)
-                        for kind in range(2)
-                    ]
-                )
-    return dims, swap, groups
-
-
-def per_device(dims, swap, groups, embeddings, clusters, cluster_owner):
+    trips = [
+        pairs(lambda y, c, x, z, m=m: (y ^ (m >> 1 & 1), c, x ^ (m & 1), z ^ (m >> 2)))
+        for m in (0, 1, 2, 4, 3, 5, 6, 7)
+    ]
+    return dims, swap, trips
+
+
+def per_device(dims, swap, trips, embeddings, clusters, cluster_owner):
     rows, width = embeddings.shape
     send = lambda a, pairs: lax.ppermute(a, axes, pairs)
     group_axis, tile = lax.axis_index("group"), lax.axis_index("tile")
-    x = tile // 4
-    kind = ((x + 1) // 2) % 2
-    me = ((group_axis // 2) * 2 + kind).astype(jnp.int32).reshape(1)
-    cluster_row = clusters.reshape(1, rows)
+    kind = lambda at: (at + 1) // 2 % 2
+    me = kind(tile // 4) + 2 * kind(group_axis // 2) + 4 * kind(tile % 4)
+    me = me.astype(jnp.int32).reshape(1)
     smem = pl.BlockSpec(memory_space=pltpu.SMEM)
+    packet = jax.ShapeDtypeStruct((packet_rows, width), bf16)
     packets = pl.pallas_call(
         place_kernel,
-        out_shape=jax.ShapeDtypeStruct((8 * packet_rows, width), bf16),
+        out_shape=[packet] * 8,
         in_specs=[smem, smem] + vmem_specs(2),
-        out_specs=vmem_specs(1)[0],
+        out_specs=vmem_specs(8),
         compiler_params=params,
         name="place",
-    )(me, cluster_owner, cluster_row, embeddings)
-    arrived = lax.all_to_all(
-        packets.reshape(8, packet_rows, width), axes, 0, 0, axis_index_groups=groups, tiled=True
-    )
-    q_own, big, small = pl.pallas_call(
-        pack_kernel,
-        out_shape=[
-            jax.ShapeDtypeStruct((count * block_rows, width), bf16) for count in (parts, 2, 1)
-        ],
-        in_specs=vmem_specs(1),
-        out_specs=vmem_specs(3),
-        compiler_params=params,
-        name="pack",
-    )(arrived)
+    )(me, cluster_owner, clusters, embeddings)
+    arrived = [packets[0]] + [send(packets[n], trips[n]) for n in range(1, 8)]
+    big, small = pack((0, 1), arrived), pack((2,), arrived)
     wide = [
         [pair for pair in dims[s % 3] if pair[0] // 16 % 2 == 0]
         + [pair for pair in dims[(s + 1) % 3] if pair[0] // 16 % 2 == 1]
@@ -358,13 +373,13 @@
     ]
     narrow = [dims[(s + 2) % 3] for s in range(3)]
     big0, small0 = send(big, wide[0]), send(small, narrow[0])
-    q_other = send(q_own, swap)
+    q_own, q_other = (big, small), (send(big, swap), send(small, swap))
     big0, small0 = lax.optimization_barrier((big0, small0))
     big, small = jnp.concatenate([big, big0], axis=0), jnp.concatenate([small, small0], axis=0)
     big1, small1 = send(big, wide[1]), send(small, narrow[1])
     big2, small2 = send(big, wide[2]), send(small, narrow[2])
     queries, owns = [q_other, q_own], [False, True]
-    states = flash(queries, owns, [q_own, big0, small0], None, False)
+    states = flash(queries, owns, [*q_own, big0, small0], None, False)
     big1, small1, states[1] = lax.optimization_barrier((big1, small1, states[1]))
     big3, small3 = send(big1, wide[2]), send(small1, narrow[2])
     states = flash(queries, owns, [big1, small1], states, False)
@@ -374,32 +389,30 @@
     theirs = send(partial, swap)
     answers = pl.pallas_call(
         combine_kernel,
-        out_shape=jax.ShapeDtypeStruct((8, packet_rows, width), bf16),
+        out_shape=[packet] * 8,
         in_specs=vmem_specs(4),
-        out_specs=vmem_specs(1)[0],
+        out_specs=vmem_specs(8),
         compiler_params=params,
         name="combine",
     )(*mine, theirs)
-    back = lax.all_to_all(answers, axes, 0, 0, axis_index_groups=groups, tiled=True)
+    back = [answers[0]] + [send(answers[n], trips[n]) for n in range(1, 8)]
     neighbours, log_mass = pl.pallas_call(
         final_kernel,
-        out_shape=[
-            jax.ShapeDtypeStruct((rows, width), bf16),
-            jax.ShapeDtypeStruct((1, rows), f32),
-        ],
-        in_specs=[smem, smem] + vmem_specs(2),
+        out_shape=[jax.ShapeDtypeStruct((rows, width), bf16), jax.ShapeDtypeStruct((rows,), f32)],
+        in_specs=[smem, smem] + vmem_specs(9),
         out_specs=vmem_specs(2),
+        scratch_shapes=[pltpu.VMEM((8 * packet_rows, width), bf16)],
         compiler_params=params,
         name="final",
-    )(me, cluster_owner, cluster_row, back.reshape(8 * packet_rows, width))
-    return neighbours, log_mass.reshape(rows)
+    )(me, cluster_owner, clusters, *back)
+    return neighbours, log_mass
 
 
 def solution(mesh):
     placed = (P(axes, None), P(axes), P())
-    dims, swap, groups = links(mesh)
+    dims, swap, trips = links(mesh)
     return jax.shard_map(
-        functools.partial(per_device, dims, swap, groups),
+        functools.partial(per_device, dims, swap, trips),
         mesh=mesh,
         in_specs=placed,
         out_specs=(P(axes, None), P(axes)),

time: 112 us -> 114 us (1.018)
  blocking collectives: 36.4 us -> 0 us
  starting transfers between devices: 17.8 us -> 46.9 us
  waiting for transfers between devices: 18.9 us -> 28 us
    all_to_all x2 -> x0, blocking collectives: 36.4 us -> none  [the longest x1 19.6 us: per_device(): lax.all_to_all(packets.reshape(8, packet_rows, width), axes, 0, 0, axis_i...]
    ppermute x10 -> x25, starting transfers between devices: 17.8 us -> 46.9 us  [per_device(): send = lambda a, pairs: lax.ppermute(a, axes, pairs)]
    ppermute x10 -> x25, waiting for transfers between devices: 18.9 us -> 28 us  [per_device(): send = lambda a, pairs: lax.ppermute(a, axes, pairs)]
    unnamed x8 -> x10, local copies, waits for them, and re-layouts: 1.79 us -> 2.41 us
    pallas_call x3 -> x4, Pallas kernels: 2.96 us -> 2.95 us  [the longest x1 2.08 us: per_device(): pl.pallas_call(place_kernel, out_shape=[packet] * 8, in_specs=[smem, smem...]
  transfers between devices with their start and end apart: 10 -> 25, of which waited for: 6 -> 11; matrix products, arithmetic and copies ran while one was open for 0% -> 0% of each run, Pallas kernels for 23% -> 23%
where the time goes in v3:
time: 114 us
  starting transfers between devices  46.9 us (41%)
  Pallas kernels  35.3 us (31%)
  waiting for transfers between devices  28 us (25%)
  local copies, waits for them, and re-layouts  2.41 us (2%)
    ppermute x25, starting transfers between devices, per_device(): send = lambda a, pairs: lax.ppermute(a, axes, pairs)  46.9 us
    pallas_call x5, Pallas kernels, flash(): pl.pallas_call(functools.partial(flash_kernel, blocks, first, owns, finis...  30 us
    ppermute x25, waiting for transfers between devices, per_device(): send = lambda a, pairs: lax.ppermute(a, axes, pairs)  28 us
    unnamed x10, local copies, waits for them, and re-layouts  2.41 us
  transfers between devices with their start and end apart: 25, of which 11 were waited for; matrix products, arithmetic and copies ran while one was open for 0% of the time, Pallas kernels for 23%

profile of v3, /device:TPU:1, one launch (start us, length us, event | category | flops | bytes accessed | tf_op | source)
XLA Modules:
  0.0 113.7 jit_solution(13037073301719090818)
XLA Ops:
  0.8 1.1 copy-done
  3.2 2.1 %place.1 = (bf16[80,768]{1,0:T(8,128)(2,1)S(1)}, bf16[80,768]{1,0:T(8,128)(2,1)S(1)}, bf16[80,768]{1,0:T(8,128)(2,1)S(1)}, bf16[80,768]{1,0:T(8,128)(2,1)S(1)}, ...) custom-call(s32[1]{0:T(128)} %bitcast.me_ref, ...), custom_call_target="tpu_custom_call" | custom-call | tf_op jit(solution)/shard_map/place/pallas_call | solution.py:359
  5.3 2.1 %collective-permute-start = (bf16[80,768]{1,0:T(8,128)(2,1)S(1)}, bf16[80,768]{1,0:T(8,128)(2,1)S(1)}, u32[]{:S(2)}, u32[]{:S(2)}) collective-permute-start(bf16[80,768]{1,0:T(8,128)(2,1)S(1)} %get-tuple-element.47), channel_id=1, source_target_pairs={{0,4},{1,5},{2,6},{3,7},{4,0},{5,1},{6,2},{7,3},{8,12},{9,13},{10,... | collective-permute-start | bytes 368648 | tf_op jit(solution)/shard_map/ppermute | solution.py:352
  7.4 1.3 %collective-permute-start.1 = (bf16[80,768]{1,0:T(8,128)(2,1)S(1)}, bf16[80,768]{1,0:T(8,128)(2,1)S(1)}, u32[]{:S(2)}, u32[]{:S(2)}) collective-permute-start(bf16[80,768]{1,0:T(8,128)(2,1)S(1)} %get-tuple-element.48), channel_id=1, source_target_pairs={{0,32},{1,33},{2,34},{3,35},{4,36},{5,37},{6,38},{7,39},{8,40},{9,... | collective-permute-start | bytes 368648 | tf_op jit(solution)/shard_map/ppermute | solution.py:352
  8.7 1.6 %collective-permute-start.2 = (bf16[80,768]{1,0:T(8,128)(2,1)S(1)}, bf16[80,768]{1,0:T(8,128)(2,1)S(1)}, u32[]{:S(2)}, u32[]{:S(2)}) collective-permute-start(bf16[80,768]{1,0:T(8,128)(2,1)S(1)} %get-tuple-element.49), channel_id=1, source_target_pairs={{0,1},{1,0},{2,3},{3,2},{4,5},{5,4},{6,7},{7,6},{8,9},{9,8},{10,11... | collective-permute-start | bytes 368648 | tf_op jit(solution)/shard_map/ppermute | solution.py:352
  10.5 0.9 collective-permute-start.4
  11.4 1.4 %collective-permute-done.2.refs_3_ = bf16[80,768]{1,0:T(8,128)(2,1)S(1)} collective-permute-done((bf16[80,768]{1,0:T(8,128)(2,1)S(1)}, bf16[80,768]{1,0:T(8,128)(2,1)S(1)}, u32[]{:S(2)}, u32[]{:S(2)}) %collective-permute-start.2) | collective-permute-done | bytes 122912 | tf_op jit(solution)/shard_map/ppermute | solution.py:352
  12.8 2.1 %collective-permute-done.3.refs_4_ = bf16[80,768]{1,0:T(8,128)(2,1)S(1)} collective-permute-done((bf16[80,768]{1,0:T(8,128)(2,1)S(1)}, bf16[80,768]{1,0:T(8,128)(2,1)S(1)}, u32[]{:S(2)}, u32[]{:S(2)}) %collective-permute-start.3) | collective-permute-done | bytes 122912 | tf_op jit(solution)/shard_map/ppermute | solution.py:352
  14.9 1.6 %collective-permute-done.4.refs_5_.refs_0_ = bf16[80,768]{1,0:T(8,128)(2,1)S(1)} collective-permute-done((bf16[80,768]{1,0:T(8,128)(2,1)S(1)}, bf16[80,768]{1,0:T(8,128)(2,1)S(1)}, u32[]{:S(2)}, u32[]{:S(2)}) %collective-permute-start.4) | collective-permute-done | bytes 122912 | tf_op jit(solution)/shard_map/ppermute | solution.py:352
  16.6 2.9 %collective-permute-start.7 = (bf16[416,768]{1,0:T(8,128)(2,1)S(1)}, bf16[416,768]{1,0:T(8,128)(2,1)S(1)}, u32[]{:S(2)}, u32[]{:S(2)}) collective-permute-start(bf16[416,768]{1,0:T(8,128)(2,1)S(1)} %pack.2.refs_2_.refs_4_.refs_0_), channel_id=1, source_target_pairs={{0,12},{1,13},{2,14},{3,15},{4,8},{5,9},{6,10},{7,11},{8,4},{9,5},... | collective-permute-start | bytes 1916936 | tf_op jit(solution)/shard_map/ppermute | solution.py:352
  19.8 3.4 %collective-permute-start.6 = (bf16[80,768]{1,0:T(8,128)(2,1)S(1)}, bf16[80,768]{1,0:T(8,128)(2,1)S(1)}, u32[]{:S(2)}, u32[]{:S(2)}) collective-permute-start(bf16[80,768]{1,0:T(8,128)(2,1)S(1)} %get-tuple-element.53), channel_id=1, source_target_pairs={{0,37},{1,36},{2,39},{3,38},{4,33},{5,32},{6,35},{7,34},{8,45},{9,... | collective-permute-start | bytes 368648 | tf_op jit(solution)/shard_map/ppermute | solution.py:352
  23.1 1.3 %collective-permute-done.5.refs_1_ = bf16[80,768]{1,0:T(8,128)(2,1)S(1)} collective-permute-done((bf16[80,768]{1,0:T(8,128)(2,1)S(1)}, bf16[80,768]{1,0:T(8,128)(2,1)S(1)}, u32[]{:S(2)}, u32[]{:S(2)}) %collective-permute-start.5) | collective-permute-done | bytes 122912 | tf_op jit(solution)/shard_map/ppermute | solution.py:352
  24.4 1.0 collective-permute-done.6.refs_2_
  25.5 3.4 %collective-permute-start.8 = (bf16[208,768]{1,0:T(8,128)(2,1)S(1)}, bf16[208,768]{1,0:T(8,128)(2,1)S(1)}, u32[]{:S(2)}, u32[]{:S(2)}) collective-permute-start(bf16[208,768]{1,0:T(8,128)(2,1)S(1)} %pack.3.refs_3_.refs_5_.refs_1_), channel_id=1, source_target_pairs={{0,3},{1,2},{2,1},{3,0},{4,7},{5,6},{6,5},{7,4},{8,11},{9,10},{10,... | collective-permute-start | bytes 958472 | tf_op jit(solution)/shard_map/ppermute | solution.py:352
  28.9 4.5 %collective-permute-start.11 = (bf16[416,768]{1,0:T(8,128)(2,1)S(1)}, bf16[416,768]{1,0:T(8,128)(2,1)S(1)}, u32[]{:S(2)}, u32[]{:S(2)}) collective-permute-start(bf16[416,768]{1,0:T(8,128)(2,1)S(1)} %pack.2.refs_2_.refs_4_.refs_0_), channel_id=1, source_target_pairs={{0,16},{1,17},{2,18},{3,19},{4,20},{5,21},{6,22},{7,23},{8,24},{9,... | collective-permute-start | bytes 1916936 | tf_op jit(solution)/shard_map/ppermute | solution.py:352
  33.5 2.7 %collective-permute-start.9 = (bf16[832,768]{1,0:T(8,128)(2,1)S(1)}, bf16[832,768]{1,0:T(8,128)(2,1)S(1)}, u32[]{:S(2)}, u32[]{:S(2)}) collective-permute-start(bf16[832,768]{1,0:T(8,128)(2,1)S(1)} %pad_maximum_fusion), channel_id=1, source_target_pairs={{0,96},{1,97},{2,98},{3,99},{4,100},{5,101},{6,102},{7,103},{8,104... | collective-permute-start | bytes 3833864 | tf_op jit(solution)/shard_map/ppermute | solution.py:352
  36.1 6.9 %collective-permute-start.12 = (bf16[208,768]{1,0:T(8,128)(2,1)S(1)}, bf16[208,768]{1,0:T(8,128)(2,1)S(1)}, u32[]{:S(2)}, u32[]{:S(2)}) collective-permute-start(bf16[208,768]{1,0:T(8,128)(2,1)S(1)} %pack.3.refs_3_.refs_5_.refs_1_), channel_id=1, source_target_pairs={{0,16},{1,17},{2,18},{3,19},{4,20},{5,21},{6,22},{7,23},{8,24},{9,... | collective-permute-start | bytes 958472 | tf_op jit(solution)/shard_map/ppermute | solution.py:352
  43.2 2.3 %collective-permute-start.10 = (bf16[416,768]{1,0:T(8,128)(2,1)S(1)}, bf16[416,768]{1,0:T(8,128)(2,1)S(1)}, u32[]{:S(2)}, u32[]{:S(2)}) collective-permute-start(bf16[416,768]{1,0:T(8,128)(2,1)S(1)} %pad_maximum_fusion.1), channel_id=1, source_target_pairs={{0,12},{1,13},{2,14},{3,15},{4,8},{5,9},{6,10},{7,11},{8,4},{9,5},... | collective-permute-start | bytes 1916936 | tf_op jit(solution)/shard_map/ppermute | solution.py:352
  45.9 6.9 %flash.5 = (f32[576,1]{1,0:T(8,128)S(1)}, f32[576,1]{1,0:T(8,128)S(1)}, f32[576,768]{1,0:T(8,128)S(1)}, f32[576,1]{1,0:T(8,128)S(1)}, f32[576,1]{1,0:T(8,128)S(1)}, /*index=5*/f32[576,768]{1,0:T(8,128)S(1)}) custom-call(bf16[416,768]{1,0:T(8,128)(2,1)S(1)} %collective-permute-done.11.refs_0_, bf16[208,768]{1,0:T(8,128)(2,1)S(1)} %collective-permute-done.12.refs_1_, ...), custom_call_target="tpu_custom_call" | custom-call | flops 8153726976 | bytes 7077888 | tf_op jit(solution)/shard_map/flash/pallas_call | solution.py:245
  52.9 7.6 %collective-permute-done.10.refs_5_ = bf16[416,768]{1,0:T(8,128)(2,1)S(1)} collective-permute-done((bf16[416,768]{1,0:T(8,128)(2,1)S(1)}, bf16[416,768]{1,0:T(8,128)(2,1)S(1)}, u32[]{:S(2)}, u32[]{:S(2)}) %collective-permute-start.10) | collective-permute-done | bytes 639008 | tf_op jit(solution)/shard_map/ppermute | solution.py:352
  60.4 2.3 %collective-permute-start.14 = (bf16[416,768]{1,0:T(8,128)(2,1)S(1)}, bf16[416,768]{1,0:T(8,128)(2,1)S(1)}, u32[]{:S(2)}, u32[]{:S(2)}) collective-permute-start(bf16[416,768]{1,0:T(8,128)(2,1)S(1)} %collective-permute-done.10.refs_5_), channel_id=1, source_target_pairs={{0,96},{1,97},{2,98},{3,99},{4,100},{5,101},{6,102},{7,103},{8,104... | collective-permute-start | bytes 1916936 | tf_op jit(solution)/shard_map/ppermute | solution.py:352
  62.7 4.6 %collective-permute-start.13 = (bf16[832,768]{1,0:T(8,128)(2,1)S(1)}, bf16[832,768]{1,0:T(8,128)(2,1)S(1)}, u32[]{:S(2)}, u32[]{:S(2)}) collective-permute-start(bf16[832,768]{1,0:T(8,128)(2,1)S(1)} %collective-permute-done.9.refs_4_), channel_id=1, source_target_pairs={{0,3},{1,2},{2,1},{3,0},{4,7},{5,6},{6,5},{7,4},{8,11},{9,10},{10,... | collective-permute-start | bytes 3833864 | tf_op jit(solution)/shard_map/ppermute | solution.py:352
  67.3 7.5 %flash.6 = (f32[576,1]{1,0:T(8,128)S(1)}, f32[576,1]{1,0:T(8,128)S(1)}, f32[576,768]{1,0:T(8,128)S(1)}, f32[576,1]{1,0:T(8,128)S(1)}, f32[576,1]{1,0:T(8,128)S(1)}, /*index=5*/f32[576,768]{1,0:T(8,128)S(1)}) custom-call(bf16[416,768]{1,0:T(8,128)(2,1)S(1)} %collective-permute-done.11.refs_0_, bf16[208,768]{1,0:T(8,128)(2,1)S(1)} %collective-permute-done.12.refs_1_, ...), custom_call_target="tpu_custom_call" | custom-call | flops 8153726976 | bytes 7077888 | tf_op jit(solution)/shard_map/flash/pallas_call | solution.py:245
  74.8 7.6 %flash.7 = (f32[576,1]{1,0:T(8,128)S(1)}, f32[576,1]{1,0:T(8,128)S(1)}, f32[576,768]{1,0:T(8,128)S(1)}, f32[576,1]{1,0:T(8,128)S(1)}, f32[576,1]{1,0:T(8,128)S(1)}, /*index=5*/f32[576,768]{1,0:T(8,128)S(1)}) custom-call(bf16[416,768]{1,0:T(8,128)(2,1)S(1)} %collective-permute-done.11.refs_0_, bf16[208,768]{1,0:T(8,128)(2,1)S(1)} %collective-permute-done.12.refs_1_, ...), custom_call_target="tpu_custom_call" | custom-call | flops 8153726976 | bytes 7077888 | tf_op jit(solution)/shard_map/flash/pallas_call | solution.py:245
  82.4 5.5 %collective-permute-done.13.refs_2_ = bf16[832,768]{1,0:T(8,128)(2,1)S(1)} collective-permute-done((bf16[832,768]{1,0:T(8,128)(2,1)S(1)}, bf16[832,768]{1,0:T(8,128)(2,1)S(1)}, u32[]{:S(2)}, u32[]{:S(2)}) %collective-permute-start.13) | collective-permute-done | bytes 1277984 | tf_op jit(solution)/shard_map/ppermute | solution.py:352
  87.9 4.0 %flash.9 = bf16[592,768]{1,0:T(8,128)(2,1)S(1)} custom-call(bf16[416,768]{1,0:T(8,128)(2,1)S(1)} %collective-permute-done.11.refs_0_, bf16[208,768]{1,0:T(8,128)(2,1)S(1)} %collective-permute-done.12.refs_1_, bf16[832,768]{1,0:T(8,128)(2,1)S(1)} %collective-permute-done.13.refs_2_, bf16[416,768]{1,0:T(8,128)(2,1)S(1)} %collective-permute-done.14.refs_3_, ...), custom_call_target="tpu_custom_call" | custom-call | flops 4076863488 | bytes 4423680 | tf_op jit(solution)/shard_map/flash/pallas_call | solution.py:245
  92.2 4.0 %flash.8 = (f32[576,1]{1,0:T(8,128)S(1)}, f32[576,1]{1,0:T(8,128)S(1)}, f32[576,768]{1,0:T(8,128)S(1)}) custom-call(bf16[416,768]{1,0:T(8,128)(2,1)S(1)} %pack.2.refs_2_.refs_4_.refs_0_, bf16[208,768]{1,0:T(8,128)(2,1)S(1)} %pack.3.refs_3_.refs_5_.refs_1_, bf16[832,768]{1,0:T(8,128)(2,1)S(1)} %collective-permute-done.13.refs_2_, ...), custom_call_target="tpu_custom_call" | custom-call | flops 4076863488 | bytes 4423680 | tf_op jit(solution)/shard_map/flash/pallas_call | solution.py:245
  98.3 1.9 %collective-permute-start.21 = (bf16[80,768]{1,0:T(8,128)(2,1)S(1)}, bf16[80,768]{1,0:T(8,128)(2,1)S(1)}, u32[]{:S(2)}, u32[]{:S(2)}) collective-permute-start(bf16[80,768]{1,0:T(8,128)(2,1)S(1)} %get-tuple-element.86), channel_id=1, source_target_pairs={{0,36},{1,37},{2,38},{3,39},{4,32},{5,33},{6,34},{7,35},{8,44},{9,... | collective-permute-start | bytes 368648 | tf_op jit(solution)/shard_map/ppermute | solution.py:352
  102.1 2.4 %collective-permute-start.24 = (bf16[80,768]{1,0:T(8,128)(2,1)S(1)}, bf16[80,768]{1,0:T(8,128)(2,1)S(1)}, u32[]{:S(2)}, u32[]{:S(2)}) collective-permute-start(bf16[80,768]{1,0:T(8,128)(2,1)S(1)} %get-tuple-element.89), channel_id=1, source_target_pairs={{0,37},{1,36},{2,39},{3,38},{4,33},{5,32},{6,35},{7,34},{8,45},{9,... | collective-permute-start | bytes 368648 | tf_op jit(solution)/shard_map/ppermute | solution.py:352
  104.7 2.2 %collective-permute-done.22.refs_5_ = bf16[80,768]{1,0:T(8,128)(2,1)S(1)} collective-permute-done((bf16[80,768]{1,0:T(8,128)(2,1)S(1)}, bf16[80,768]{1,0:T(8,128)(2,1)S(1)}, u32[]{:S(2)}, u32[]{:S(2)}) %collective-permute-start.22) | collective-permute-done | bytes 122912 | tf_op jit(solution)/shard_map/ppermute | solution.py:352
  106.9 4.5 %collective-permute-done.23.refs_6_ = bf16[80,768]{1,0:T(8,128)(2,1)S(1)} collective-permute-done((bf16[80,768]{1,0:T(8,128)(2,1)S(1)}, bf16[80,768]{1,0:T(8,128)(2,1)S(1)}, u32[]{:S(2)}, u32[]{:S(2)}) %collective-permute-start.23) | collective-permute-done | bytes 122912 | tf_op jit(solution)/shard_map/ppermute | solution.py:352
  111.4 2.3 %final.1 = (bf16[384,768]{1,0:T(8,128)(2,1)}, f32[384]{0:T(512)}) custom-call(s32[1]{0:T(128)} %bitcast.me_ref, s32[32]{0:T(128)S(1)} %copy-done.4, s32[384]{0:T(512)S(1)} %copy-done.2, bf16[80,768]{1,0:T(8,128)(2,1)S(1)} %get-tuple-element.82.refs_0_, bf16[80,768]{1,0:T(8,128)(2,1)S(1)} %collective-permute-done.18.refs_1_, ...), custom_call_target="tpu_custom_call" | custom-call | tf_op jit(solution)/shard_map/final/pallas_call | solution.py:399
  (40 shorter events, 6.9 us)
Async XLA Ops:
  0.8 1.1 copy-start
  1.8 0.7 copy-start.1
  2.5 0.7 copy-start.3
  5.3 6.1 %collective-permute-start = (bf16[80,768]{1,0:T(8,128)(2,1)S(1)}, bf16[80,768]{1,0:T(8,128)(2,1)S(1)}, u32[]{:S(2)}, u32[]{:S(2)}) collective-permute-start(bf16[80,768]{1,0:T(8,128)(2,1)S(1)} %get-tuple-element.47), channel_id=1, source_target_pairs={{0,4},{1,5},{2,6},{3,7},{4,0},{5,1},{6,2},{7,3},{8,12},{9,13},{10,... | collective-permute-start | bytes 368648 | tf_op jit(solution)/shard_map/ppermute | solution.py:352
  7.4 4.0 %collective-permute-start.1 = (bf16[80,768]{1,0:T(8,128)(2,1)S(1)}, bf16[80,768]{1,0:T(8,128)(2,1)S(1)}, u32[]{:S(2)}, u32[]{:S(2)}) collective-permute-start(bf16[80,768]{1,0:T(8,128)(2,1)S(1)} %get-tuple-element.48), channel_id=1, source_target_pairs={{0,32},{1,33},{2,34},{3,35},{4,36},{5,37},{6,38},{7,39},{8,40},{9,... | collective-permute-start | bytes 368648 | tf_op jit(solution)/shard_map/ppermute | solution.py:352
  8.7 4.1 %collective-permute-start.2 = (bf16[80,768]{1,0:T(8,128)(2,1)S(1)}, bf16[80,768]{1,0:T(8,128)(2,1)S(1)}, u32[]{:S(2)}, u32[]{:S(2)}) collective-permute-start(bf16[80,768]{1,0:T(8,128)(2,1)S(1)} %get-tuple-element.49), channel_id=1, source_target_pairs={{0,1},{1,0},{2,3},{3,2},{4,5},{5,4},{6,7},{7,6},{8,9},{9,8},{10,11... | collective-permute-start | bytes 368648 | tf_op jit(solution)/shard_map/ppermute | solution.py:352
  10.3 4.6 %collective-permute-start.3 = (bf16[80,768]{1,0:T(8,128)(2,1)S(1)}, bf16[80,768]{1,0:T(8,128)(2,1)S(1)}, u32[]{:S(2)}, u32[]{:S(2)}) collective-permute-start(bf16[80,768]{1,0:T(8,128)(2,1)S(1)} %get-tuple-element.50), channel_id=1, source_target_pairs={{0,36},{1,37},{2,38},{3,39},{4,32},{5,33},{6,34},{7,35},{8,44},{9,... | collective-permute-start | bytes 368648 | tf_op jit(solution)/shard_map/ppermute | solution.py:352
  10.5 6.0 %collective-permute-start.4 = (bf16[80,768]{1,0:T(8,128)(2,1)S(1)}, bf16[80,768]{1,0:T(8,128)(2,1)S(1)}, u32[]{:S(2)}, u32[]{:S(2)}) collective-permute-start(bf16[80,768]{1,0:T(8,128)(2,1)S(1)} %get-tuple-element.51), channel_id=1, source_target_pairs={{0,5},{1,4},{2,7},{3,6},{4,1},{5,0},{6,3},{7,2},{8,13},{9,12},{10,... | collective-permute-start | bytes 368648 | tf_op jit(solution)/shard_map/ppermute | solution.py:352
  16.6 16.8 %collective-permute-start.7 = (bf16[416,768]{1,0:T(8,128)(2,1)S(1)}, bf16[416,768]{1,0:T(8,128)(2,1)S(1)}, u32[]{:S(2)}, u32[]{:S(2)}) collective-permute-start(bf16[416,768]{1,0:T(8,128)(2,1)S(1)} %pack.2.refs_2_.refs_4_.refs_0_), channel_id=1, source_target_pairs={{0,12},{1,13},{2,14},{3,15},{4,8},{5,9},{6,10},{7,11},{8,4},{9,5},... | collective-permute-start | bytes 1916936 | tf_op jit(solution)/shard_map/ppermute | solution.py:352
  19.5 4.9 %collective-permute-start.5 = (bf16[80,768]{1,0:T(8,128)(2,1)S(1)}, bf16[80,768]{1,0:T(8,128)(2,1)S(1)}, u32[]{:S(2)}, u32[]{:S(2)}) collective-permute-start(bf16[80,768]{1,0:T(8,128)(2,1)S(1)} %get-tuple-element.52), channel_id=1, source_target_pairs={{0,33},{1,32},{2,35},{3,34},{4,37},{5,36},{6,39},{7,38},{8,41},{9,... | collective-permute-start | bytes 368648 | tf_op jit(solution)/shard_map/ppermute | solution.py:352
  19.8 5.7 %collective-permute-start.6 = (bf16[80,768]{1,0:T(8,128)(2,1)S(1)}, bf16[80,768]{1,0:T(8,128)(2,1)S(1)}, u32[]{:S(2)}, u32[]{:S(2)}) collective-permute-start(bf16[80,768]{1,0:T(8,128)(2,1)S(1)} %get-tuple-element.53), channel_id=1, source_target_pairs={{0,37},{1,36},{2,39},{3,38},{4,33},{5,32},{6,35},{7,34},{8,45},{9,... | collective-permute-start | bytes 368648 | tf_op jit(solution)/shard_map/ppermute | solution.py:352
  25.5 7.9 %collective-permute-start.8 = (bf16[208,768]{1,0:T(8,128)(2,1)S(1)}, bf16[208,768]{1,0:T(8,128)(2,1)S(1)}, u32[]{:S(2)}, u32[]{:S(2)}) collective-permute-start(bf16[208,768]{1,0:T(8,128)(2,1)S(1)} %pack.3.refs_3_.refs_5_.refs_1_), channel_id=1, source_target_pairs={{0,3},{1,2},{2,1},{3,0},{4,7},{5,6},{6,5},{7,4},{8,11},{9,10},{10,... | collective-permute-start | bytes 958472 | tf_op jit(solution)/shard_map/ppermute | solution.py:352
  28.9 17.0 %collective-permute-start.11 = (bf16[416,768]{1,0:T(8,128)(2,1)S(1)}, bf16[416,768]{1,0:T(8,128)(2,1)S(1)}, u32[]{:S(2)}, u32[]{:S(2)}) collective-permute-start(bf16[416,768]{1,0:T(8,128)(2,1)S(1)} %pack.2.refs_2_.refs_4_.refs_0_), channel_id=1, source_target_pairs={{0,16},{1,17},{2,18},{3,19},{4,20},{5,21},{6,22},{7,23},{8,24},{9,... | collective-permute-start | bytes 1916936 | tf_op jit(solution)/shard_map/ppermute | solution.py:352
  33.5 27.0 %collective-permute-start.9 = (bf16[832,768]{1,0:T(8,128)(2,1)S(1)}, bf16[832,768]{1,0:T(8,128)(2,1)S(1)}, u32[]{:S(2)}, u32[]{:S(2)}) collective-permute-start(bf16[832,768]{1,0:T(8,128)(2,1)S(1)} %pad_maximum_fusion), channel_id=1, source_target_pairs={{0,96},{1,97},{2,98},{3,99},{4,100},{5,101},{6,102},{7,103},{8,104... | collective-permute-start | bytes 3833864 | tf_op jit(solution)/shard_map/ppermute | solution.py:352
  36.1 9.4 %collective-permute-start.12 = (bf16[208,768]{1,0:T(8,128)(2,1)S(1)}, bf16[208,768]{1,0:T(8,128)(2,1)S(1)}, u32[]{:S(2)}, u32[]{:S(2)}) collective-permute-start(bf16[208,768]{1,0:T(8,128)(2,1)S(1)} %pack.3.refs_3_.refs_5_.refs_1_), channel_id=1, source_target_pairs={{0,16},{1,17},{2,18},{3,19},{4,20},{5,21},{6,22},{7,23},{8,24},{9,... | collective-permute-start | bytes 958472 | tf_op jit(solution)/shard_map/ppermute | solution.py:352
  43.1 31.7 %collective-permute-start.16 = (bf16[416,768]{1,0:T(8,128)(2,1)S(1)}, bf16[416,768]{1,0:T(8,128)(2,1)S(1)}, u32[]{:S(2)}, u32[]{:S(2)}) collective-permute-start(bf16[416,768]{1,0:T(8,128)(2,1)S(1)} %pad_maximum_fusion.1), channel_id=1, source_target_pairs={{0,96},{1,97},{2,98},{3,99},{4,100},{5,101},{6,102},{7,103},{8,104... | collective-permute-start | bytes 1916936 | tf_op jit(solution)/shard_map/ppermute | solution.py:352
  43.2 17.3 %collective-permute-start.10 = (bf16[416,768]{1,0:T(8,128)(2,1)S(1)}, bf16[416,768]{1,0:T(8,128)(2,1)S(1)}, u32[]{:S(2)}, u32[]{:S(2)}) collective-permute-start(bf16[416,768]{1,0:T(8,128)(2,1)S(1)} %pad_maximum_fusion.1), channel_id=1, source_target_pairs={{0,12},{1,13},{2,14},{3,15},{4,8},{5,9},{6,10},{7,11},{8,4},{9,5},... | collective-permute-start | bytes 1916936 | tf_op jit(solution)/shard_map/ppermute | solution.py:352
  45.5 29.3 %collective-permute-start.15 = (bf16[832,768]{1,0:T(8,128)(2,1)S(1)}, bf16[832,768]{1,0:T(8,128)(2,1)S(1)}, u32[]{:S(2)}, u32[]{:S(2)}) collective-permute-start(bf16[832,768]{1,0:T(8,128)(2,1)S(1)} %pad_maximum_fusion), channel_id=1, source_target_pairs={{0,3},{1,2},{2,1},{3,0},{4,7},{5,6},{6,5},{7,4},{8,11},{9,10},{10,... | collective-permute-start | bytes 3833864 | tf_op jit(solution)/shard_map/ppermute | solution.py:352
  60.4 22.0 %collective-permute-start.14 = (bf16[416,768]{1,0:T(8,128)(2,1)S(1)}, bf16[416,768]{1,0:T(8,128)(2,1)S(1)}, u32[]{:S(2)}, u32[]{:S(2)}) collective-permute-start(bf16[416,768]{1,0:T(8,128)(2,1)S(1)} %collective-permute-done.10.refs_5_), channel_id=1, source_target_pairs={{0,96},{1,97},{2,98},{3,99},{4,100},{5,101},{6,102},{7,103},{8,104... | collective-permute-start | bytes 1916936 | tf_op jit(solution)/shard_map/ppermute | solution.py:352
  62.7 25.2 %collective-permute-start.13 = (bf16[832,768]{1,0:T(8,128)(2,1)S(1)}, bf16[832,768]{1,0:T(8,128)(2,1)S(1)}, u32[]{:S(2)}, u32[]{:S(2)}) collective-permute-start(bf16[832,768]{1,0:T(8,128)(2,1)S(1)} %collective-permute-done.9.refs_4_), channel_id=1, source_target_pairs={{0,3},{1,2},{2,1},{3,0},{4,7},{5,6},{6,5},{7,4},{8,11},{9,10},{10,... | collective-permute-start | bytes 3833864 | tf_op jit(solution)/shard_map/ppermute | solution.py:352
  92.0 4.3 %collective-permute-start.17 = (bf16[592,768]{1,0:T(8,128)(2,1)S(1)}, bf16[592,768]{1,0:T(8,128)(2,1)S(1)}, u32[]{:S(2)}, u32[]{:S(2)}) collective-permute-start(bf16[592,768]{1,0:T(8,128)(2,1)S(1)} %flash.9), channel_id=1, source_target_pairs={{0,16},{1,17},{2,18},{3,19},{4,20},{5,21},{6,22},{7,23},{8,24},{9,... | collective-permute-start | bytes 2727944 | tf_op jit(solution)/shard_map/ppermute | solution.py:352
  96.2 15.2 %copy-start.2 = (s32[384]{0:T(512)S(1)}, s32[384]{0:T(512)}, u32[]{:S(2)}) copy-start(s32[384]{0:T(512)} %clusters_ref.3) | copy-start | bytes 4612
  96.2 15.2 %copy-start.4 = (s32[32]{0:T(128)S(1)}, s32[32]{0:T(128)}, u32[]{:S(2)}) copy-start(s32[32]{0:T(128)} %owner_ref.3) | copy-start | bytes 388
  97.0 4.6 %collective-permute-start.18 = (bf16[80,768]{1,0:T(8,128)(2,1)S(1)}, bf16[80,768]{1,0:T(8,128)(2,1)S(1)}, u32[]{:S(2)}, u32[]{:S(2)}) collective-permute-start(bf16[80,768]{1,0:T(8,128)(2,1)S(1)} %get-tuple-element.83), channel_id=1, source_target_pairs={{0,4},{1,5},{2,6},{3,7},{4,0},{5,1},{6,2},{7,3},{8,12},{9,13},{10,... | collective-permute-start | bytes 368648 | tf_op jit(solution)/shard_map/ppermute | solution.py:352
  97.1 5.0 %collective-permute-start.19 = (bf16[80,768]{1,0:T(8,128)(2,1)S(1)}, bf16[80,768]{1,0:T(8,128)(2,1)S(1)}, u32[]{:S(2)}, u32[]{:S(2)}) collective-permute-start(bf16[80,768]{1,0:T(8,128)(2,1)S(1)} %get-tuple-element.84), channel_id=1, source_target_pairs={{0,32},{1,33},{2,34},{3,35},{4,36},{5,37},{6,38},{7,39},{8,40},{9,... | collective-permute-start | bytes 368648 | tf_op jit(solution)/shard_map/ppermute | solution.py:352
  97.9 6.6 %collective-permute-start.20 = (bf16[80,768]{1,0:T(8,128)(2,1)S(1)}, bf16[80,768]{1,0:T(8,128)(2,1)S(1)}, u32[]{:S(2)}, u32[]{:S(2)}) collective-permute-start(bf16[80,768]{1,0:T(8,128)(2,1)S(1)} %get-tuple-element.85), channel_id=1, source_target_pairs={{0,1},{1,0},{2,3},{3,2},{4,5},{5,4},{6,7},{7,6},{8,9},{9,8},{10,11... | collective-permute-start | bytes 368648 | tf_op jit(solution)/shard_map/ppermute | solution.py:352
  98.3 6.4 %collective-permute-start.21 = (bf16[80,768]{1,0:T(8,128)(2,1)S(1)}, bf16[80,768]{1,0:T(8,128)(2,1)S(1)}, u32[]{:S(2)}, u32[]{:S(2)}) collective-permute-start(bf16[80,768]{1,0:T(8,128)(2,1)S(1)} %get-tuple-element.86), channel_id=1, source_target_pairs={{0,36},{1,37},{2,38},{3,39},{4,32},{5,33},{6,34},{7,35},{8,44},{9,... | collective-permute-start | bytes 368648 | tf_op jit(solution)/shard_map/ppermute | solution.py:352
  100.2 6.6 %collective-permute-start.22 = (bf16[80,768]{1,0:T(8,128)(2,1)S(1)}, bf16[80,768]{1,0:T(8,128)(2,1)S(1)}, u32[]{:S(2)}, u32[]{:S(2)}) collective-permute-start(bf16[80,768]{1,0:T(8,128)(2,1)S(1)} %get-tuple-element.87), channel_id=1, source_target_pairs={{0,5},{1,4},{2,7},{3,6},{4,1},{5,0},{6,3},{7,2},{8,13},{9,12},{10,... | collective-permute-start | bytes 368648 | tf_op jit(solution)/shard_map/ppermute | solution.py:352
  101.7 9.7 %collective-permute-start.23 = (bf16[80,768]{1,0:T(8,128)(2,1)S(1)}, bf16[80,768]{1,0:T(8,128)(2,1)S(1)}, u32[]{:S(2)}, u32[]{:S(2)}) collective-permute-start(bf16[80,768]{1,0:T(8,128)(2,1)S(1)} %get-tuple-element.88), channel_id=1, source_target_pairs={{0,33},{1,32},{2,35},{3,34},{4,37},{5,36},{6,39},{7,38},{8,41},{9,... | collective-permute-start | bytes 368648 | tf_op jit(solution)/shard_map/ppermute | solution.py:352
  102.1 9.3 %collective-permute-start.24 = (bf16[80,768]{1,0:T(8,128)(2,1)S(1)}, bf16[80,768]{1,0:T(8,128)(2,1)S(1)}, u32[]{:S(2)}, u32[]{:S(2)}) collective-permute-start(bf16[80,768]{1,0:T(8,128)(2,1)S(1)} %get-tuple-element.89), channel_id=1, source_target_pairs={{0,37},{1,36},{2,39},{3,38},{4,33},{5,32},{6,35},{7,34},{8,45},{9,... | collective-permute-start | bytes 368648 | tf_op jit(solution)/shard_map/ppermute | solution.py:352

commit v4 on v3

--- a/solution.py
+++ b/solution.py
@@ -18,7 +18,8 @@
 filled = 72
 packet_rows = 80
 block_keys = 192
-block_rows = 208
+big_rows = 400
+small_rows = 200
 query_rows = 288
 f32 = jnp.float32
 bf16 = jnp.bfloat16
@@ -60,12 +61,24 @@
     return hits(count, target).astype(f32).astype(bf16)
 
 
-def place_kernel(me_ref, owner_ref, clusters_ref, rows_ref, *out_refs):
+def place_kernel(me_ref, owner_hbm, clusters_hbm, rows_hbm, *refs):
+    out_refs, (owner_ref, clusters_ref, rows_ref, done) = refs[:8], refs[8:]
+    copies = [
+        pltpu.make_async_copy(source, target, done.at[n])
+        for n, (source, target) in enumerate(
+            ((owner_hbm, owner_ref), (clusters_hbm, clusters_ref), (rows_hbm, rows_ref))
+        )
+    ]
+    for copy in copies:
+        copy.start()
+    copies[0].wait()
+    copies[1].wait()
     cluster, packet, rank, part, lane = row_facts(
         clusters_ref[...].reshape(1, clusters_ref.shape[0]), owner_ref, me_ref[0]
     )
     width = rows_ref.shape[1]
     total = 8 * packet_rows
+    copies[2].wait()
     placed = jnp.dot(
         ones_at(total, packet * packet_rows + rank), rows_ref[...], preferred_element_type=f32
     )
@@ -94,31 +107,33 @@
     return found
 
 
-def pack_kernel(blocks, names, *refs):
-    packets = {n: ref[...].astype(f32) for n, ref in zip(names, refs)}
-    out_ref = refs[-1]
-    for k, p in enumerate(blocks):
-        rows = [packets[n][low:high] for n, low, high in spans(p)]
-        ids = sum(packets[n][filled : filled + 8] for n, _, _ in spans(p))
-        at = lax.broadcasted_iota(jnp.int32, ids.shape, 0)
-        row = jnp.sum(jnp.where(at == p, ids, 0.0), axis=0, keepdims=True)
-        tail = jnp.where(at == 0, row, 0.0)
-        out_ref[k * block_rows : (k + 1) * block_rows, :] = jnp.concatenate(
-            rows + [tail, jnp.zeros_like(tail)], axis=0
-        ).astype(bf16)
-
-
-def pack(blocks, packets):
-    names = sorted({n for p in blocks for n, _, _ in spans(p)})
+def pack_kernel(*refs):
+    packets = [ref[...].astype(f32) for ref in refs[:8]]
+    big_ref, small_ref = refs[8:]
+    blocks = [
+        jnp.concatenate([packets[n][low:high] for n, low, high in spans(p)], axis=0)
+        for p in range(parts)
+    ]
+    ids = sum(packet[filled:packet_rows] for packet in packets)
+    at = lax.broadcasted_iota(jnp.int32, ids.shape, 0)
+    big_ref[0 : 2 * block_keys, :] = jnp.concatenate(blocks[:2], axis=0).astype(bf16)
+    big_ref[2 * block_keys : big_rows, :] = jnp.concatenate(
+        [jnp.where(at < 2, ids, 0.0), jnp.zeros_like(ids)], axis=0
+    ).astype(bf16)
+    last = jnp.sum(jnp.where(at == 2, ids, 0.0), axis=0, keepdims=True)
+    small_ref[...] = jnp.concatenate([blocks[2], jnp.where(at == 0, last, 0.0)], axis=0).astype(bf16)
+
+
+def pack(packets):
     width = packets[0].shape[1]
     return pl.pallas_call(
-        functools.partial(pack_kernel, blocks, names),
-        out_shape=jax.ShapeDtypeStruct((len(blocks) * block_rows, width), bf16),
-        in_specs=vmem_specs(len(names)),
-        out_specs=vmem_specs(1)[0],
+        pack_kernel,
+        out_shape=[jax.ShapeDtypeStruct((count, width), bf16) for count in (big_rows, small_rows)],
+        in_specs=vmem_specs(8),
+        out_specs=vmem_specs(2),
         compiler_params=params,
         name="pack",
-    )(*[packets[n] for n in names])
+    )(*packets)
 
 
 def column_of(row):
@@ -143,44 +158,42 @@
     return high, value - high
 
 
-def gather_keys(key_refs, blocks, keys):
+def gather_rows(refs, wides, store):
     id_rows = []
-    number = 0
-    for ref, count in zip(key_refs, blocks):
-        for b in range(count):
-            keys[number * block_keys : (number + 1) * block_keys, :] = ref[
-                b * block_rows : b * block_rows + block_keys, :
-            ]
-            ids = ref[b * block_rows + block_keys : (b + 1) * block_rows, 0:256].astype(f32)
-            id_rows.append(ids[0:8])
-            number += 1
+    for ref, wide in zip(refs, wides):
+        step, count = (big_rows, 2) if wide else (small_rows, 1)
+        for start in range(0, ref.shape[0], step):
+            end = start + count * block_keys
+            first = len(id_rows) * block_keys
+            store[first : first + count * block_keys, :] = ref[start:end, :]
+            ids = ref[end : end + 8 * count, 0:256].astype(f32)[0:8]
+            id_rows += [ids, pltpu.roll(ids, 7, 0)][:count]
+    return id_rows
+
+
+def side_by_side(id_rows):
     pieces = []
-    for b in range(0, number, 2):
-        even = id_rows[b]
-        odd = pltpu.roll(id_rows[b + 1], 64, 1)
+    for even, odd in zip(id_rows[::2], id_rows[1::2]):
+        odd = pltpu.roll(odd, 64, 1)
         pieces += [even[:, 0:128], even[:, 128:256] + odd[:, 0:128], odd[:, 128:256]]
     return jnp.concatenate(pieces, axis=1)[0:1]
 
 
-def flash_kernel(blocks, first, owns, finish, *refs):
+def flash_kernel(wides, first, owns, finish, *refs):
     refs = list(refs)
     count = len(owns)
     q_refs = [[refs.pop(0), refs.pop(0)] for _ in range(count)]
-    key_refs = [refs.pop(0) for _ in blocks]
+    key_refs = [refs.pop(0) for _ in wides]
     states = None if first else [[refs.pop(0) for _ in range(3)] for _ in range(count)]
     outs = [[refs.pop(0)] if finish else [refs.pop(0) for _ in range(3)] for _ in range(count)]
     keys, queries, labels = refs
     width = q_refs[0][0].shape[1]
     scale = score_scale / math.sqrt(width) * log2e
-    key_id = gather_keys(key_refs, blocks, keys)
+    key_id = side_by_side(gather_rows(key_refs, wides, keys))
     other = jnp.where(key_id == 0.0, masked, -penalty * log2e)
     for n in range(count):
-        for p in range(parts):
-            at = slice(p * block_keys, (p + 1) * block_keys)
-            ref, first_row = q_refs[n][p // 2], (p % 2) * block_rows
-            queries[n, at, :] = ref[first_row : first_row + block_keys, :]
-            ids = ref[first_row + block_keys : first_row + block_rows, 0:256]
-            labels[n, at, :] = column_of(ids.astype(f32)[0:1])
+        for p, ids in enumerate(gather_rows(q_refs[n], (True, False), queries.at[n])):
+            labels[n, p * block_keys : (p + 1) * block_keys, :] = column_of(ids[0:1])
     for n in range(count):
         for start in range(0, parts * block_keys, query_rows):
             at = slice(start, start + query_rows)
@@ -228,8 +241,13 @@
 
 def flash(qs, owns, key_arrays, states, finish):
     width = qs[0][0].shape[1]
-    blocks = [a.shape[0] // block_rows for a in key_arrays]
-    total = sum(blocks) * block_keys
+    wides = [wide for _, wide in key_arrays]
+    key_arrays = [a for a, _ in key_arrays]
+    total = sum(
+        a.shape[0] // big_rows * 2 if wide else a.shape[0] // small_rows
+        for a, wide in zip(key_arrays, wides)
+    )
+    total *= block_keys
     rows = parts * block_keys
     first = states is None
     if finish:
@@ -241,9 +259,9 @@
             jax.ShapeDtypeStruct((rows, width), f32),
         ]
     count = len(qs)
-    args = [a for q in qs for a in q] + list(key_arrays) + ([] if first else [a for state in states for a in state])
+    args = [a for q in qs for a in q] + key_arrays + ([] if first else [a for state in states for a in state])
     out = pl.pallas_call(
-        functools.partial(flash_kernel, blocks, first, owns, finish),
+        functools.partial(flash_kernel, wides, first, owns, finish),
         out_shape=each * count,
         in_specs=vmem_specs(len(args)),
         out_specs=vmem_specs(len(each) * count),
@@ -359,13 +377,19 @@
     packets = pl.pallas_call(
         place_kernel,
         out_shape=[packet] * 8,
-        in_specs=[smem, smem] + vmem_specs(2),
+        in_specs=[smem] + [pl.BlockSpec(memory_space=pltpu.HBM)] * 3,
         out_specs=vmem_specs(8),
+        scratch_shapes=[
+            pltpu.SMEM(cluster_owner.shape, jnp.int32),
+            pltpu.VMEM(clusters.shape, jnp.int32),
+            pltpu.VMEM(embeddings.shape, bf16),
+            pltpu.SemaphoreType.DMA((3,)),
+        ],
         compiler_params=params,
         name="place",
     )(me, cluster_owner, clusters, embeddings)
     arrived = [packets[0]] + [send(packets[n], trips[n]) for n in range(1, 8)]
-    big, small = pack((0, 1), arrived), pack((2,), arrived)
+    big, small = pack(arrived)
     wide = [
         [pair for pair in dims[s % 3] if pair[0] // 16 % 2 == 0]
         + [pair for pair in dims[(s + 1) % 3] if pair[0] // 16 % 2 == 1]
@@ -377,15 +401,16 @@
     big0, small0 = lax.optimization_barrier((big0, small0))
     big, small = jnp.concatenate([big, big0], axis=0), jnp.concatenate([small, small0], axis=0)
     big1, small1 = send(big, wide[1]), send(small, narrow[1])
+    queries, owns = [q_other, q_own], [False, True]
+    pairs = lambda *units: list(zip(units, (True, False) * 2))
+    states = flash(queries, owns, pairs(*q_own, big0, small0), None, False)
+    big, small, states[1] = lax.optimization_barrier((big, small, states[1]))
     big2, small2 = send(big, wide[2]), send(small, narrow[2])
-    queries, owns = [q_other, q_own], [False, True]
-    states = flash(queries, owns, [*q_own, big0, small0], None, False)
-    big1, small1, states[1] = lax.optimization_barrier((big1, small1, states[1]))
     big3, small3 = send(big1, wide[2]), send(small1, narrow[2])
-    states = flash(queries, owns, [big1, small1], states, False)
-    states = flash(queries, owns, [big2, small2], states, False)
-    (partial,) = flash(queries[:1], owns[:1], [big3, small3], states[:1], True)
-    (mine,) = flash(queries[1:], owns[1:], [big3, small3], states[1:], False)
+    states = flash(queries, owns, pairs(big1, small1), states, False)
+    states = flash(queries, owns, pairs(big2, small2), states, False)
+    (partial,) = flash(queries[:1], owns[:1], pairs(big3, small3), states[:1], True)
+    (mine,) = flash(queries[1:], owns[1:], pairs(big3, small3), states[1:], False)
     theirs = send(partial, swap)
     answers = pl.pallas_call(
         combine_kernel,

time: 114 us -> 109 us (0.956)
  starting transfers between devices: 46.9 us -> 38.3 us
  waiting for transfers between devices: 28 us -> 31.2 us
    ppermute x25, starting transfers between devices: 46.9 us -> 38.3 us  [per_device(): send = lambda a, pairs: lax.ppermute(a, axes, pairs)]
    ppermute x25, waiting for transfers between devices: 28 us -> 31.2 us  [per_device(): send = lambda a, pairs: lax.ppermute(a, axes, pairs)]
    unnamed x10 -> x12, local copies, waits for them, and re-layouts: 2.41 us -> 2.47 us
    pallas_call x8 -> x7, Pallas kernels: 32.2 us -> 32.3 us  [the longest x5 30.1 us: flash(): pl.pallas_call(functools.partial(flash_kernel, wides, first, owns, finish...]
  transfers between devices with their start and end apart: 25 -> 25, of which waited for: 11 -> 16; matrix products, arithmetic and copies ran while one was open for 0% -> 0% of each run, Pallas kernels for 23% -> 24%
where the time goes in v4:
time: 109 us; the launch traced here: 108 us
  starting transfers between devices  38.3 us (35%)
  Pallas kernels  35.3 us (32%)
  waiting for transfers between devices  31.2 us (29%)
  local copies, waits for them, and re-layouts  2.53 us (2%)
    ppermute x25, starting transfers between devices, per_device(): send = lambda a, pairs: lax.ppermute(a, axes, pairs)  38.3 us
    ppermute x25, waiting for transfers between devices, per_device(): send = lambda a, pairs: lax.ppermute(a, axes, pairs)  31.2 us
    pallas_call x5, Pallas kernels, flash(): pl.pallas_call(functools.partial(flash_kernel, wides, first, owns, finish...  30.1 us
    unnamed x12, local copies, waits for them, and re-layouts  2.47 us
    pallas_call x1, Pallas kernels, per_device(): pl.pallas_call(final_kernel, out_shape=[jax.ShapeDtypeStruct((rows, width...  2.26 us
  transfers between devices with their start and end apart: 25, of which 16 were waited for; matrix products, arithmetic and copies ran while one was open for 0% of the time, Pallas kernels for 24%

profile of v4, /device:TPU:1, one launch (start us, length us, event | category | flops | bytes accessed | tf_op | source)
XLA Modules:
  0.0 108.2 jit_solution(13005625545711894029)
XLA Ops:
  0.8 1.1 copy-done
  3.2 2.1 %place.1 = (bf16[80,768]{1,0:T(8,128)(2,1)S(1)}, bf16[80,768]{1,0:T(8,128)(2,1)S(1)}, bf16[80,768]{1,0:T(8,128)(2,1)S(1)}, bf16[80,768]{1,0:T(8,128)(2,1)S(1)}, ...) custom-call(s32[1]{0:T(128)} %bitcast.me_ref, ...), custom_call_target="tpu_custom_call" | custom-call | tf_op jit(solution)/shard_map/place/pallas_call | solution.py:377
  5.3 2.1 %collective-permute-start = (bf16[80,768]{1,0:T(8,128)(2,1)S(1)}, bf16[80,768]{1,0:T(8,128)(2,1)S(1)}, u32[]{:S(2)}, u32[]{:S(2)}) collective-permute-start(bf16[80,768]{1,0:T(8,128)(2,1)S(1)} %get-tuple-element.49), channel_id=1, source_target_pairs={{0,4},{1,5},{2,6},{3,7},{4,0},{5,1},{6,2},{7,3},{8,12},{9,13},{10,... | collective-permute-start | bytes 368648 | tf_op jit(solution)/shard_map/ppermute | solution.py:370
  7.4 1.3 %collective-permute-start.1 = (bf16[80,768]{1,0:T(8,128)(2,1)S(1)}, bf16[80,768]{1,0:T(8,128)(2,1)S(1)}, u32[]{:S(2)}, u32[]{:S(2)}) collective-permute-start(bf16[80,768]{1,0:T(8,128)(2,1)S(1)} %get-tuple-element.50), channel_id=1, source_target_pairs={{0,32},{1,33},{2,34},{3,35},{4,36},{5,37},{6,38},{7,39},{8,40},{9,... | collective-permute-start | bytes 368648 | tf_op jit(solution)/shard_map/ppermute | solution.py:370
  8.7 1.6 %collective-permute-start.2 = (bf16[80,768]{1,0:T(8,128)(2,1)S(1)}, bf16[80,768]{1,0:T(8,128)(2,1)S(1)}, u32[]{:S(2)}, u32[]{:S(2)}) collective-permute-start(bf16[80,768]{1,0:T(8,128)(2,1)S(1)} %get-tuple-element.51), channel_id=1, source_target_pairs={{0,1},{1,0},{2,3},{3,2},{4,5},{5,4},{6,7},{7,6},{8,9},{9,8},{10,11... | collective-permute-start | bytes 368648 | tf_op jit(solution)/shard_map/ppermute | solution.py:370
  11.4 2.5 %collective-permute-start.5 = (bf16[80,768]{1,0:T(8,128)(2,1)S(1)}, bf16[80,768]{1,0:T(8,128)(2,1)S(1)}, u32[]{:S(2)}, u32[]{:S(2)}) collective-permute-start(bf16[80,768]{1,0:T(8,128)(2,1)S(1)} %get-tuple-element.54), channel_id=1, source_target_pairs={{0,33},{1,32},{2,35},{3,34},{4,37},{5,36},{6,39},{7,38},{8,41},{9,... | collective-permute-start | bytes 368648 | tf_op jit(solution)/shard_map/ppermute | solution.py:370
  15.0 1.6 %collective-permute-done.4.refs_5_ = bf16[80,768]{1,0:T(8,128)(2,1)S(1)} collective-permute-done((bf16[80,768]{1,0:T(8,128)(2,1)S(1)}, bf16[80,768]{1,0:T(8,128)(2,1)S(1)}, u32[]{:S(2)}, u32[]{:S(2)}) %collective-permute-start.4) | collective-permute-done | bytes 122912 | tf_op jit(solution)/shard_map/ppermute | solution.py:370
  16.5 2.1 %collective-permute-done.5.refs_6_ = bf16[80,768]{1,0:T(8,128)(2,1)S(1)} collective-permute-done((bf16[80,768]{1,0:T(8,128)(2,1)S(1)}, bf16[80,768]{1,0:T(8,128)(2,1)S(1)}, u32[]{:S(2)}, u32[]{:S(2)}) %collective-permute-start.5) | collective-permute-done | bytes 122912 | tf_op jit(solution)/shard_map/ppermute | solution.py:370
  18.6 1.8 %collective-permute-done.6.refs_7_ = bf16[80,768]{1,0:T(8,128)(2,1)S(1)} collective-permute-done((bf16[80,768]{1,0:T(8,128)(2,1)S(1)}, bf16[80,768]{1,0:T(8,128)(2,1)S(1)}, u32[]{:S(2)}, u32[]{:S(2)}) %collective-permute-start.6) | collective-permute-done | bytes 122912 | tf_op jit(solution)/shard_map/ppermute | solution.py:370
  20.5 4.8 %collective-permute-start.7 = (bf16[400,768]{1,0:T(8,128)(2,1)S(1)}, bf16[400,768]{1,0:T(8,128)(2,1)S(1)}, u32[]{:S(2)}, u32[]{:S(2)}) collective-permute-start(bf16[400,768]{1,0:T(8,128)(2,1)S(1)} %get-tuple-element.56.refs_2_.refs_4_.refs_0_), channel_id=1, source_target_pairs={{0,12},{1,13},{2,14},{3,15},{4,8},{5,9},{6,10},{7,11},{8,4},{9,5},... | collective-permute-start | bytes 1843208 | tf_op jit(solution)/shard_map/ppermute | solution.py:370
  26.1 2.7 %collective-permute-start.8 = (bf16[200,768]{1,0:T(8,128)(2,1)S(1)}, bf16[200,768]{1,0:T(8,128)(2,1)S(1)}, u32[]{:S(2)}, u32[]{:S(2)}) collective-permute-start(bf16[200,768]{1,0:T(8,128)(2,1)S(1)} %get-tuple-element.57.refs_3_.refs_5_.refs_1_), channel_id=1, source_target_pairs={{0,3},{1,2},{2,1},{3,0},{4,7},{5,6},{6,5},{7,4},{8,11},{9,10},{10,... | collective-permute-start | bytes 921608 | tf_op jit(solution)/shard_map/ppermute | solution.py:370
  29.1 7.1 %collective-permute-done.8.refs_7_ = bf16[200,768]{1,0:T(8,128)(2,1)S(1)} collective-permute-done((bf16[200,768]{1,0:T(8,128)(2,1)S(1)}, bf16[200,768]{1,0:T(8,128)(2,1)S(1)}, u32[]{:S(2)}, u32[]{:S(2)}) %collective-permute-start.8) | collective-permute-done | bytes 307232 | tf_op jit(solution)/shard_map/ppermute | solution.py:370
  36.2 1.0 collective-permute-start.11
  37.3 2.6 %collective-permute-start.9 = (bf16[800,768]{1,0:T(8,128)(2,1)S(1)}, bf16[800,768]{1,0:T(8,128)(2,1)S(1)}, u32[]{:S(2)}, u32[]{:S(2)}) collective-permute-start(bf16[800,768]{1,0:T(8,128)(2,1)S(1)} %constant_dynamic-update-slice_fusion), channel_id=1, source_target_pairs={{0,96},{1,97},{2,98},{3,99},{4,100},{5,101},{6,102},{7,103},{8,104... | collective-permute-start | bytes 3686408 | tf_op jit(solution)/shard_map/ppermute | solution.py:370
  40.0 6.9 %flash.5 = (f32[576,1]{1,0:T(8,128)S(1)}, f32[576,1]{1,0:T(8,128)S(1)}, f32[576,768]{1,0:T(8,128)S(1)}, f32[576,1]{1,0:T(8,128)S(1)}, f32[576,1]{1,0:T(8,128)S(1)}, /*index=5*/f32[576,768]{1,0:T(8,128)S(1)}) custom-call(bf16[400,768]{1,0:T(8,128)(2,1)S(1)} %collective-permute-done.13.refs_0_, bf16[200,768]{1,0:T(8,128)(2,1)S(1)} %collective-permute-done.14.refs_1_, ...), custom_call_target="tpu_custom_call" | custom-call | flops 8153726976 | bytes 7077888 | tf_op jit(solution)/shard_map/flash/pallas_call | solution.py:263
  46.8 1.9 %collective-permute-start.15 = (bf16[800,768]{1,0:T(8,128)(2,1)S(1)}, bf16[800,768]{1,0:T(8,128)(2,1)S(1)}, u32[]{:S(2)}, u32[]{:S(2)}) collective-permute-start(bf16[800,768]{1,0:T(8,128)(2,1)S(1)} %constant_dynamic-update-slice_fusion), channel_id=1, source_target_pairs={{0,3},{1,2},{2,1},{3,0},{4,7},{5,6},{6,5},{7,4},{8,11},{9,10},{10,... | collective-permute-start | bytes 3686408 | tf_op jit(solution)/shard_map/ppermute | solution.py:370
  48.7 2.9 %collective-permute-start.16 = (bf16[400,768]{1,0:T(8,128)(2,1)S(1)}, bf16[400,768]{1,0:T(8,128)(2,1)S(1)}, u32[]{:S(2)}, u32[]{:S(2)}) collective-permute-start(bf16[400,768]{1,0:T(8,128)(2,1)S(1)} %constant_dynamic-update-slice_fusion.2), channel_id=1, source_target_pairs={{0,96},{1,97},{2,98},{3,99},{4,100},{5,101},{6,102},{7,103},{8,104... | collective-permute-start | bytes 1843208 | tf_op jit(solution)/shard_map/ppermute | solution.py:370
  52.1 2.9 %collective-permute-start.12 = (bf16[400,768]{1,0:T(8,128)(2,1)S(1)}, bf16[400,768]{1,0:T(8,128)(2,1)S(1)}, u32[]{:S(2)}, u32[]{:S(2)}) collective-permute-start(bf16[400,768]{1,0:T(8,128)(2,1)S(1)} %collective-permute-done.11.refs_5_), channel_id=1, source_target_pairs={{0,96},{1,97},{2,98},{3,99},{4,100},{5,101},{6,102},{7,103},{8,104... | collective-permute-start | bytes 1843208 | tf_op jit(solution)/shard_map/ppermute | solution.py:370
  56.0 1.6 %collective-permute-start.10 = (bf16[800,768]{1,0:T(8,128)(2,1)S(1)}, bf16[800,768]{1,0:T(8,128)(2,1)S(1)}, u32[]{:S(2)}, u32[]{:S(2)}) collective-permute-start(bf16[800,768]{1,0:T(8,128)(2,1)S(1)} %collective-permute-done.9.refs_4_), channel_id=1, source_target_pairs={{0,3},{1,2},{2,1},{3,0},{4,7},{5,6},{6,5},{7,4},{8,11},{9,10},{10,... | collective-permute-start | bytes 3686408 | tf_op jit(solution)/shard_map/ppermute | solution.py:370
  57.6 7.6 %flash.6 = (f32[576,1]{1,0:T(8,128)S(1)}, f32[576,1]{1,0:T(8,128)S(1)}, f32[576,768]{1,0:T(8,128)S(1)}, f32[576,1]{1,0:T(8,128)S(1)}, f32[576,1]{1,0:T(8,128)S(1)}, /*index=5*/f32[576,768]{1,0:T(8,128)S(1)}) custom-call(bf16[400,768]{1,0:T(8,128)(2,1)S(1)} %collective-permute-done.13.refs_0_, bf16[200,768]{1,0:T(8,128)(2,1)S(1)} %collective-permute-done.14.refs_1_, ...), custom_call_target="tpu_custom_call" | custom-call | flops 8153726976 | bytes 7077888 | tf_op jit(solution)/shard_map/flash/pallas_call | solution.py:263
  66.6 7.7 %flash.7 = (f32[576,1]{1,0:T(8,128)S(1)}, f32[576,1]{1,0:T(8,128)S(1)}, f32[576,768]{1,0:T(8,128)S(1)}, f32[576,1]{1,0:T(8,128)S(1)}, f32[576,1]{1,0:T(8,128)S(1)}, /*index=5*/f32[576,768]{1,0:T(8,128)S(1)}) custom-call(bf16[400,768]{1,0:T(8,128)(2,1)S(1)} %collective-permute-done.13.refs_0_, bf16[200,768]{1,0:T(8,128)(2,1)S(1)} %collective-permute-done.14.refs_1_, ...), custom_call_target="tpu_custom_call" | custom-call | flops 8153726976 | bytes 7077888 | tf_op jit(solution)/shard_map/flash/pallas_call | solution.py:263
  74.3 5.1 %collective-permute-done.12.refs_3_ = bf16[400,768]{1,0:T(8,128)(2,1)S(1)} collective-permute-done((bf16[400,768]{1,0:T(8,128)(2,1)S(1)}, bf16[400,768]{1,0:T(8,128)(2,1)S(1)}, u32[]{:S(2)}, u32[]{:S(2)}) %collective-permute-start.12) | collective-permute-done | bytes 614432 | tf_op jit(solution)/shard_map/ppermute | solution.py:370
  79.7 4.0 %flash.9 = bf16[592,768]{1,0:T(8,128)(2,1)S(1)} custom-call(bf16[400,768]{1,0:T(8,128)(2,1)S(1)} %collective-permute-done.13.refs_0_, bf16[200,768]{1,0:T(8,128)(2,1)S(1)} %collective-permute-done.14.refs_1_, bf16[800,768]{1,0:T(8,128)(2,1)S(1)} %collective-permute-done.10.refs_2_, bf16[400,768]{1,0:T(8,128)(2,1)S(1)} %collective-permute-done.12.refs_3_, ...), custom_call_target="tpu_custom_call" | custom-call | flops 4076863488 | bytes 4423680 | tf_op jit(solution)/shard_map/flash/pallas_call | solution.py:263
  83.7 3.7 %collective-permute-start.17 = (bf16[592,768]{1,0:T(8,128)(2,1)S(1)}, bf16[592,768]{1,0:T(8,128)(2,1)S(1)}, u32[]{:S(2)}, u32[]{:S(2)}) collective-permute-start(bf16[592,768]{1,0:T(8,128)(2,1)S(1)} %flash.9), channel_id=1, source_target_pairs={{0,16},{1,17},{2,18},{3,19},{4,20},{5,21},{6,22},{7,23},{8,24},{9,... | collective-permute-start | bytes 2727944 | tf_op jit(solution)/shard_map/ppermute | solution.py:370
  87.4 4.0 %flash.8 = (f32[576,1]{1,0:T(8,128)S(1)}, f32[576,1]{1,0:T(8,128)S(1)}, f32[576,768]{1,0:T(8,128)S(1)}) custom-call(bf16[400,768]{1,0:T(8,128)(2,1)S(1)} %get-tuple-element.56.refs_2_.refs_4_.refs_0_, bf16[200,768]{1,0:T(8,128)(2,1)S(1)} %get-tuple-element.57.refs_3_.refs_5_.refs_1_, bf16[800,768]{1,0:T(8,128)(2,1)S(1)} %collective-permute-done.10.refs_2_, ...), custom_call_target="tpu_custom_call" | custom-call | flops 4076863488 | bytes 4423680 | tf_op jit(solution)/shard_map/flash/pallas_call | solution.py:263
  92.6 2.3 %collective-permute-start.21 = (bf16[80,768]{1,0:T(8,128)(2,1)S(1)}, bf16[80,768]{1,0:T(8,128)(2,1)S(1)}, u32[]{:S(2)}, u32[]{:S(2)}) collective-permute-start(bf16[80,768]{1,0:T(8,128)(2,1)S(1)} %get-tuple-element.90), channel_id=1, source_target_pairs={{0,36},{1,37},{2,38},{3,39},{4,32},{5,33},{6,34},{7,35},{8,44},{9,... | collective-permute-start | bytes 368648 | tf_op jit(solution)/shard_map/ppermute | solution.py:370
  94.9 1.3 %collective-permute-start.22 = (bf16[80,768]{1,0:T(8,128)(2,1)S(1)}, bf16[80,768]{1,0:T(8,128)(2,1)S(1)}, u32[]{:S(2)}, u32[]{:S(2)}) collective-permute-start(bf16[80,768]{1,0:T(8,128)(2,1)S(1)} %get-tuple-element.91), channel_id=1, source_target_pairs={{0,5},{1,4},{2,7},{3,6},{4,1},{5,0},{6,3},{7,2},{8,13},{9,12},{10,... | collective-permute-start | bytes 368648 | tf_op jit(solution)/shard_map/ppermute | solution.py:370
  97.2 2.4 %collective-permute-done.19.refs_2_ = bf16[80,768]{1,0:T(8,128)(2,1)S(1)} collective-permute-done((bf16[80,768]{1,0:T(8,128)(2,1)S(1)}, bf16[80,768]{1,0:T(8,128)(2,1)S(1)}, u32[]{:S(2)}, u32[]{:S(2)}) %collective-permute-start.19) | collective-permute-done | bytes 122912 | tf_op jit(solution)/shard_map/ppermute | solution.py:370
  99.7 1.9 %collective-permute-done.22.refs_5_ = bf16[80,768]{1,0:T(8,128)(2,1)S(1)} collective-permute-done((bf16[80,768]{1,0:T(8,128)(2,1)S(1)}, bf16[80,768]{1,0:T(8,128)(2,1)S(1)}, u32[]{:S(2)}, u32[]{:S(2)}) %collective-permute-start.22) | collective-permute-done | bytes 122912 | tf_op jit(solution)/shard_map/ppermute | solution.py:370
  101.6 1.2 %collective-permute-done.23.refs_6_ = bf16[80,768]{1,0:T(8,128)(2,1)S(1)} collective-permute-done((bf16[80,768]{1,0:T(8,128)(2,1)S(1)}, bf16[80,768]{1,0:T(8,128)(2,1)S(1)}, u32[]{:S(2)}, u32[]{:S(2)}) %collective-permute-start.23) | collective-permute-done | bytes 122912 | tf_op jit(solution)/shard_map/ppermute | solution.py:370
  102.8 3.2 %collective-permute-done.24.refs_7_ = bf16[80,768]{1,0:T(8,128)(2,1)S(1)} collective-permute-done((bf16[80,768]{1,0:T(8,128)(2,1)S(1)}, bf16[80,768]{1,0:T(8,128)(2,1)S(1)}, u32[]{:S(2)}, u32[]{:S(2)}) %collective-permute-start.24) | collective-permute-done | bytes 122912 | tf_op jit(solution)/shard_map/ppermute | solution.py:370
  105.9 2.3 %final.1 = (bf16[384,768]{1,0:T(8,128)(2,1)}, f32[384]{0:T(512)}) custom-call(s32[1]{0:T(128)} %bitcast.me_ref, s32[32]{0:T(128)S(1)} %copy-done.4, s32[384]{0:T(512)S(1)} %copy-done.2, bf16[80,768]{1,0:T(8,128)(2,1)S(1)} %get-tuple-element.86.refs_0_, bf16[80,768]{1,0:T(8,128)(2,1)S(1)} %collective-permute-done.18.refs_1_, ...), custom_call_target="tpu_custom_call" | custom-call | tf_op jit(solution)/shard_map/final/pallas_call | solution.py:424
  (41 shorter events, 10.2 us)
Async XLA Ops:
  0.8 1.1 copy-start
  1.8 0.7 copy-start.1
  2.5 0.7 copy-start.3
  5.3 6.1 %collective-permute-start = (bf16[80,768]{1,0:T(8,128)(2,1)S(1)}, bf16[80,768]{1,0:T(8,128)(2,1)S(1)}, u32[]{:S(2)}, u32[]{:S(2)}) collective-permute-start(bf16[80,768]{1,0:T(8,128)(2,1)S(1)} %get-tuple-element.49), channel_id=1, source_target_pairs={{0,4},{1,5},{2,6},{3,7},{4,0},{5,1},{6,2},{7,3},{8,12},{9,13},{10,... | collective-permute-start | bytes 368648 | tf_op jit(solution)/shard_map/ppermute | solution.py:370
  7.4 6.5 %collective-permute-start.1 = (bf16[80,768]{1,0:T(8,128)(2,1)S(1)}, bf16[80,768]{1,0:T(8,128)(2,1)S(1)}, u32[]{:S(2)}, u32[]{:S(2)}) collective-permute-start(bf16[80,768]{1,0:T(8,128)(2,1)S(1)} %get-tuple-element.50), channel_id=1, source_target_pairs={{0,32},{1,33},{2,34},{3,35},{4,36},{5,37},{6,38},{7,39},{8,40},{9,... | collective-permute-start | bytes 368648 | tf_op jit(solution)/shard_map/ppermute | solution.py:370
  8.7 5.6 %collective-permute-start.2 = (bf16[80,768]{1,0:T(8,128)(2,1)S(1)}, bf16[80,768]{1,0:T(8,128)(2,1)S(1)}, u32[]{:S(2)}, u32[]{:S(2)}) collective-permute-start(bf16[80,768]{1,0:T(8,128)(2,1)S(1)} %get-tuple-element.51), channel_id=1, source_target_pairs={{0,1},{1,0},{2,3},{3,2},{4,5},{5,4},{6,7},{7,6},{8,9},{9,8},{10,11... | collective-permute-start | bytes 368648 | tf_op jit(solution)/shard_map/ppermute | solution.py:370
  10.3 4.6 %collective-permute-start.3 = (bf16[80,768]{1,0:T(8,128)(2,1)S(1)}, bf16[80,768]{1,0:T(8,128)(2,1)S(1)}, u32[]{:S(2)}, u32[]{:S(2)}) collective-permute-start(bf16[80,768]{1,0:T(8,128)(2,1)S(1)} %get-tuple-element.52), channel_id=1, source_target_pairs={{0,36},{1,37},{2,38},{3,39},{4,32},{5,33},{6,34},{7,35},{8,44},{9,... | collective-permute-start | bytes 368648 | tf_op jit(solution)/shard_map/ppermute | solution.py:370
  10.5 6.0 %collective-permute-start.4 = (bf16[80,768]{1,0:T(8,128)(2,1)S(1)}, bf16[80,768]{1,0:T(8,128)(2,1)S(1)}, u32[]{:S(2)}, u32[]{:S(2)}) collective-permute-start(bf16[80,768]{1,0:T(8,128)(2,1)S(1)} %get-tuple-element.53), channel_id=1, source_target_pairs={{0,5},{1,4},{2,7},{3,6},{4,1},{5,0},{6,3},{7,2},{8,13},{9,12},{10,... | collective-permute-start | bytes 368648 | tf_op jit(solution)/shard_map/ppermute | solution.py:370
  11.4 7.2 %collective-permute-start.5 = (bf16[80,768]{1,0:T(8,128)(2,1)S(1)}, bf16[80,768]{1,0:T(8,128)(2,1)S(1)}, u32[]{:S(2)}, u32[]{:S(2)}) collective-permute-start(bf16[80,768]{1,0:T(8,128)(2,1)S(1)} %get-tuple-element.54), channel_id=1, source_target_pairs={{0,33},{1,32},{2,35},{3,34},{4,37},{5,36},{6,39},{7,38},{8,41},{9,... | collective-permute-start | bytes 368648 | tf_op jit(solution)/shard_map/ppermute | solution.py:370
  13.9 6.5 %collective-permute-start.6 = (bf16[80,768]{1,0:T(8,128)(2,1)S(1)}, bf16[80,768]{1,0:T(8,128)(2,1)S(1)}, u32[]{:S(2)}, u32[]{:S(2)}) collective-permute-start(bf16[80,768]{1,0:T(8,128)(2,1)S(1)} %get-tuple-element.55), channel_id=1, source_target_pairs={{0,37},{1,36},{2,39},{3,38},{4,33},{5,32},{6,35},{7,34},{8,45},{9,... | collective-permute-start | bytes 368648 | tf_op jit(solution)/shard_map/ppermute | solution.py:370
  20.5 15.7 %collective-permute-start.7 = (bf16[400,768]{1,0:T(8,128)(2,1)S(1)}, bf16[400,768]{1,0:T(8,128)(2,1)S(1)}, u32[]{:S(2)}, u32[]{:S(2)}) collective-permute-start(bf16[400,768]{1,0:T(8,128)(2,1)S(1)} %get-tuple-element.56.refs_2_.refs_4_.refs_0_), channel_id=1, source_target_pairs={{0,12},{1,13},{2,14},{3,15},{4,8},{5,9},{6,10},{7,11},{8,4},{9,5},... | collective-permute-start | bytes 1843208 | tf_op jit(solution)/shard_map/ppermute | solution.py:370
  25.3 14.7 %collective-permute-start.13 = (bf16[400,768]{1,0:T(8,128)(2,1)S(1)}, bf16[400,768]{1,0:T(8,128)(2,1)S(1)}, u32[]{:S(2)}, u32[]{:S(2)}) collective-permute-start(bf16[400,768]{1,0:T(8,128)(2,1)S(1)} %get-tuple-element.56.refs_2_.refs_4_.refs_0_), channel_id=1, source_target_pairs={{0,16},{1,17},{2,18},{3,19},{4,20},{5,21},{6,22},{7,23},{8,24},{9,... | collective-permute-start | bytes 1843208 | tf_op jit(solution)/shard_map/ppermute | solution.py:370
  26.1 10.1 %collective-permute-start.8 = (bf16[200,768]{1,0:T(8,128)(2,1)S(1)}, bf16[200,768]{1,0:T(8,128)(2,1)S(1)}, u32[]{:S(2)}, u32[]{:S(2)}) collective-permute-start(bf16[200,768]{1,0:T(8,128)(2,1)S(1)} %get-tuple-element.57.refs_3_.refs_5_.refs_1_), channel_id=1, source_target_pairs={{0,3},{1,2},{2,1},{3,0},{4,7},{5,6},{6,5},{7,4},{8,11},{9,10},{10,... | collective-permute-start | bytes 921608 | tf_op jit(solution)/shard_map/ppermute | solution.py:370
  28.7 11.2 %collective-permute-start.14 = (bf16[200,768]{1,0:T(8,128)(2,1)S(1)}, bf16[200,768]{1,0:T(8,128)(2,1)S(1)}, u32[]{:S(2)}, u32[]{:S(2)}) collective-permute-start(bf16[200,768]{1,0:T(8,128)(2,1)S(1)} %get-tuple-element.57.refs_3_.refs_5_.refs_1_), channel_id=1, source_target_pairs={{0,16},{1,17},{2,18},{3,19},{4,20},{5,21},{6,22},{7,23},{8,24},{9,... | collective-permute-start | bytes 921608 | tf_op jit(solution)/shard_map/ppermute | solution.py:370
  36.2 15.9 %collective-permute-start.11 = (bf16[400,768]{1,0:T(8,128)(2,1)S(1)}, bf16[400,768]{1,0:T(8,128)(2,1)S(1)}, u32[]{:S(2)}, u32[]{:S(2)}) collective-permute-start(bf16[400,768]{1,0:T(8,128)(2,1)S(1)} %constant_dynamic-update-slice_fusion.2), channel_id=1, source_target_pairs={{0,12},{1,13},{2,14},{3,15},{4,8},{5,9},{6,10},{7,11},{8,4},{9,5},... | collective-permute-start | bytes 1843208 | tf_op jit(solution)/shard_map/ppermute | solution.py:370
  37.3 18.7 %collective-permute-start.9 = (bf16[800,768]{1,0:T(8,128)(2,1)S(1)}, bf16[800,768]{1,0:T(8,128)(2,1)S(1)}, u32[]{:S(2)}, u32[]{:S(2)}) collective-permute-start(bf16[800,768]{1,0:T(8,128)(2,1)S(1)} %constant_dynamic-update-slice_fusion), channel_id=1, source_target_pairs={{0,96},{1,97},{2,98},{3,99},{4,100},{5,101},{6,102},{7,103},{8,104... | collective-permute-start | bytes 3686408 | tf_op jit(solution)/shard_map/ppermute | solution.py:370
  46.8 19.7 %collective-permute-start.15 = (bf16[800,768]{1,0:T(8,128)(2,1)S(1)}, bf16[800,768]{1,0:T(8,128)(2,1)S(1)}, u32[]{:S(2)}, u32[]{:S(2)}) collective-permute-start(bf16[800,768]{1,0:T(8,128)(2,1)S(1)} %constant_dynamic-update-slice_fusion), channel_id=1, source_target_pairs={{0,3},{1,2},{2,1},{3,0},{4,7},{5,6},{6,5},{7,4},{8,11},{9,10},{10,... | collective-permute-start | bytes 3686408 | tf_op jit(solution)/shard_map/ppermute | solution.py:370
  48.7 17.4 %collective-permute-start.16 = (bf16[400,768]{1,0:T(8,128)(2,1)S(1)}, bf16[400,768]{1,0:T(8,128)(2,1)S(1)}, u32[]{:S(2)}, u32[]{:S(2)}) collective-permute-start(bf16[400,768]{1,0:T(8,128)(2,1)S(1)} %constant_dynamic-update-slice_fusion.2), channel_id=1, source_target_pairs={{0,96},{1,97},{2,98},{3,99},{4,100},{5,101},{6,102},{7,103},{8,104... | collective-permute-start | bytes 1843208 | tf_op jit(solution)/shard_map/ppermute | solution.py:370
  52.1 27.2 %collective-permute-start.12 = (bf16[400,768]{1,0:T(8,128)(2,1)S(1)}, bf16[400,768]{1,0:T(8,128)(2,1)S(1)}, u32[]{:S(2)}, u32[]{:S(2)}) collective-permute-start(bf16[400,768]{1,0:T(8,128)(2,1)S(1)} %collective-permute-done.11.refs_5_), channel_id=1, source_target_pairs={{0,96},{1,97},{2,98},{3,99},{4,100},{5,101},{6,102},{7,103},{8,104... | collective-permute-start | bytes 1843208 | tf_op jit(solution)/shard_map/ppermute | solution.py:370
  56.0 23.8 %collective-permute-start.10 = (bf16[800,768]{1,0:T(8,128)(2,1)S(1)}, bf16[800,768]{1,0:T(8,128)(2,1)S(1)}, u32[]{:S(2)}, u32[]{:S(2)}) collective-permute-start(bf16[800,768]{1,0:T(8,128)(2,1)S(1)} %collective-permute-done.9.refs_4_), channel_id=1, source_target_pairs={{0,3},{1,2},{2,1},{3,0},{4,7},{5,6},{6,5},{7,4},{8,11},{9,10},{10,... | collective-permute-start | bytes 3686408 | tf_op jit(solution)/shard_map/ppermute | solution.py:370
  83.7 7.7 %collective-permute-start.17 = (bf16[592,768]{1,0:T(8,128)(2,1)S(1)}, bf16[592,768]{1,0:T(8,128)(2,1)S(1)}, u32[]{:S(2)}, u32[]{:S(2)}) collective-permute-start(bf16[592,768]{1,0:T(8,128)(2,1)S(1)} %flash.9), channel_id=1, source_target_pairs={{0,16},{1,17},{2,18},{3,19},{4,20},{5,21},{6,22},{7,23},{8,24},{9,... | collective-permute-start | bytes 2727944 | tf_op jit(solution)/shard_map/ppermute | solution.py:370
  91.4 14.5 %copy-start.2 = (s32[384]{0:T(512)S(1)}, s32[384]{0:T(512)}, u32[]{:S(2)}) copy-start(s32[384]{0:T(512)} %clusters_ref.1) | copy-start | bytes 4612
  91.4 14.5 %copy-start.4 = (s32[32]{0:T(128)S(1)}, s32[32]{0:T(128)}, u32[]{:S(2)}) copy-start(s32[32]{0:T(128)} %owner_ref.1) | copy-start | bytes 388
  92.2 5.0 %collective-permute-start.18 = (bf16[80,768]{1,0:T(8,128)(2,1)S(1)}, bf16[80,768]{1,0:T(8,128)(2,1)S(1)}, u32[]{:S(2)}, u32[]{:S(2)}) collective-permute-start(bf16[80,768]{1,0:T(8,128)(2,1)S(1)} %get-tuple-element.87), channel_id=1, source_target_pairs={{0,4},{1,5},{2,6},{3,7},{4,0},{5,1},{6,2},{7,3},{8,12},{9,13},{10,... | collective-permute-start | bytes 368648 | tf_op jit(solution)/shard_map/ppermute | solution.py:370
  92.3 7.3 %collective-permute-start.19 = (bf16[80,768]{1,0:T(8,128)(2,1)S(1)}, bf16[80,768]{1,0:T(8,128)(2,1)S(1)}, u32[]{:S(2)}, u32[]{:S(2)}) collective-permute-start(bf16[80,768]{1,0:T(8,128)(2,1)S(1)} %get-tuple-element.88), channel_id=1, source_target_pairs={{0,32},{1,33},{2,34},{3,35},{4,36},{5,37},{6,38},{7,39},{8,40},{9,... | collective-permute-start | bytes 368648 | tf_op jit(solution)/shard_map/ppermute | solution.py:370
  92.4 7.3 %collective-permute-start.20 = (bf16[80,768]{1,0:T(8,128)(2,1)S(1)}, bf16[80,768]{1,0:T(8,128)(2,1)S(1)}, u32[]{:S(2)}, u32[]{:S(2)}) collective-permute-start(bf16[80,768]{1,0:T(8,128)(2,1)S(1)} %get-tuple-element.89), channel_id=1, source_target_pairs={{0,1},{1,0},{2,3},{3,2},{4,5},{5,4},{6,7},{7,6},{8,9},{9,8},{10,11... | collective-permute-start | bytes 368648 | tf_op jit(solution)/shard_map/ppermute | solution.py:370
  92.6 7.1 %collective-permute-start.21 = (bf16[80,768]{1,0:T(8,128)(2,1)S(1)}, bf16[80,768]{1,0:T(8,128)(2,1)S(1)}, u32[]{:S(2)}, u32[]{:S(2)}) collective-permute-start(bf16[80,768]{1,0:T(8,128)(2,1)S(1)} %get-tuple-element.90), channel_id=1, source_target_pairs={{0,36},{1,37},{2,38},{3,39},{4,32},{5,33},{6,34},{7,35},{8,44},{9,... | collective-permute-start | bytes 368648 | tf_op jit(solution)/shard_map/ppermute | solution.py:370
  94.9 6.7 %collective-permute-start.22 = (bf16[80,768]{1,0:T(8,128)(2,1)S(1)}, bf16[80,768]{1,0:T(8,128)(2,1)S(1)}, u32[]{:S(2)}, u32[]{:S(2)}) collective-permute-start(bf16[80,768]{1,0:T(8,128)(2,1)S(1)} %get-tuple-element.91), channel_id=1, source_target_pairs={{0,5},{1,4},{2,7},{3,6},{4,1},{5,0},{6,3},{7,2},{8,13},{9,12},{10,... | collective-permute-start | bytes 368648 | tf_op jit(solution)/shard_map/ppermute | solution.py:370
  97.2 5.5 %collective-permute-start.23 = (bf16[80,768]{1,0:T(8,128)(2,1)S(1)}, bf16[80,768]{1,0:T(8,128)(2,1)S(1)}, u32[]{:S(2)}, u32[]{:S(2)}) collective-permute-start(bf16[80,768]{1,0:T(8,128)(2,1)S(1)} %get-tuple-element.92), channel_id=1, source_target_pairs={{0,33},{1,32},{2,35},{3,34},{4,37},{5,36},{6,39},{7,38},{8,41},{9,... | collective-permute-start | bytes 368648 | tf_op jit(solution)/shard_map/ppermute | solution.py:370
  99.6 6.3 %collective-permute-start.24 = (bf16[80,768]{1,0:T(8,128)(2,1)S(1)}, bf16[80,768]{1,0:T(8,128)(2,1)S(1)}, u32[]{:S(2)}, u32[]{:S(2)}) collective-permute-start(bf16[80,768]{1,0:T(8,128)(2,1)S(1)} %get-tuple-element.93), channel_id=1, source_target_pairs={{0,37},{1,36},{2,39},{3,38},{4,33},{5,32},{6,35},{7,34},{8,45},{9,... | collective-permute-start | bytes 368648 | tf_op jit(solution)/shard_map/ppermute | solution.py:370

commit v5 on v4

--- a/solution.py
+++ b/solution.py
@@ -192,41 +192,51 @@
     key_id = side_by_side(gather_rows(key_refs, wides, keys))
     other = jnp.where(key_id == 0.0, masked, -penalty * log2e)
     for n in range(count):
-        for p, ids in enumerate(gather_rows(q_refs[n], (True, False), queries.at[n])):
-            labels[n, p * block_keys : (p + 1) * block_keys, :] = column_of(ids[0:1])
-    for n in range(count):
-        for start in range(0, parts * block_keys, query_rows):
-            at = slice(start, start + query_rows)
-            scores = lax.dot_general(
-                queries[n, at, :], keys[...], (((1,), (1,)), ((), ())), preferred_element_type=f32
+        wide_ids = q_refs[n][0][2 * block_keys : big_rows, 0:256].astype(f32)
+        small_ids = q_refs[n][1][block_keys:small_rows, 0:256].astype(f32)
+        for p, ids in enumerate((wide_ids[0:1], wide_ids[1:2], small_ids[0:1])):
+            labels[n, p * block_keys : (p + 1) * block_keys, :] = column_of(ids)
+    work = [(n, start, rows) for n in range(count) for start, rows in ((0, 384), (384, 192))]
+
+    def product(n, start, query_rows):
+        rows = q_refs[n][start // 384][0:query_rows, :]
+        return lax.dot_general(
+            rows, keys[...], (((1,), (1,)), ((), ())), preferred_element_type=f32
+        )
+
+    ahead = product(*work[0])
+    for k, (n, start, query_rows) in enumerate(work):
+        at = slice(start, start + query_rows)
+        scores = ahead
+        if k + 1 < len(work):
+            ahead = product(*work[k + 1])
+        scores = scores * scale + jnp.where(key_id == labels[n, at, :], 0.0, other)
+        if first and owns[n]:
+            row = lax.broadcasted_iota(jnp.int32, scores.shape, 0) + start
+            scores = jnp.where(
+                row == lax.broadcasted_iota(jnp.int32, scores.shape, 1), masked, scores
             )
-            scores = scores * scale + jnp.where(key_id == labels[n, at, :], 0.0, other)
-            if first and owns[n]:
-                row = lax.broadcasted_iota(jnp.int32, scores.shape, 0) + start
-                scores = jnp.where(
-                    row == lax.broadcasted_iota(jnp.int32, scores.shape, 1), masked, scores
-                )
-            highest = jnp.max(scores, axis=1, keepdims=True)
-            if first:
-                peak = jnp.maximum(highest, 0.0)
-            else:
-                former = states[n][0][at, :]
-                peak = jnp.maximum(former, highest)
-                fade = jnp.exp2(former - peak)
-            weights = jnp.exp2(scores - peak)
-            mass = jnp.sum(weights, axis=1, keepdims=True)
-            acc = jnp.dot(weights.astype(bf16), keys[...], preferred_element_type=f32)
-            if not first:
-                mass = mass + states[n][1][at, :] * fade
-                acc = acc + states[n][2][at, :] * fade
-            elif owns[n]:
-                mass = mass + jnp.exp2(-peak)
-            if not finish:
-                outs[n][0][at, :], outs[n][1][at, :], outs[n][2][at, :] = peak, mass, acc
-                continue
-            safe = jnp.where(mass > 0.0, mass, 1.0)
-            outs[n][0][at, :] = (acc / safe).astype(bf16)
-            labels[n, at, :] = jnp.where(mass > 0.0, peak + jnp.log2(safe), masked)
+        highest = jnp.max(scores, axis=1, keepdims=True)
+        if first:
+            peak = jnp.maximum(highest, 0.0)
+        else:
+            former = states[n][0][at, :]
+            peak = jnp.maximum(former, highest)
+            fade = jnp.exp2(former - peak)
+        weights = jnp.exp2(scores - peak)
+        mass = jnp.sum(weights, axis=1, keepdims=True)
+        acc = jnp.dot(weights.astype(bf16), keys[...], preferred_element_type=f32)
+        if not first:
+            mass = mass + states[n][1][at, :] * fade
+            acc = acc + states[n][2][at, :] * fade
+        elif owns[n]:
+            mass = mass + jnp.exp2(-peak)
+        if not finish:
+            outs[n][0][at, :], outs[n][1][at, :], outs[n][2][at, :] = peak, mass, acc
+            continue
+        safe = jnp.where(mass > 0.0, mass, 1.0)
+        outs[n][0][at, :] = (acc / safe).astype(bf16)
+        labels[n, at, :] = jnp.where(mass > 0.0, peak + jnp.log2(safe), masked)
     if finish:
         rows = parts * block_keys
         for n in range(count):
@@ -267,7 +277,7 @@
         out_specs=vmem_specs(len(each) * count),
         scratch_shapes=[
             pltpu.VMEM((total, width), bf16),
-            pltpu.VMEM((count, rows, width), bf16),
+            pltpu.VMEM((8, 128), bf16),
             pltpu.VMEM((count, rows, 1), f32),
         ],
         compiler_params=params,
@@ -387,7 +397,10 @@
         ],
         compiler_params=params,
         name="place",
-    )(me, cluster_owner, clusters, embeddings)
+    )(
+        me,
+        *(pltpu.with_memory_space_constraint(a, pltpu.HBM) for a in (cluster_owner, clusters, embeddings)),
+    )
     arrived = [packets[0]] + [send(packets[n], trips[n]) for n in range(1, 8)]
     big, small = pack(arrived)
     wide = [
@@ -403,8 +416,10 @@
     big1, small1 = send(big, wide[1]), send(small, narrow[1])
     queries, owns = [q_other, q_own], [False, True]
     pairs = lambda *units: list(zip(units, (True, False) * 2))
-    states = flash(queries, owns, pairs(*q_own, big0, small0), None, False)
-    big, small, states[1] = lax.optimization_barrier((big, small, states[1]))
+    begin = pairs(*q_own, big0, small0)
+    states = flash(queries[1:], owns[1:], begin, None, False)
+    big, small, states[0] = lax.optimization_barrier((big, small, states[0]))
+    states = flash(queries[:1], owns[:1], begin, None, False) + states
     big2, small2 = send(big, wide[2]), send(small, narrow[2])
     big3, small3 = send(big1, wide[2]), send(small1, narrow[2])
     states = flash(queries, owns, pairs(big1, small1), states, False)

time: 109 us -> 105 us (0.963)
  waiting for transfers between devices: 31.2 us -> 37.7 us
  Pallas kernels: 35.3 us -> 31.3 us
  starting transfers between devices: 38.3 us -> 34.9 us
  local copies, waits for them, and re-layouts: 2.53 us -> 0.14 us
    ppermute x25, waiting for transfers between devices: 31.2 us -> 37.7 us  [per_device(): send = lambda a, pairs: lax.ppermute(a, axes, pairs)]
    pallas_call x5 -> x6, Pallas kernels: 30.1 us -> 25.7 us  [flash(): pl.pallas_call(functools.partial(flash_kernel, wides, first, owns, finish...]
    ppermute x25, starting transfers between devices: 38.3 us -> 34.9 us  [per_device(): send = lambda a, pairs: lax.ppermute(a, axes, pairs)]
    unnamed x12 -> x6, local copies, waits for them, and re-layouts: 2.47 us -> 0.07 us
  transfers between devices with their start and end apart: 25 -> 25, of which waited for: 16 -> 11; matrix products, arithmetic and copies ran while one was open for 0% -> 0% of each run, Pallas kernels for 24% -> 21%
where the time goes in v5:
time: 105 us
  waiting for transfers between devices  37.7 us (36%)
  starting transfers between devices  34.9 us (33%)
  Pallas kernels  31.3 us (30%)
    ppermute x25, waiting for transfers between devices, per_device(): send = lambda a, pairs: lax.ppermute(a, axes, pairs)  37.7 us
    ppermute x25, starting transfers between devices, per_device(): send = lambda a, pairs: lax.ppermute(a, axes, pairs)  34.9 us
    pallas_call x6, Pallas kernels, flash(): pl.pallas_call(functools.partial(flash_kernel, wides, first, owns, finish...  25.7 us
    pallas_call x1, Pallas kernels, per_device(): pl.pallas_call(place_kernel, out_shape=[packet] * 8, in_specs=[smem] + [p...  2.46 us
    pallas_call x1, Pallas kernels, per_device(): pl.pallas_call(final_kernel, out_shape=[jax.ShapeDtypeStruct((rows, width...  2.26 us
  transfers between devices with their start and end apart: 25, of which 11 were waited for; matrix products, arithmetic and copies ran while one was open for 0% of the time, Pallas kernels for 21%

profile of v5, /device:TPU:1, one launch (start us, length us, event | category | flops | bytes accessed | tf_op | source)
XLA Modules:
  0.0 104.9 jit_solution(17037373506622069342)
XLA Ops:
  0.8 2.5 %place.1 = (bf16[80,768]{1,0:T(8,128)(2,1)S(1)}, bf16[80,768]{1,0:T(8,128)(2,1)S(1)}, bf16[80,768]{1,0:T(8,128)(2,1)S(1)}, bf16[80,768]{1,0:T(8,128)(2,1)S(1)}, ...) custom-call(s32[1]{0:T(128)} %bitcast.me_ref, ...), custom_call_target="tpu_custom_call" | custom-call | tf_op jit(solution)/shard_map/place/pallas_call | solution.py:387
  3.2 2.1 %collective-permute-start = (bf16[80,768]{1,0:T(8,128)(2,1)S(1)}, bf16[80,768]{1,0:T(8,128)(2,1)S(1)}, u32[]{:S(2)}, u32[]{:S(2)}) collective-permute-start(bf16[80,768]{1,0:T(8,128)(2,1)S(1)} %get-tuple-element.49), channel_id=1, source_target_pairs={{0,4},{1,5},{2,6},{3,7},{4,0},{5,1},{6,2},{7,3},{8,12},{9,13},{10,... | collective-permute-start | bytes 368648 | tf_op jit(solution)/shard_map/ppermute | solution.py:380
  5.4 1.3 %collective-permute-start.1 = (bf16[80,768]{1,0:T(8,128)(2,1)S(1)}, bf16[80,768]{1,0:T(8,128)(2,1)S(1)}, u32[]{:S(2)}, u32[]{:S(2)}) collective-permute-start(bf16[80,768]{1,0:T(8,128)(2,1)S(1)} %get-tuple-element.50), channel_id=1, source_target_pairs={{0,32},{1,33},{2,34},{3,35},{4,36},{5,37},{6,38},{7,39},{8,40},{9,... | collective-permute-start | bytes 368648 | tf_op jit(solution)/shard_map/ppermute | solution.py:380
  6.7 1.6 %collective-permute-start.2 = (bf16[80,768]{1,0:T(8,128)(2,1)S(1)}, bf16[80,768]{1,0:T(8,128)(2,1)S(1)}, u32[]{:S(2)}, u32[]{:S(2)}) collective-permute-start(bf16[80,768]{1,0:T(8,128)(2,1)S(1)} %get-tuple-element.51), channel_id=1, source_target_pairs={{0,1},{1,0},{2,3},{3,2},{4,5},{5,4},{6,7},{7,6},{8,9},{9,8},{10,11... | collective-permute-start | bytes 368648 | tf_op jit(solution)/shard_map/ppermute | solution.py:380
  8.4 0.9 collective-permute-start.4
  9.4 2.5 %collective-permute-start.5 = (bf16[80,768]{1,0:T(8,128)(2,1)S(1)}, bf16[80,768]{1,0:T(8,128)(2,1)S(1)}, u32[]{:S(2)}, u32[]{:S(2)}) collective-permute-start(bf16[80,768]{1,0:T(8,128)(2,1)S(1)} %get-tuple-element.54), channel_id=1, source_target_pairs={{0,33},{1,32},{2,35},{3,34},{4,37},{5,36},{6,39},{7,38},{8,41},{9,... | collective-permute-start | bytes 368648 | tf_op jit(solution)/shard_map/ppermute | solution.py:380
  12.9 1.5 %collective-permute-done.4.refs_5_ = bf16[80,768]{1,0:T(8,128)(2,1)S(1)} collective-permute-done((bf16[80,768]{1,0:T(8,128)(2,1)S(1)}, bf16[80,768]{1,0:T(8,128)(2,1)S(1)}, u32[]{:S(2)}, u32[]{:S(2)}) %collective-permute-start.4) | collective-permute-done | bytes 122912 | tf_op jit(solution)/shard_map/ppermute | solution.py:380
  14.5 2.1 %collective-permute-done.5.refs_6_ = bf16[80,768]{1,0:T(8,128)(2,1)S(1)} collective-permute-done((bf16[80,768]{1,0:T(8,128)(2,1)S(1)}, bf16[80,768]{1,0:T(8,128)(2,1)S(1)}, u32[]{:S(2)}, u32[]{:S(2)}) %collective-permute-start.5) | collective-permute-done | bytes 122912 | tf_op jit(solution)/shard_map/ppermute | solution.py:380
  16.6 1.8 %collective-permute-done.6.refs_7_ = bf16[80,768]{1,0:T(8,128)(2,1)S(1)} collective-permute-done((bf16[80,768]{1,0:T(8,128)(2,1)S(1)}, bf16[80,768]{1,0:T(8,128)(2,1)S(1)}, u32[]{:S(2)}, u32[]{:S(2)}) %collective-permute-start.6) | collective-permute-done | bytes 122912 | tf_op jit(solution)/shard_map/ppermute | solution.py:380
  18.5 4.8 %collective-permute-start.7 = (bf16[400,768]{1,0:T(8,128)(2,1)S(1)}, bf16[400,768]{1,0:T(8,128)(2,1)S(1)}, u32[]{:S(2)}, u32[]{:S(2)}) collective-permute-start(bf16[400,768]{1,0:T(8,128)(2,1)S(1)} %get-tuple-element.56.refs_0_.refs_2_), channel_id=1, source_target_pairs={{0,12},{1,13},{2,14},{3,15},{4,8},{5,9},{6,10},{7,11},{8,4},{9,5},... | collective-permute-start | bytes 1843208 | tf_op jit(solution)/shard_map/ppermute | solution.py:380
  23.3 1.5 %collective-permute-start.8 = (bf16[200,768]{1,0:T(8,128)(2,1)S(1)}, bf16[200,768]{1,0:T(8,128)(2,1)S(1)}, u32[]{:S(2)}, u32[]{:S(2)}) collective-permute-start(bf16[200,768]{1,0:T(8,128)(2,1)S(1)} %get-tuple-element.57.refs_1_.refs_3_), channel_id=1, source_target_pairs={{0,3},{1,2},{2,1},{3,0},{4,7},{5,6},{6,5},{7,4},{8,11},{9,10},{10,... | collective-permute-start | bytes 921608 | tf_op jit(solution)/shard_map/ppermute | solution.py:380
  24.8 7.6 %collective-permute-done.8.refs_5_ = bf16[200,768]{1,0:T(8,128)(2,1)S(1)} collective-permute-done((bf16[200,768]{1,0:T(8,128)(2,1)S(1)}, bf16[200,768]{1,0:T(8,128)(2,1)S(1)}, u32[]{:S(2)}, u32[]{:S(2)}) %collective-permute-start.8) | collective-permute-done | bytes 307232 | tf_op jit(solution)/shard_map/ppermute | solution.py:380
  33.0 3.0 %collective-permute-start.13 = (bf16[400,768]{1,0:T(8,128)(2,1)S(1)}, bf16[400,768]{1,0:T(8,128)(2,1)S(1)}, u32[]{:S(2)}, u32[]{:S(2)}) collective-permute-start(bf16[400,768]{1,0:T(8,128)(2,1)S(1)} %get-tuple-element.56.refs_0_.refs_2_), channel_id=1, source_target_pairs={{0,16},{1,17},{2,18},{3,19},{4,20},{5,21},{6,22},{7,23},{8,24},{9,... | collective-permute-start | bytes 1843208 | tf_op jit(solution)/shard_map/ppermute | solution.py:380
  36.1 2.5 %collective-permute-start.11 = (bf16[400,768]{1,0:T(8,128)(2,1)S(1)}, bf16[400,768]{1,0:T(8,128)(2,1)S(1)}, u32[]{:S(2)}, u32[]{:S(2)}) collective-permute-start(bf16[400,768]{1,0:T(8,128)(2,1)S(1)} %constant_dynamic-update-slice_fusion.2), channel_id=1, source_target_pairs={{0,12},{1,13},{2,14},{3,15},{4,8},{5,9},{6,10},{7,11},{8,4},{9,5},... | collective-permute-start | bytes 1843208 | tf_op jit(solution)/shard_map/ppermute | solution.py:380
  38.6 3.1 %flash.6 = (f32[576,1]{1,0:T(8,128)S(1)}, f32[576,1]{1,0:T(8,128)S(1)}, f32[576,768]{1,0:T(8,128)S(1)}) custom-call(bf16[400,768]{1,0:T(8,128)(2,1)S(1)} %get-tuple-element.56.refs_0_.refs_2_, bf16[200,768]{1,0:T(8,128)(2,1)S(1)} %get-tuple-element.57.refs_1_.refs_3_, bf16[400,768]{1,0:T(8,128)(2,1)S(1)} %get-tuple-element.56.refs_0_.refs_2_, ...), custom_call_target="tpu_custom_call" | custom-call | flops 4076863488 | bytes 4423680 | tf_op jit(solution)/shard_map/flash/pallas_call | solution.py:273
  42.1 1.2 %collective-permute-start.16 = (bf16[400,768]{1,0:T(8,128)(2,1)S(1)}, bf16[400,768]{1,0:T(8,128)(2,1)S(1)}, u32[]{:S(2)}, u32[]{:S(2)}) collective-permute-start(bf16[400,768]{1,0:T(8,128)(2,1)S(1)} %constant_dynamic-update-slice_fusion.2), channel_id=1, source_target_pairs={{0,96},{1,97},{2,98},{3,99},{4,100},{5,101},{6,102},{7,103},{8,104... | collective-permute-start | bytes 1843208 | tf_op jit(solution)/shard_map/ppermute | solution.py:380
  43.3 3.1 %flash.7 = (f32[576,1]{1,0:T(8,128)S(1)}, f32[576,1]{1,0:T(8,128)S(1)}, f32[576,768]{1,0:T(8,128)S(1)}) custom-call(bf16[400,768]{1,0:T(8,128)(2,1)S(1)} %collective-permute-done.13.refs_0_, bf16[200,768]{1,0:T(8,128)(2,1)S(1)} %collective-permute-done.14.refs_1_, bf16[400,768]{1,0:T(8,128)(2,1)S(1)} %get-tuple-element.56.refs_0_.refs_2_, ...), custom_call_target="tpu_custom_call" | custom-call | flops 4076863488 | bytes 4423680 | tf_op jit(solution)/shard_map/flash/pallas_call | solution.py:273
  46.4 5.9 %collective-permute-done.11.refs_5_ = bf16[400,768]{1,0:T(8,128)(2,1)S(1)} collective-permute-done((bf16[400,768]{1,0:T(8,128)(2,1)S(1)}, bf16[400,768]{1,0:T(8,128)(2,1)S(1)}, u32[]{:S(2)}, u32[]{:S(2)}) %collective-permute-start.11) | collective-permute-done | bytes 614432 | tf_op jit(solution)/shard_map/ppermute | solution.py:380
  52.3 1.2 %collective-permute-start.12 = (bf16[400,768]{1,0:T(8,128)(2,1)S(1)}, bf16[400,768]{1,0:T(8,128)(2,1)S(1)}, u32[]{:S(2)}, u32[]{:S(2)}) collective-permute-start(bf16[400,768]{1,0:T(8,128)(2,1)S(1)} %collective-permute-done.11.refs_5_), channel_id=1, source_target_pairs={{0,96},{1,97},{2,98},{3,99},{4,100},{5,101},{6,102},{7,103},{8,104... | collective-permute-start | bytes 1843208 | tf_op jit(solution)/shard_map/ppermute | solution.py:380
  53.5 3.8 %collective-permute-start.10 = (bf16[800,768]{1,0:T(8,128)(2,1)S(1)}, bf16[800,768]{1,0:T(8,128)(2,1)S(1)}, u32[]{:S(2)}, u32[]{:S(2)}) collective-permute-start(bf16[800,768]{1,0:T(8,128)(2,1)S(1)} %collective-permute-done.9.refs_4_), channel_id=1, source_target_pairs={{0,3},{1,2},{2,1},{3,0},{4,7},{5,6},{6,5},{7,4},{8,11},{9,10},{10,... | collective-permute-start | bytes 3686408 | tf_op jit(solution)/shard_map/ppermute | solution.py:380
  57.3 6.3 %flash.8 = (f32[576,1]{1,0:T(8,128)S(1)}, f32[576,1]{1,0:T(8,128)S(1)}, f32[576,768]{1,0:T(8,128)S(1)}, f32[576,1]{1,0:T(8,128)S(1)}, f32[576,1]{1,0:T(8,128)S(1)}, /*index=5*/f32[576,768]{1,0:T(8,128)S(1)}) custom-call(bf16[400,768]{1,0:T(8,128)(2,1)S(1)} %collective-permute-done.13.refs_0_, bf16[200,768]{1,0:T(8,128)(2,1)S(1)} %collective-permute-done.14.refs_1_, ...), custom_call_target="tpu_custom_call" | custom-call | flops 8153726976 | bytes 7077888 | tf_op jit(solution)/shard_map/flash/pallas_call | solution.py:273
  63.7 2.8 %collective-permute-done.15.refs_4_ = bf16[800,768]{1,0:T(8,128)(2,1)S(1)} collective-permute-done((bf16[800,768]{1,0:T(8,128)(2,1)S(1)}, bf16[800,768]{1,0:T(8,128)(2,1)S(1)}, u32[]{:S(2)}, u32[]{:S(2)}) %collective-permute-start.15) | collective-permute-done | bytes 1228832 | tf_op jit(solution)/shard_map/ppermute | solution.py:380
  66.4 6.2 %flash.9 = (f32[576,1]{1,0:T(8,128)S(1)}, f32[576,1]{1,0:T(8,128)S(1)}, f32[576,768]{1,0:T(8,128)S(1)}, f32[576,1]{1,0:T(8,128)S(1)}, f32[576,1]{1,0:T(8,128)S(1)}, /*index=5*/f32[576,768]{1,0:T(8,128)S(1)}) custom-call(bf16[400,768]{1,0:T(8,128)(2,1)S(1)} %collective-permute-done.13.refs_0_, bf16[200,768]{1,0:T(8,128)(2,1)S(1)} %collective-permute-done.14.refs_1_, ...), custom_call_target="tpu_custom_call" | custom-call | flops 8153726976 | bytes 7077888 | tf_op jit(solution)/shard_map/flash/pallas_call | solution.py:273
  72.7 6.6 %collective-permute-done.10.refs_2_ = bf16[800,768]{1,0:T(8,128)(2,1)S(1)} collective-permute-done((bf16[800,768]{1,0:T(8,128)(2,1)S(1)}, bf16[800,768]{1,0:T(8,128)(2,1)S(1)}, u32[]{:S(2)}, u32[]{:S(2)}) %collective-permute-start.10) | collective-permute-done | bytes 1228832 | tf_op jit(solution)/shard_map/ppermute | solution.py:380
  79.3 3.6 %flash.11 = bf16[592,768]{1,0:T(8,128)(2,1)S(1)} custom-call(bf16[400,768]{1,0:T(8,128)(2,1)S(1)} %collective-permute-done.13.refs_0_, bf16[200,768]{1,0:T(8,128)(2,1)S(1)} %collective-permute-done.14.refs_1_, bf16[800,768]{1,0:T(8,128)(2,1)S(1)} %collective-permute-done.10.refs_2_, bf16[400,768]{1,0:T(8,128)(2,1)S(1)} %collective-permute-done.12.refs_3_, ...), custom_call_target="tpu_custom_call" | custom-call | flops 4076863488 | bytes 4423680 | tf_op jit(solution)/shard_map/flash/pallas_call | solution.py:273
  83.0 3.4 %flash.10 = (f32[576,1]{1,0:T(8,128)S(1)}, f32[576,1]{1,0:T(8,128)S(1)}, f32[576,768]{1,0:T(8,128)S(1)}) custom-call(bf16[400,768]{1,0:T(8,128)(2,1)S(1)} %get-tuple-element.56.refs_0_.refs_2_, bf16[200,768]{1,0:T(8,128)(2,1)S(1)} %get-tuple-element.57.refs_1_.refs_3_, bf16[800,768]{1,0:T(8,128)(2,1)S(1)} %collective-permute-done.10.refs_2_, ...), custom_call_target="tpu_custom_call" | custom-call | flops 4076863488 | bytes 4423680 | tf_op jit(solution)/shard_map/flash/pallas_call | solution.py:273
  87.3 1.4 %collective-permute-start.20 = (bf16[80,768]{1,0:T(8,128)(2,1)S(1)}, bf16[80,768]{1,0:T(8,128)(2,1)S(1)}, u32[]{:S(2)}, u32[]{:S(2)}) collective-permute-start(bf16[80,768]{1,0:T(8,128)(2,1)S(1)} %get-tuple-element.89), channel_id=1, source_target_pairs={{0,1},{1,0},{2,3},{3,2},{4,5},{5,4},{6,7},{7,6},{8,9},{9,8},{10,11... | collective-permute-start | bytes 368648 | tf_op jit(solution)/shard_map/ppermute | solution.py:380
  88.7 2.5 %collective-permute-start.21 = (bf16[80,768]{1,0:T(8,128)(2,1)S(1)}, bf16[80,768]{1,0:T(8,128)(2,1)S(1)}, u32[]{:S(2)}, u32[]{:S(2)}) collective-permute-start(bf16[80,768]{1,0:T(8,128)(2,1)S(1)} %get-tuple-element.90), channel_id=1, source_target_pairs={{0,36},{1,37},{2,38},{3,39},{4,32},{5,33},{6,34},{7,35},{8,44},{9,... | collective-permute-start | bytes 368648 | tf_op jit(solution)/shard_map/ppermute | solution.py:380
  92.4 2.2 %collective-permute-start.24 = (bf16[80,768]{1,0:T(8,128)(2,1)S(1)}, bf16[80,768]{1,0:T(8,128)(2,1)S(1)}, u32[]{:S(2)}, u32[]{:S(2)}) collective-permute-start(bf16[80,768]{1,0:T(8,128)(2,1)S(1)} %get-tuple-element.93), channel_id=1, source_target_pairs={{0,37},{1,36},{2,39},{3,38},{4,33},{5,32},{6,35},{7,34},{8,45},{9,... | collective-permute-start | bytes 368648 | tf_op jit(solution)/shard_map/ppermute | solution.py:380
  94.6 3.9 %collective-permute-done.22.refs_5_ = bf16[80,768]{1,0:T(8,128)(2,1)S(1)} collective-permute-done((bf16[80,768]{1,0:T(8,128)(2,1)S(1)}, bf16[80,768]{1,0:T(8,128)(2,1)S(1)}, u32[]{:S(2)}, u32[]{:S(2)}) %collective-permute-start.22) | collective-permute-done | bytes 122912 | tf_op jit(solution)/shard_map/ppermute | solution.py:380
  98.6 4.1 %collective-permute-done.23.refs_6_ = bf16[80,768]{1,0:T(8,128)(2,1)S(1)} collective-permute-done((bf16[80,768]{1,0:T(8,128)(2,1)S(1)}, bf16[80,768]{1,0:T(8,128)(2,1)S(1)}, u32[]{:S(2)}, u32[]{:S(2)}) %collective-permute-start.23) | collective-permute-done | bytes 122912 | tf_op jit(solution)/shard_map/ppermute | solution.py:380
  102.7 2.3 %final.1 = (bf16[384,768]{1,0:T(8,128)(2,1)}, f32[384]{0:T(512)}) custom-call(s32[1]{0:T(128)} %bitcast.me_ref, s32[32]{0:T(128)S(1)} %copy-done.1, s32[384]{0:T(512)S(1)} %copy-done, bf16[80,768]{1,0:T(8,128)(2,1)S(1)} %get-tuple-element.86.refs_0_, bf16[80,768]{1,0:T(8,128)(2,1)S(1)} %collective-permute-done.18.refs_1_, ...), custom_call_target="tpu_custom_call" | custom-call | tf_op jit(solution)/shard_map/final/pallas_call | solution.py:439
  (36 shorter events, 4.5 us)
Async XLA Ops:
  3.2 6.1 %collective-permute-start = (bf16[80,768]{1,0:T(8,128)(2,1)S(1)}, bf16[80,768]{1,0:T(8,128)(2,1)S(1)}, u32[]{:S(2)}, u32[]{:S(2)}) collective-permute-start(bf16[80,768]{1,0:T(8,128)(2,1)S(1)} %get-tuple-element.49), channel_id=1, source_target_pairs={{0,4},{1,5},{2,6},{3,7},{4,0},{5,1},{6,2},{7,3},{8,12},{9,13},{10,... | collective-permute-start | bytes 368648 | tf_op jit(solution)/shard_map/ppermute | solution.py:380
  5.4 6.5 %collective-permute-start.1 = (bf16[80,768]{1,0:T(8,128)(2,1)S(1)}, bf16[80,768]{1,0:T(8,128)(2,1)S(1)}, u32[]{:S(2)}, u32[]{:S(2)}) collective-permute-start(bf16[80,768]{1,0:T(8,128)(2,1)S(1)} %get-tuple-element.50), channel_id=1, source_target_pairs={{0,32},{1,33},{2,34},{3,35},{4,36},{5,37},{6,38},{7,39},{8,40},{9,... | collective-permute-start | bytes 368648 | tf_op jit(solution)/shard_map/ppermute | solution.py:380
  6.7 5.5 %collective-permute-start.2 = (bf16[80,768]{1,0:T(8,128)(2,1)S(1)}, bf16[80,768]{1,0:T(8,128)(2,1)S(1)}, u32[]{:S(2)}, u32[]{:S(2)}) collective-permute-start(bf16[80,768]{1,0:T(8,128)(2,1)S(1)} %get-tuple-element.51), channel_id=1, source_target_pairs={{0,1},{1,0},{2,3},{3,2},{4,5},{5,4},{6,7},{7,6},{8,9},{9,8},{10,11... | collective-permute-start | bytes 368648 | tf_op jit(solution)/shard_map/ppermute | solution.py:380
  8.3 4.6 %collective-permute-start.3 = (bf16[80,768]{1,0:T(8,128)(2,1)S(1)}, bf16[80,768]{1,0:T(8,128)(2,1)S(1)}, u32[]{:S(2)}, u32[]{:S(2)}) collective-permute-start(bf16[80,768]{1,0:T(8,128)(2,1)S(1)} %get-tuple-element.52), channel_id=1, source_target_pairs={{0,36},{1,37},{2,38},{3,39},{4,32},{5,33},{6,34},{7,35},{8,44},{9,... | collective-permute-start | bytes 368648 | tf_op jit(solution)/shard_map/ppermute | solution.py:380
  8.4 6.0 %collective-permute-start.4 = (bf16[80,768]{1,0:T(8,128)(2,1)S(1)}, bf16[80,768]{1,0:T(8,128)(2,1)S(1)}, u32[]{:S(2)}, u32[]{:S(2)}) collective-permute-start(bf16[80,768]{1,0:T(8,128)(2,1)S(1)} %get-tuple-element.53), channel_id=1, source_target_pairs={{0,5},{1,4},{2,7},{3,6},{4,1},{5,0},{6,3},{7,2},{8,13},{9,12},{10,... | collective-permute-start | bytes 368648 | tf_op jit(solution)/shard_map/ppermute | solution.py:380
  9.4 7.2 %collective-permute-start.5 = (bf16[80,768]{1,0:T(8,128)(2,1)S(1)}, bf16[80,768]{1,0:T(8,128)(2,1)S(1)}, u32[]{:S(2)}, u32[]{:S(2)}) collective-permute-start(bf16[80,768]{1,0:T(8,128)(2,1)S(1)} %get-tuple-element.54), channel_id=1, source_target_pairs={{0,33},{1,32},{2,35},{3,34},{4,37},{5,36},{6,39},{7,38},{8,41},{9,... | collective-permute-start | bytes 368648 | tf_op jit(solution)/shard_map/ppermute | solution.py:380
  11.8 6.5 %collective-permute-start.6 = (bf16[80,768]{1,0:T(8,128)(2,1)S(1)}, bf16[80,768]{1,0:T(8,128)(2,1)S(1)}, u32[]{:S(2)}, u32[]{:S(2)}) collective-permute-start(bf16[80,768]{1,0:T(8,128)(2,1)S(1)} %get-tuple-element.55), channel_id=1, source_target_pairs={{0,37},{1,36},{2,39},{3,38},{4,33},{5,32},{6,35},{7,34},{8,45},{9,... | collective-permute-start | bytes 368648 | tf_op jit(solution)/shard_map/ppermute | solution.py:380
  18.5 14.0 %collective-permute-start.7 = (bf16[400,768]{1,0:T(8,128)(2,1)S(1)}, bf16[400,768]{1,0:T(8,128)(2,1)S(1)}, u32[]{:S(2)}, u32[]{:S(2)}) collective-permute-start(bf16[400,768]{1,0:T(8,128)(2,1)S(1)} %get-tuple-element.56.refs_0_.refs_2_), channel_id=1, source_target_pairs={{0,12},{1,13},{2,14},{3,15},{4,8},{5,9},{6,10},{7,11},{8,4},{9,5},... | collective-permute-start | bytes 1843208 | tf_op jit(solution)/shard_map/ppermute | solution.py:380
  23.3 9.2 %collective-permute-start.8 = (bf16[200,768]{1,0:T(8,128)(2,1)S(1)}, bf16[200,768]{1,0:T(8,128)(2,1)S(1)}, u32[]{:S(2)}, u32[]{:S(2)}) collective-permute-start(bf16[200,768]{1,0:T(8,128)(2,1)S(1)} %get-tuple-element.57.refs_1_.refs_3_), channel_id=1, source_target_pairs={{0,3},{1,2},{2,1},{3,0},{4,7},{5,6},{6,5},{7,4},{8,11},{9,10},{10,... | collective-permute-start | bytes 921608 | tf_op jit(solution)/shard_map/ppermute | solution.py:380
  32.5 21.0 %collective-permute-start.9 = (bf16[800,768]{1,0:T(8,128)(2,1)S(1)}, bf16[800,768]{1,0:T(8,128)(2,1)S(1)}, u32[]{:S(2)}, u32[]{:S(2)}) collective-permute-start(bf16[800,768]{1,0:T(8,128)(2,1)S(1)} %constant_dynamic-update-slice_fusion), channel_id=1, source_target_pairs={{0,96},{1,97},{2,98},{3,99},{4,100},{5,101},{6,102},{7,103},{8,104... | collective-permute-start | bytes 3686408 | tf_op jit(solution)/shard_map/ppermute | solution.py:380
  33.0 10.3 %collective-permute-start.13 = (bf16[400,768]{1,0:T(8,128)(2,1)S(1)}, bf16[400,768]{1,0:T(8,128)(2,1)S(1)}, u32[]{:S(2)}, u32[]{:S(2)}) collective-permute-start(bf16[400,768]{1,0:T(8,128)(2,1)S(1)} %get-tuple-element.56.refs_0_.refs_2_), channel_id=1, source_target_pairs={{0,16},{1,17},{2,18},{3,19},{4,20},{5,21},{6,22},{7,23},{8,24},{9,... | collective-permute-start | bytes 1843208 | tf_op jit(solution)/shard_map/ppermute | solution.py:380
  36.1 6.0 %collective-permute-start.14 = (bf16[200,768]{1,0:T(8,128)(2,1)S(1)}, bf16[200,768]{1,0:T(8,128)(2,1)S(1)}, u32[]{:S(2)}, u32[]{:S(2)}) collective-permute-start(bf16[200,768]{1,0:T(8,128)(2,1)S(1)} %get-tuple-element.57.refs_1_.refs_3_), channel_id=1, source_target_pairs={{0,16},{1,17},{2,18},{3,19},{4,20},{5,21},{6,22},{7,23},{8,24},{9,... | collective-permute-start | bytes 921608 | tf_op jit(solution)/shard_map/ppermute | solution.py:380
  36.1 16.2 %collective-permute-start.11 = (bf16[400,768]{1,0:T(8,128)(2,1)S(1)}, bf16[400,768]{1,0:T(8,128)(2,1)S(1)}, u32[]{:S(2)}, u32[]{:S(2)}) collective-permute-start(bf16[400,768]{1,0:T(8,128)(2,1)S(1)} %constant_dynamic-update-slice_fusion.2), channel_id=1, source_target_pairs={{0,12},{1,13},{2,14},{3,15},{4,8},{5,9},{6,10},{7,11},{8,4},{9,5},... | collective-permute-start | bytes 1843208 | tf_op jit(solution)/shard_map/ppermute | solution.py:380
  41.7 24.7 %collective-permute-start.15 = (bf16[800,768]{1,0:T(8,128)(2,1)S(1)}, bf16[800,768]{1,0:T(8,128)(2,1)S(1)}, u32[]{:S(2)}, u32[]{:S(2)}) collective-permute-start(bf16[800,768]{1,0:T(8,128)(2,1)S(1)} %constant_dynamic-update-slice_fusion), channel_id=1, source_target_pairs={{0,3},{1,2},{2,1},{3,0},{4,7},{5,6},{6,5},{7,4},{8,11},{9,10},{10,... | collective-permute-start | bytes 3686408 | tf_op jit(solution)/shard_map/ppermute | solution.py:380
  42.1 21.6 %collective-permute-start.16 = (bf16[400,768]{1,0:T(8,128)(2,1)S(1)}, bf16[400,768]{1,0:T(8,128)(2,1)S(1)}, u32[]{:S(2)}, u32[]{:S(2)}) collective-permute-start(bf16[400,768]{1,0:T(8,128)(2,1)S(1)} %constant_dynamic-update-slice_fusion.2), channel_id=1, source_target_pairs={{0,96},{1,97},{2,98},{3,99},{4,100},{5,101},{6,102},{7,103},{8,104... | collective-permute-start | bytes 1843208 | tf_op jit(solution)/shard_map/ppermute | solution.py:380
  52.3 20.4 %collective-permute-start.12 = (bf16[400,768]{1,0:T(8,128)(2,1)S(1)}, bf16[400,768]{1,0:T(8,128)(2,1)S(1)}, u32[]{:S(2)}, u32[]{:S(2)}) collective-permute-start(bf16[400,768]{1,0:T(8,128)(2,1)S(1)} %collective-permute-done.11.refs_5_), channel_id=1, source_target_pairs={{0,96},{1,97},{2,98},{3,99},{4,100},{5,101},{6,102},{7,103},{8,104... | collective-permute-start | bytes 1843208 | tf_op jit(solution)/shard_map/ppermute | solution.py:380
  53.5 25.8 %collective-permute-start.10 = (bf16[800,768]{1,0:T(8,128)(2,1)S(1)}, bf16[800,768]{1,0:T(8,128)(2,1)S(1)}, u32[]{:S(2)}, u32[]{:S(2)}) collective-permute-start(bf16[800,768]{1,0:T(8,128)(2,1)S(1)} %collective-permute-done.9.refs_4_), channel_id=1, source_target_pairs={{0,3},{1,2},{2,1},{3,0},{4,7},{5,6},{6,5},{7,4},{8,11},{9,10},{10,... | collective-permute-start | bytes 3686408 | tf_op jit(solution)/shard_map/ppermute | solution.py:380
  82.9 3.5 %collective-permute-start.17 = (bf16[592,768]{1,0:T(8,128)(2,1)S(1)}, bf16[592,768]{1,0:T(8,128)(2,1)S(1)}, u32[]{:S(2)}, u32[]{:S(2)}) collective-permute-start(bf16[592,768]{1,0:T(8,128)(2,1)S(1)} %flash.11), channel_id=1, source_target_pairs={{0,16},{1,17},{2,18},{3,19},{4,20},{5,21},{6,22},{7,23},{8,24},{9,... | collective-permute-start | bytes 2727944 | tf_op jit(solution)/shard_map/ppermute | solution.py:380
  86.4 16.3 %copy-start = (s32[384]{0:T(512)S(1)}, s32[384]{0:T(512)}, u32[]{:S(2)}) copy-start(s32[384]{0:T(512)} %clusters_ref.1) | copy-start | bytes 4612
  86.4 16.3 %copy-start.1 = (s32[32]{0:T(128)S(1)}, s32[32]{0:T(128)}, u32[]{:S(2)}) copy-start(s32[32]{0:T(128)} %owner_ref.1) | copy-start | bytes 388
  87.2 4.5 %collective-permute-start.18 = (bf16[80,768]{1,0:T(8,128)(2,1)S(1)}, bf16[80,768]{1,0:T(8,128)(2,1)S(1)}, u32[]{:S(2)}, u32[]{:S(2)}) collective-permute-start(bf16[80,768]{1,0:T(8,128)(2,1)S(1)} %get-tuple-element.87), channel_id=1, source_target_pairs={{0,4},{1,5},{2,6},{3,7},{4,0},{5,1},{6,2},{7,3},{8,12},{9,13},{10,... | collective-permute-start | bytes 368648 | tf_op jit(solution)/shard_map/ppermute | solution.py:380
  87.3 5.1 %collective-permute-start.19 = (bf16[80,768]{1,0:T(8,128)(2,1)S(1)}, bf16[80,768]{1,0:T(8,128)(2,1)S(1)}, u32[]{:S(2)}, u32[]{:S(2)}) collective-permute-start(bf16[80,768]{1,0:T(8,128)(2,1)S(1)} %get-tuple-element.88), channel_id=1, source_target_pairs={{0,32},{1,33},{2,34},{3,35},{4,36},{5,37},{6,38},{7,39},{8,40},{9,... | collective-permute-start | bytes 368648 | tf_op jit(solution)/shard_map/ppermute | solution.py:380
  87.3 7.3 %collective-permute-start.20 = (bf16[80,768]{1,0:T(8,128)(2,1)S(1)}, bf16[80,768]{1,0:T(8,128)(2,1)S(1)}, u32[]{:S(2)}, u32[]{:S(2)}) collective-permute-start(bf16[80,768]{1,0:T(8,128)(2,1)S(1)} %get-tuple-element.89), channel_id=1, source_target_pairs={{0,1},{1,0},{2,3},{3,2},{4,5},{5,4},{6,7},{7,6},{8,9},{9,8},{10,11... | collective-permute-start | bytes 368648 | tf_op jit(solution)/shard_map/ppermute | solution.py:380
  88.7 5.9 %collective-permute-start.21 = (bf16[80,768]{1,0:T(8,128)(2,1)S(1)}, bf16[80,768]{1,0:T(8,128)(2,1)S(1)}, u32[]{:S(2)}, u32[]{:S(2)}) collective-permute-start(bf16[80,768]{1,0:T(8,128)(2,1)S(1)} %get-tuple-element.90), channel_id=1, source_target_pairs={{0,36},{1,37},{2,38},{3,39},{4,32},{5,33},{6,34},{7,35},{8,44},{9,... | collective-permute-start | bytes 368648 | tf_op jit(solution)/shard_map/ppermute | solution.py:380
  91.2 7.4 %collective-permute-start.22 = (bf16[80,768]{1,0:T(8,128)(2,1)S(1)}, bf16[80,768]{1,0:T(8,128)(2,1)S(1)}, u32[]{:S(2)}, u32[]{:S(2)}) collective-permute-start(bf16[80,768]{1,0:T(8,128)(2,1)S(1)} %get-tuple-element.91), channel_id=1, source_target_pairs={{0,5},{1,4},{2,7},{3,6},{4,1},{5,0},{6,3},{7,2},{8,13},{9,12},{10,... | collective-permute-start | bytes 368648 | tf_op jit(solution)/shard_map/ppermute | solution.py:380
  91.6 11.0 %collective-permute-start.23 = (bf16[80,768]{1,0:T(8,128)(2,1)S(1)}, bf16[80,768]{1,0:T(8,128)(2,1)S(1)}, u32[]{:S(2)}, u32[]{:S(2)}) collective-permute-start(bf16[80,768]{1,0:T(8,128)(2,1)S(1)} %get-tuple-element.92), channel_id=1, source_target_pairs={{0,33},{1,32},{2,35},{3,34},{4,37},{5,36},{6,39},{7,38},{8,41},{9,... | collective-permute-start | bytes 368648 | tf_op jit(solution)/shard_map/ppermute | solution.py:380
  92.4 10.3 %collective-permute-start.24 = (bf16[80,768]{1,0:T(8,128)(2,1)S(1)}, bf16[80,768]{1,0:T(8,128)(2,1)S(1)}, u32[]{:S(2)}, u32[]{:S(2)}) collective-permute-start(bf16[80,768]{1,0:T(8,128)(2,1)S(1)} %get-tuple-element.93), channel_id=1, source_target_pairs={{0,37},{1,36},{2,39},{3,38},{4,33},{5,32},{6,35},{7,34},{8,45},{9,... | collective-permute-start | bytes 368648 | tf_op jit(solution)/shard_map/ppermute | solution.py:380

commit v6 on v5

--- a/solution.py
+++ b/solution.py
@@ -107,37 +107,33 @@
     return found
 
 
-def pack_kernel(*refs):
-    packets = [ref[...].astype(f32) for ref in refs[:8]]
-    big_ref, small_ref = refs[8:]
-    blocks = [
-        jnp.concatenate([packets[n][low:high] for n, low, high in spans(p)], axis=0)
-        for p in range(parts)
-    ]
-    ids = sum(packet[filled:packet_rows] for packet in packets)
+def pack_kernel(blocks, names, *refs):
+    packets = {n: ref[...].astype(f32) for n, ref in zip(names, refs)}
+    ids = sum(packet[filled:packet_rows] for packet in packets.values())
     at = lax.broadcasted_iota(jnp.int32, ids.shape, 0)
-    big_ref[0 : 2 * block_keys, :] = jnp.concatenate(blocks[:2], axis=0).astype(bf16)
-    big_ref[2 * block_keys : big_rows, :] = jnp.concatenate(
-        [jnp.where(at < 2, ids, 0.0), jnp.zeros_like(ids)], axis=0
-    ).astype(bf16)
-    last = jnp.sum(jnp.where(at == 2, ids, 0.0), axis=0, keepdims=True)
-    small_ref[...] = jnp.concatenate([blocks[2], jnp.where(at == 0, last, 0.0)], axis=0).astype(bf16)
-
-
-def pack(packets):
-    width = packets[0].shape[1]
+    rows = [packets[n][low:high] for p in blocks for n, low, high in spans(p)]
+    if len(blocks) == 2:
+        tail = [jnp.where(at < 2, ids, 0.0), jnp.zeros_like(ids)]
+    else:
+        last = jnp.sum(jnp.where(at == 2, ids, 0.0), axis=0, keepdims=True)
+        tail = [jnp.where(at == 0, last, 0.0)]
+    refs[-1][...] = jnp.concatenate(rows + tail, axis=0).astype(bf16)
+
+
+def pack(blocks, packets):
+    names = sorted({n for p in blocks for n, _, _ in spans(p)})
+    rows, width = (big_rows if len(blocks) == 2 else small_rows), packets[0].shape[1]
     return pl.pallas_call(
-        pack_kernel,
-        out_shape=[jax.ShapeDtypeStruct((count, width), bf16) for count in (big_rows, small_rows)],
-        in_specs=vmem_specs(8),
-        out_specs=vmem_specs(2),
+        functools.partial(pack_kernel, blocks, names),
+        out_shape=jax.ShapeDtypeStruct((rows, width), bf16),
+        in_specs=vmem_specs(len(names)),
+        out_specs=vmem_specs(1)[0],
         compiler_params=params,
         name="pack",
-    )(*packets)
-
-
-def column_of(row):
-    count = block_keys
+    )(*[packets[n] for n in names])
+
+
+def column_of(row, count=block_keys):
     wide = row.shape[1]
     eye = lax.broadcasted_iota(jnp.int32, (count, wide), 0) == lax.broadcasted_iota(
         jnp.int32, (count, wide), 1
@@ -326,27 +322,33 @@
         out_refs[n][...] = jnp.concatenate(pieces + [levels], axis=0).astype(bf16)
 
 
-def final_kernel(me_ref, owner_ref, clusters_ref, *refs):
-    backs, (rows_ref, mass_ref, back) = refs[:8], refs[8:]
+def choose_kernel(me_ref, owner_ref, clusters_ref, rows_ref, lanes_ref, chosen_ref):
     _, packet, rank, part, lane = row_facts(
         clusters_ref[...].reshape(1, clusters_ref.shape[0]), owner_ref, me_ref[0]
     )
+    count, total = rows_ref.shape
+    target = column_of((packet * packet_rows + rank).astype(f32), count).astype(jnp.int32)
+    at = lax.broadcasted_iota(jnp.int32, (count, total), 1)
+    rows_ref[...] = (at == target).astype(f32).astype(bf16)
+    lanes_ref[...] = ones_at(lanes_ref.shape[0], lane)
+    chosen = hits(64, packet * 8 + part) | hits(64, packet * 8 + 3 + part)
+    chosen_ref[...] = chosen.astype(f32)
+
+
+def final_kernel(choice_ref, lanes_ref, chosen_ref, *refs):
+    backs, (rows_ref, mass_ref, back) = refs[:8], refs[8:]
     for n in range(8):
         back[n * packet_rows : (n + 1) * packet_rows, :] = backs[n][...]
-    rows_ref[...] = lax.dot_general(
-        ones_at(8 * packet_rows, packet * packet_rows + rank),
-        back[...],
-        (((0,), (0,)), ((), ())),
-        preferred_element_type=f32,
+    rows_ref[...] = jnp.dot(
+        choice_ref[...], back[...], preferred_element_type=f32
     ).astype(bf16)
     levels = jnp.concatenate(
         [backs[n][64:packet_rows, 0:256].astype(f32)[8:16] for n in range(8)], axis=0
     ).astype(bf16)
-    found = jnp.dot(levels, ones_at(256, lane), preferred_element_type=f32)
-    chosen = hits(64, packet * 8 + part) | hits(64, packet * 8 + 3 + part)
-    mass_ref[...] = jnp.sum(jnp.where(chosen, found, 0.0), axis=0, keepdims=True).reshape(
-        mass_ref.shape
-    )
+    found = jnp.dot(levels, lanes_ref[...], preferred_element_type=f32)
+    mass_ref[...] = jnp.sum(
+        jnp.where(chosen_ref[...] > 0.0, found, 0.0), axis=0, keepdims=True
+    ).reshape(mass_ref.shape)
 
 
 def links(mesh):
@@ -402,7 +404,7 @@
         *(pltpu.with_memory_space_constraint(a, pltpu.HBM) for a in (cluster_owner, clusters, embeddings)),
     )
     arrived = [packets[0]] + [send(packets[n], trips[n]) for n in range(1, 8)]
-    big, small = pack(arrived)
+    big, small = pack((0, 1), arrived), pack((2,), arrived)
     wide = [
         [pair for pair in dims[s % 3] if pair[0] // 16 % 2 == 0]
         + [pair for pair in dims[(s + 1) % 3] if pair[0] // 16 % 2 == 1]
@@ -411,7 +413,6 @@
     narrow = [dims[(s + 2) % 3] for s in range(3)]
     big0, small0 = send(big, wide[0]), send(small, narrow[0])
     q_own, q_other = (big, small), (send(big, swap), send(small, swap))
-    big0, small0 = lax.optimization_barrier((big0, small0))
     big, small = jnp.concatenate([big, big0], axis=0), jnp.concatenate([small, small0], axis=0)
     big1, small1 = send(big, wide[1]), send(small, narrow[1])
     queries, owns = [q_other, q_own], [False, True]
@@ -436,15 +437,27 @@
         name="combine",
     )(*mine, theirs)
     back = [answers[0]] + [send(answers[n], trips[n]) for n in range(1, 8)]
+    choice = pl.pallas_call(
+        choose_kernel,
+        out_shape=[
+            jax.ShapeDtypeStruct((rows, 8 * packet_rows), bf16),
+            jax.ShapeDtypeStruct((256, rows), bf16),
+            jax.ShapeDtypeStruct((64, rows), f32),
+        ],
+        in_specs=[smem, smem] + vmem_specs(1),
+        out_specs=vmem_specs(3),
+        compiler_params=params,
+        name="choose",
+    )(me, cluster_owner, clusters)
     neighbours, log_mass = pl.pallas_call(
         final_kernel,
         out_shape=[jax.ShapeDtypeStruct((rows, width), bf16), jax.ShapeDtypeStruct((rows,), f32)],
-        in_specs=[smem, smem] + vmem_specs(9),
+        in_specs=vmem_specs(11),
         out_specs=vmem_specs(2),
         scratch_shapes=[pltpu.VMEM((8 * packet_rows, width), bf16)],
         compiler_params=params,
         name="final",
-    )(me, cluster_owner, clusters, *back)
+    )(*choice, *back)
     return neighbours, log_mass
 
 

time: 105 us -> 103 us (0.981); the launches traced: 105 us -> 101 us
  waiting for transfers between devices: 37.7 us -> 29.7 us
  starting transfers between devices: 34.9 us -> 38.8 us
    ppermute x25, waiting for transfers between devices: 37.7 us -> 29.7 us  [per_device(): send = lambda a, pairs: lax.ppermute(a, axes, pairs)]
    ppermute x25, starting transfers between devices: 34.9 us -> 38.8 us  [per_device(): send = lambda a, pairs: lax.ppermute(a, axes, pairs)]
  transfers between devices with their start and end apart: 25 -> 25, of which waited for: 11 -> 13; matrix products, arithmetic and copies ran while one was open for 0% -> 0% of each run, Pallas kernels for 21% -> 23%
where the time goes in v6:
time: 103 us; the launch traced here: 101 us
  starting transfers between devices  38.8 us (38%)
  Pallas kernels  31.5 us (31%)
  waiting for transfers between devices  29.7 us (29%)
    ppermute x25, starting transfers between devices, per_device(): send = lambda a, pairs: lax.ppermute(a, axes, pairs)  38.8 us
    ppermute x25, waiting for transfers between devices, per_device(): send = lambda a, pairs: lax.ppermute(a, axes, pairs)  29.7 us
    pallas_call x6, Pallas kernels, flash(): pl.pallas_call(functools.partial(flash_kernel, wides, first, owns, finish...  25.7 us
    pallas_call x1, Pallas kernels, per_device(): pl.pallas_call(place_kernel, out_shape=[packet] * 8, in_specs=[smem] + [p...  2.46 us
  transfers between devices with their start and end apart: 25, of which 13 were waited for; matrix products, arithmetic and copies ran while one was open for 0% of the time, Pallas kernels for 23%

profile of v6, /device:TPU:1, one launch (start us, length us, event | category | flops | bytes accessed | tf_op | source)
XLA Modules:
  0.0 101.2 jit_solution(11145359420963893259)
XLA Ops:
  0.8 2.5 %place.1 = (bf16[80,768]{1,0:T(8,128)(2,1)S(1)}, bf16[80,768]{1,0:T(8,128)(2,1)S(1)}, bf16[80,768]{1,0:T(8,128)(2,1)S(1)}, bf16[80,768]{1,0:T(8,128)(2,1)S(1)}, ...) custom-call(s32[1]{0:T(128)} %bitcast.me_ref, ...), custom_call_target="tpu_custom_call" | custom-call | tf_op jit(solution)/shard_map/place/pallas_call | solution.py:389
  3.2 3.5 %collective-permute-start.4 = (bf16[80,768]{1,0:T(8,128)(2,1)S(1)}, bf16[80,768]{1,0:T(8,128)(2,1)S(1)}, u32[]{:S(2)}, u32[]{:S(2)}) collective-permute-start(bf16[80,768]{1,0:T(8,128)(2,1)S(1)} %get-tuple-element.55), channel_id=1, source_target_pairs={{0,5},{1,4},{2,7},{3,6},{4,1},{5,0},{6,3},{7,2},{8,13},{9,12},{10,... | collective-permute-start | bytes 368648 | tf_op jit(solution)/shard_map/ppermute | solution.py:382
  7.0 1.3 %collective-permute-start.1 = (bf16[80,768]{1,0:T(8,128)(2,1)S(1)}, bf16[80,768]{1,0:T(8,128)(2,1)S(1)}, u32[]{:S(2)}, u32[]{:S(2)}) collective-permute-start(bf16[80,768]{1,0:T(8,128)(2,1)S(1)} %get-tuple-element.52), channel_id=1, source_target_pairs={{0,32},{1,33},{2,34},{3,35},{4,36},{5,37},{6,38},{7,39},{8,40},{9,... | collective-permute-start | bytes 368648 | tf_op jit(solution)/shard_map/ppermute | solution.py:382
  8.4 1.0 collective-permute-start.3
  9.8 2.6 %collective-permute-done.refs_1_ = bf16[80,768]{1,0:T(8,128)(2,1)S(1)} collective-permute-done((bf16[80,768]{1,0:T(8,128)(2,1)S(1)}, bf16[80,768]{1,0:T(8,128)(2,1)S(1)}, u32[]{:S(2)}, u32[]{:S(2)}) %collective-permute-start) | collective-permute-done | bytes 122912 | tf_op jit(solution)/shard_map/ppermute | solution.py:382
  12.5 3.4 %collective-permute-done.3.refs_4_ = bf16[80,768]{1,0:T(8,128)(2,1)S(1)} collective-permute-done((bf16[80,768]{1,0:T(8,128)(2,1)S(1)}, bf16[80,768]{1,0:T(8,128)(2,1)S(1)}, u32[]{:S(2)}, u32[]{:S(2)}) %collective-permute-start.3) | collective-permute-done | bytes 122912 | tf_op jit(solution)/shard_map/ppermute | solution.py:382
  16.0 2.0 %collective-permute-start.7 = (bf16[400,768]{1,0:T(8,128)(2,1)S(1)}, bf16[400,768]{1,0:T(8,128)(2,1)S(1)}, u32[]{:S(2)}, u32[]{:S(2)}) collective-permute-start(bf16[400,768]{1,0:T(8,128)(2,1)S(1)} %pack.2.refs_0_.refs_2_), channel_id=1, source_target_pairs={{0,12},{1,13},{2,14},{3,15},{4,8},{5,9},{6,10},{7,11},{8,4},{9,5},... | collective-permute-start | bytes 1843208 | tf_op jit(solution)/shard_map/ppermute | solution.py:382
  18.2 3.1 %collective-permute-start.6 = (bf16[80,768]{1,0:T(8,128)(2,1)S(1)}, bf16[80,768]{1,0:T(8,128)(2,1)S(1)}, u32[]{:S(2)}, u32[]{:S(2)}) collective-permute-start(bf16[80,768]{1,0:T(8,128)(2,1)S(1)} %get-tuple-element.57), channel_id=1, source_target_pairs={{0,37},{1,36},{2,39},{3,38},{4,33},{5,32},{6,35},{7,34},{8,45},{9,... | collective-permute-start | bytes 368648 | tf_op jit(solution)/shard_map/ppermute | solution.py:382
  21.3 3.0 %collective-permute-done.5.refs_1_ = bf16[80,768]{1,0:T(8,128)(2,1)S(1)} collective-permute-done((bf16[80,768]{1,0:T(8,128)(2,1)S(1)}, bf16[80,768]{1,0:T(8,128)(2,1)S(1)}, u32[]{:S(2)}, u32[]{:S(2)}) %collective-permute-start.5) | collective-permute-done | bytes 122912 | tf_op jit(solution)/shard_map/ppermute | solution.py:382
  24.3 3.2 %collective-permute-start.10 = (bf16[200,768]{1,0:T(8,128)(2,1)S(1)}, bf16[200,768]{1,0:T(8,128)(2,1)S(1)}, u32[]{:S(2)}, u32[]{:S(2)}) collective-permute-start(bf16[200,768]{1,0:T(8,128)(2,1)S(1)} %pack.3.refs_1_.refs_3_), channel_id=1, source_target_pairs={{0,3},{1,2},{2,1},{3,0},{4,7},{5,6},{6,5},{7,4},{8,11},{9,10},{10,... | collective-permute-start | bytes 921608 | tf_op jit(solution)/shard_map/ppermute | solution.py:382
  27.5 1.5 %collective-permute-start.8 = (bf16[800,768]{1,0:T(8,128)(2,1)S(1)}, bf16[800,768]{1,0:T(8,128)(2,1)S(1)}, u32[]{:S(2)}, u32[]{:S(2)}) collective-permute-start(bf16[800,768]{1,0:T(8,128)(2,1)S(1)} %pad_maximum_fusion), channel_id=1, source_target_pairs={{0,96},{1,97},{2,98},{3,99},{4,100},{5,101},{6,102},{7,103},{8,104... | collective-permute-start | bytes 3686408 | tf_op jit(solution)/shard_map/ppermute | solution.py:382
  29.0 5.4 %collective-permute-start.13 = (bf16[400,768]{1,0:T(8,128)(2,1)S(1)}, bf16[400,768]{1,0:T(8,128)(2,1)S(1)}, u32[]{:S(2)}, u32[]{:S(2)}) collective-permute-start(bf16[400,768]{1,0:T(8,128)(2,1)S(1)} %pack.2.refs_0_.refs_2_), channel_id=1, source_target_pairs={{0,16},{1,17},{2,18},{3,19},{4,20},{5,21},{6,22},{7,23},{8,24},{9,... | collective-permute-start | bytes 1843208 | tf_op jit(solution)/shard_map/ppermute | solution.py:382
  34.5 3.6 %collective-permute-start.11 = (bf16[400,768]{1,0:T(8,128)(2,1)S(1)}, bf16[400,768]{1,0:T(8,128)(2,1)S(1)}, u32[]{:S(2)}, u32[]{:S(2)}) collective-permute-start(bf16[400,768]{1,0:T(8,128)(2,1)S(1)} %pad_maximum_fusion.1), channel_id=1, source_target_pairs={{0,12},{1,13},{2,14},{3,15},{4,8},{5,9},{6,10},{7,11},{8,4},{9,5},... | collective-permute-start | bytes 1843208 | tf_op jit(solution)/shard_map/ppermute | solution.py:382
  38.1 3.2 %flash.6 = (f32[576,1]{1,0:T(8,128)S(1)}, f32[576,1]{1,0:T(8,128)S(1)}, f32[576,768]{1,0:T(8,128)S(1)}) custom-call(bf16[400,768]{1,0:T(8,128)(2,1)S(1)} %pack.2.refs_0_.refs_2_, bf16[200,768]{1,0:T(8,128)(2,1)S(1)} %pack.3.refs_1_.refs_3_, bf16[400,768]{1,0:T(8,128)(2,1)S(1)} %pack.2.refs_0_.refs_2_, bf16[200,768]{1,0:T(8,128)(2,1)S(1)} %pack.3.refs_1_.refs_3_, ...), custom_call_target="tpu_custom_call" | custom-call | flops 4076863488 | bytes 4423680 | tf_op jit(solution)/shard_map/flash/pallas_call | solution.py:269
  41.5 3.1 %flash.7 = (f32[576,1]{1,0:T(8,128)S(1)}, f32[576,1]{1,0:T(8,128)S(1)}, f32[576,768]{1,0:T(8,128)S(1)}) custom-call(bf16[400,768]{1,0:T(8,128)(2,1)S(1)} %collective-permute-done.13.refs_0_, bf16[200,768]{1,0:T(8,128)(2,1)S(1)} %collective-permute-done.14.refs_1_, bf16[400,768]{1,0:T(8,128)(2,1)S(1)} %pack.2.refs_0_.refs_2_, ...), custom_call_target="tpu_custom_call" | custom-call | flops 4076863488 | bytes 4423680 | tf_op jit(solution)/shard_map/flash/pallas_call | solution.py:269
  44.6 3.3 %collective-permute-done.11.refs_5_ = bf16[400,768]{1,0:T(8,128)(2,1)S(1)} collective-permute-done((bf16[400,768]{1,0:T(8,128)(2,1)S(1)}, bf16[400,768]{1,0:T(8,128)(2,1)S(1)}, u32[]{:S(2)}, u32[]{:S(2)}) %collective-permute-start.11) | collective-permute-done | bytes 614432 | tf_op jit(solution)/shard_map/ppermute | solution.py:382
  48.4 6.5 %collective-permute-start.9 = (bf16[800,768]{1,0:T(8,128)(2,1)S(1)}, bf16[800,768]{1,0:T(8,128)(2,1)S(1)}, u32[]{:S(2)}, u32[]{:S(2)}) collective-permute-start(bf16[800,768]{1,0:T(8,128)(2,1)S(1)} %collective-permute-done.8.refs_4_), channel_id=1, source_target_pairs={{0,3},{1,2},{2,1},{3,0},{4,7},{5,6},{6,5},{7,4},{8,11},{9,10},{10,... | collective-permute-start | bytes 3686408 | tf_op jit(solution)/shard_map/ppermute | solution.py:382
  55.0 6.2 %flash.8 = (f32[576,1]{1,0:T(8,128)S(1)}, f32[576,1]{1,0:T(8,128)S(1)}, f32[576,768]{1,0:T(8,128)S(1)}, f32[576,1]{1,0:T(8,128)S(1)}, f32[576,1]{1,0:T(8,128)S(1)}, /*index=5*/f32[576,768]{1,0:T(8,128)S(1)}) custom-call(bf16[400,768]{1,0:T(8,128)(2,1)S(1)} %collective-permute-done.13.refs_0_, bf16[200,768]{1,0:T(8,128)(2,1)S(1)} %collective-permute-done.14.refs_1_, ...), custom_call_target="tpu_custom_call" | custom-call | flops 8153726976 | bytes 7077888 | tf_op jit(solution)/shard_map/flash/pallas_call | solution.py:269
  61.2 4.4 %collective-permute-done.15.refs_4_ = bf16[800,768]{1,0:T(8,128)(2,1)S(1)} collective-permute-done((bf16[800,768]{1,0:T(8,128)(2,1)S(1)}, bf16[800,768]{1,0:T(8,128)(2,1)S(1)}, u32[]{:S(2)}, u32[]{:S(2)}) %collective-permute-start.15) | collective-permute-done | bytes 1228832 | tf_op jit(solution)/shard_map/ppermute | solution.py:382
  65.7 6.3 %flash.9 = (f32[576,1]{1,0:T(8,128)S(1)}, f32[576,1]{1,0:T(8,128)S(1)}, f32[576,768]{1,0:T(8,128)S(1)}, f32[576,1]{1,0:T(8,128)S(1)}, f32[576,1]{1,0:T(8,128)S(1)}, /*index=5*/f32[576,768]{1,0:T(8,128)S(1)}) custom-call(bf16[400,768]{1,0:T(8,128)(2,1)S(1)} %collective-permute-done.13.refs_0_, bf16[200,768]{1,0:T(8,128)(2,1)S(1)} %collective-permute-done.14.refs_1_, ...), custom_call_target="tpu_custom_call" | custom-call | flops 8153726976 | bytes 7077888 | tf_op jit(solution)/shard_map/flash/pallas_call | solution.py:269
  72.0 6.6 %collective-permute-done.9.refs_2_ = bf16[800,768]{1,0:T(8,128)(2,1)S(1)} collective-permute-done((bf16[800,768]{1,0:T(8,128)(2,1)S(1)}, bf16[800,768]{1,0:T(8,128)(2,1)S(1)}, u32[]{:S(2)}, u32[]{:S(2)}) %collective-permute-start.9) | collective-permute-done | bytes 1228832 | tf_op jit(solution)/shard_map/ppermute | solution.py:382
  78.5 3.6 %flash.11 = bf16[592,768]{1,0:T(8,128)(2,1)S(1)} custom-call(bf16[400,768]{1,0:T(8,128)(2,1)S(1)} %collective-permute-done.13.refs_0_, bf16[200,768]{1,0:T(8,128)(2,1)S(1)} %collective-permute-done.14.refs_1_, bf16[800,768]{1,0:T(8,128)(2,1)S(1)} %collective-permute-done.9.refs_2_, bf16[400,768]{1,0:T(8,128)(2,1)S(1)} %collective-permute-done.12.refs_3_, ...), custom_call_target="tpu_custom_call" | custom-call | flops 4076863488 | bytes 4423680 | tf_op jit(solution)/shard_map/flash/pallas_call | solution.py:269
  82.2 3.3 %flash.10 = (f32[576,1]{1,0:T(8,128)S(1)}, f32[576,1]{1,0:T(8,128)S(1)}, f32[576,768]{1,0:T(8,128)S(1)}) custom-call(bf16[400,768]{1,0:T(8,128)(2,1)S(1)} %pack.2.refs_0_.refs_2_, bf16[200,768]{1,0:T(8,128)(2,1)S(1)} %pack.3.refs_1_.refs_3_, bf16[800,768]{1,0:T(8,128)(2,1)S(1)} %collective-permute-done.9.refs_2_, ...), custom_call_target="tpu_custom_call" | custom-call | flops 4076863488 | bytes 4423680 | tf_op jit(solution)/shard_map/flash/pallas_call | solution.py:269
  85.6 0.8 combine.1
  86.4 1.1 %collective-permute-start.19 = (bf16[80,768]{1,0:T(8,128)(2,1)S(1)}, bf16[80,768]{1,0:T(8,128)(2,1)S(1)}, u32[]{:S(2)}, u32[]{:S(2)}) collective-permute-start(bf16[80,768]{1,0:T(8,128)(2,1)S(1)} %get-tuple-element.86), channel_id=1, source_target_pairs={{0,32},{1,33},{2,34},{3,35},{4,36},{5,37},{6,38},{7,39},{8,40},{9,... | collective-permute-start | bytes 368648 | tf_op jit(solution)/shard_map/ppermute | solution.py:382
  88.1 1.6 %collective-permute-start.21 = (bf16[80,768]{1,0:T(8,128)(2,1)S(1)}, bf16[80,768]{1,0:T(8,128)(2,1)S(1)}, u32[]{:S(2)}, u32[]{:S(2)}) collective-permute-start(bf16[80,768]{1,0:T(8,128)(2,1)S(1)} %get-tuple-element.88), channel_id=1, source_target_pairs={{0,36},{1,37},{2,38},{3,39},{4,32},{5,33},{6,34},{7,35},{8,44},{9,... | collective-permute-start | bytes 368648 | tf_op jit(solution)/shard_map/ppermute | solution.py:382
  90.8 1.3 %collective-permute-start.23 = (bf16[80,768]{1,0:T(8,128)(2,1)S(1)}, bf16[80,768]{1,0:T(8,128)(2,1)S(1)}, u32[]{:S(2)}, u32[]{:S(2)}) collective-permute-start(bf16[80,768]{1,0:T(8,128)(2,1)S(1)} %get-tuple-element.90), channel_id=1, source_target_pairs={{0,33},{1,32},{2,35},{3,34},{4,37},{5,36},{6,39},{7,38},{8,41},{9,... | collective-permute-start | bytes 368648 | tf_op jit(solution)/shard_map/ppermute | solution.py:382
  92.2 1.6 %collective-permute-start.24 = (bf16[80,768]{1,0:T(8,128)(2,1)S(1)}, bf16[80,768]{1,0:T(8,128)(2,1)S(1)}, u32[]{:S(2)}, u32[]{:S(2)}) collective-permute-start(bf16[80,768]{1,0:T(8,128)(2,1)S(1)} %get-tuple-element.91), channel_id=1, source_target_pairs={{0,37},{1,36},{2,39},{3,38},{4,33},{5,32},{6,35},{7,34},{8,45},{9,... | collective-permute-start | bytes 368648 | tf_op jit(solution)/shard_map/ppermute | solution.py:382
  93.8 1.0 choose.1
  94.8 1.4 %collective-permute-done.22.refs_5_ = bf16[80,768]{1,0:T(8,128)(2,1)S(1)} collective-permute-done((bf16[80,768]{1,0:T(8,128)(2,1)S(1)}, bf16[80,768]{1,0:T(8,128)(2,1)S(1)}, u32[]{:S(2)}, u32[]{:S(2)}) %collective-permute-start.22) | collective-permute-done | bytes 122912 | tf_op jit(solution)/shard_map/ppermute | solution.py:382
  96.8 2.9 %collective-permute-done.24.refs_7_ = bf16[80,768]{1,0:T(8,128)(2,1)S(1)} collective-permute-done((bf16[80,768]{1,0:T(8,128)(2,1)S(1)}, bf16[80,768]{1,0:T(8,128)(2,1)S(1)}, u32[]{:S(2)}, u32[]{:S(2)}) %collective-permute-start.24) | collective-permute-done | bytes 122912 | tf_op jit(solution)/shard_map/ppermute | solution.py:382
  99.7 1.5 %final.1 = (bf16[384,768]{1,0:T(8,128)(2,1)}, f32[384]{0:T(512)}) custom-call(bf16[384,640]{1,0:T(8,128)(2,1)S(1)} %get-tuple-element.47.choice_ref, bf16[256,384]{1,0:T(8,128)(2,1)S(1)} %get-tuple-element.48.lanes_ref, f32[64,384]{1,0:T(8,128)S(1)} %get-tuple-element.49.chosen_ref, bf16[80,768]{1,0:T(8,128)(2,1)S(1)} %get-tuple-element.84.refs_0_, ...), custom_call_target="tpu_custom_call" | custom-call | tf_op jit(solution)/shard_map/final/pallas_call | solution.py:452
  (36 shorter events, 4.6 us)
Async XLA Ops:
  3.2 6.5 %collective-permute-start.4 = (bf16[80,768]{1,0:T(8,128)(2,1)S(1)}, bf16[80,768]{1,0:T(8,128)(2,1)S(1)}, u32[]{:S(2)}, u32[]{:S(2)}) collective-permute-start(bf16[80,768]{1,0:T(8,128)(2,1)S(1)} %get-tuple-element.55), channel_id=1, source_target_pairs={{0,5},{1,4},{2,7},{3,6},{4,1},{5,0},{6,3},{7,2},{8,13},{9,12},{10,... | collective-permute-start | bytes 368648 | tf_op jit(solution)/shard_map/ppermute | solution.py:382
  6.7 5.6 %collective-permute-start = (bf16[80,768]{1,0:T(8,128)(2,1)S(1)}, bf16[80,768]{1,0:T(8,128)(2,1)S(1)}, u32[]{:S(2)}, u32[]{:S(2)}) collective-permute-start(bf16[80,768]{1,0:T(8,128)(2,1)S(1)} %get-tuple-element.51), channel_id=1, source_target_pairs={{0,4},{1,5},{2,6},{3,7},{4,0},{5,1},{6,2},{7,3},{8,12},{9,13},{10,... | collective-permute-start | bytes 368648 | tf_op jit(solution)/shard_map/ppermute | solution.py:382
  7.0 5.4 %collective-permute-start.1 = (bf16[80,768]{1,0:T(8,128)(2,1)S(1)}, bf16[80,768]{1,0:T(8,128)(2,1)S(1)}, u32[]{:S(2)}, u32[]{:S(2)}) collective-permute-start(bf16[80,768]{1,0:T(8,128)(2,1)S(1)} %get-tuple-element.52), channel_id=1, source_target_pairs={{0,32},{1,33},{2,34},{3,35},{4,36},{5,37},{6,38},{7,39},{8,40},{9,... | collective-permute-start | bytes 368648 | tf_op jit(solution)/shard_map/ppermute | solution.py:382
  8.3 4.3 %collective-permute-start.2 = (bf16[80,768]{1,0:T(8,128)(2,1)S(1)}, bf16[80,768]{1,0:T(8,128)(2,1)S(1)}, u32[]{:S(2)}, u32[]{:S(2)}) collective-permute-start(bf16[80,768]{1,0:T(8,128)(2,1)S(1)} %get-tuple-element.53), channel_id=1, source_target_pairs={{0,1},{1,0},{2,3},{3,2},{4,5},{5,4},{6,7},{7,6},{8,9},{9,8},{10,11... | collective-permute-start | bytes 368648 | tf_op jit(solution)/shard_map/ppermute | solution.py:382
  8.4 7.6 %collective-permute-start.3 = (bf16[80,768]{1,0:T(8,128)(2,1)S(1)}, bf16[80,768]{1,0:T(8,128)(2,1)S(1)}, u32[]{:S(2)}, u32[]{:S(2)}) collective-permute-start(bf16[80,768]{1,0:T(8,128)(2,1)S(1)} %get-tuple-element.54), channel_id=1, source_target_pairs={{0,36},{1,37},{2,38},{3,39},{4,32},{5,33},{6,34},{7,35},{8,44},{9,... | collective-permute-start | bytes 368648 | tf_op jit(solution)/shard_map/ppermute | solution.py:382
  16.0 11.4 %collective-permute-start.7 = (bf16[400,768]{1,0:T(8,128)(2,1)S(1)}, bf16[400,768]{1,0:T(8,128)(2,1)S(1)}, u32[]{:S(2)}, u32[]{:S(2)}) collective-permute-start(bf16[400,768]{1,0:T(8,128)(2,1)S(1)} %pack.2.refs_0_.refs_2_), channel_id=1, source_target_pairs={{0,12},{1,13},{2,14},{3,15},{4,8},{5,9},{6,10},{7,11},{8,4},{9,5},... | collective-permute-start | bytes 1843208 | tf_op jit(solution)/shard_map/ppermute | solution.py:382
  18.0 6.2 %collective-permute-start.5 = (bf16[80,768]{1,0:T(8,128)(2,1)S(1)}, bf16[80,768]{1,0:T(8,128)(2,1)S(1)}, u32[]{:S(2)}, u32[]{:S(2)}) collective-permute-start(bf16[80,768]{1,0:T(8,128)(2,1)S(1)} %get-tuple-element.56), channel_id=1, source_target_pairs={{0,33},{1,32},{2,35},{3,34},{4,37},{5,36},{6,39},{7,38},{8,41},{9,... | collective-permute-start | bytes 368648 | tf_op jit(solution)/shard_map/ppermute | solution.py:382
  18.2 6.1 %collective-permute-start.6 = (bf16[80,768]{1,0:T(8,128)(2,1)S(1)}, bf16[80,768]{1,0:T(8,128)(2,1)S(1)}, u32[]{:S(2)}, u32[]{:S(2)}) collective-permute-start(bf16[80,768]{1,0:T(8,128)(2,1)S(1)} %get-tuple-element.57), channel_id=1, source_target_pairs={{0,37},{1,36},{2,39},{3,38},{4,33},{5,32},{6,35},{7,34},{8,45},{9,... | collective-permute-start | bytes 368648 | tf_op jit(solution)/shard_map/ppermute | solution.py:382
  24.3 10.1 %collective-permute-start.10 = (bf16[200,768]{1,0:T(8,128)(2,1)S(1)}, bf16[200,768]{1,0:T(8,128)(2,1)S(1)}, u32[]{:S(2)}, u32[]{:S(2)}) collective-permute-start(bf16[200,768]{1,0:T(8,128)(2,1)S(1)} %pack.3.refs_1_.refs_3_), channel_id=1, source_target_pairs={{0,3},{1,2},{2,1},{3,0},{4,7},{5,6},{6,5},{7,4},{8,11},{9,10},{10,... | collective-permute-start | bytes 921608 | tf_op jit(solution)/shard_map/ppermute | solution.py:382
  27.5 20.9 %collective-permute-start.8 = (bf16[800,768]{1,0:T(8,128)(2,1)S(1)}, bf16[800,768]{1,0:T(8,128)(2,1)S(1)}, u32[]{:S(2)}, u32[]{:S(2)}) collective-permute-start(bf16[800,768]{1,0:T(8,128)(2,1)S(1)} %pad_maximum_fusion), channel_id=1, source_target_pairs={{0,96},{1,97},{2,98},{3,99},{4,100},{5,101},{6,102},{7,103},{8,104... | collective-permute-start | bytes 3686408 | tf_op jit(solution)/shard_map/ppermute | solution.py:382
  29.0 12.4 %collective-permute-start.13 = (bf16[400,768]{1,0:T(8,128)(2,1)S(1)}, bf16[400,768]{1,0:T(8,128)(2,1)S(1)}, u32[]{:S(2)}, u32[]{:S(2)}) collective-permute-start(bf16[400,768]{1,0:T(8,128)(2,1)S(1)} %pack.2.refs_0_.refs_2_), channel_id=1, source_target_pairs={{0,16},{1,17},{2,18},{3,19},{4,20},{5,21},{6,22},{7,23},{8,24},{9,... | collective-permute-start | bytes 1843208 | tf_op jit(solution)/shard_map/ppermute | solution.py:382
  34.4 6.9 %collective-permute-start.14 = (bf16[200,768]{1,0:T(8,128)(2,1)S(1)}, bf16[200,768]{1,0:T(8,128)(2,1)S(1)}, u32[]{:S(2)}, u32[]{:S(2)}) collective-permute-start(bf16[200,768]{1,0:T(8,128)(2,1)S(1)} %pack.3.refs_1_.refs_3_), channel_id=1, source_target_pairs={{0,16},{1,17},{2,18},{3,19},{4,20},{5,21},{6,22},{7,23},{8,24},{9,... | collective-permute-start | bytes 921608 | tf_op jit(solution)/shard_map/ppermute | solution.py:382
  34.5 13.4 %collective-permute-start.11 = (bf16[400,768]{1,0:T(8,128)(2,1)S(1)}, bf16[400,768]{1,0:T(8,128)(2,1)S(1)}, u32[]{:S(2)}, u32[]{:S(2)}) collective-permute-start(bf16[400,768]{1,0:T(8,128)(2,1)S(1)} %pad_maximum_fusion.1), channel_id=1, source_target_pairs={{0,12},{1,13},{2,14},{3,15},{4,8},{5,9},{6,10},{7,11},{8,4},{9,5},... | collective-permute-start | bytes 1843208 | tf_op jit(solution)/shard_map/ppermute | solution.py:382
  41.3 24.4 %collective-permute-start.15 = (bf16[800,768]{1,0:T(8,128)(2,1)S(1)}, bf16[800,768]{1,0:T(8,128)(2,1)S(1)}, u32[]{:S(2)}, u32[]{:S(2)}) collective-permute-start(bf16[800,768]{1,0:T(8,128)(2,1)S(1)} %pad_maximum_fusion), channel_id=1, source_target_pairs={{0,3},{1,2},{2,1},{3,0},{4,7},{5,6},{6,5},{7,4},{8,11},{9,10},{10,... | collective-permute-start | bytes 3686408 | tf_op jit(solution)/shard_map/ppermute | solution.py:382
  41.4 19.9 %collective-permute-start.16 = (bf16[400,768]{1,0:T(8,128)(2,1)S(1)}, bf16[400,768]{1,0:T(8,128)(2,1)S(1)}, u32[]{:S(2)}, u32[]{:S(2)}) collective-permute-start(bf16[400,768]{1,0:T(8,128)(2,1)S(1)} %pad_maximum_fusion.1), channel_id=1, source_target_pairs={{0,96},{1,97},{2,98},{3,99},{4,100},{5,101},{6,102},{7,103},{8,104... | collective-permute-start | bytes 1843208 | tf_op jit(solution)/shard_map/ppermute | solution.py:382
  47.9 24.1 %collective-permute-start.12 = (bf16[400,768]{1,0:T(8,128)(2,1)S(1)}, bf16[400,768]{1,0:T(8,128)(2,1)S(1)}, u32[]{:S(2)}, u32[]{:S(2)}) collective-permute-start(bf16[400,768]{1,0:T(8,128)(2,1)S(1)} %collective-permute-done.11.refs_5_), channel_id=1, source_target_pairs={{0,96},{1,97},{2,98},{3,99},{4,100},{5,101},{6,102},{7,103},{8,104... | collective-permute-start | bytes 1843208 | tf_op jit(solution)/shard_map/ppermute | solution.py:382
  48.4 30.1 %collective-permute-start.9 = (bf16[800,768]{1,0:T(8,128)(2,1)S(1)}, bf16[800,768]{1,0:T(8,128)(2,1)S(1)}, u32[]{:S(2)}, u32[]{:S(2)}) collective-permute-start(bf16[800,768]{1,0:T(8,128)(2,1)S(1)} %collective-permute-done.8.refs_4_), channel_id=1, source_target_pairs={{0,3},{1,2},{2,1},{3,0},{4,7},{5,6},{6,5},{7,4},{8,11},{9,10},{10,... | collective-permute-start | bytes 3686408 | tf_op jit(solution)/shard_map/ppermute | solution.py:382
  82.1 3.4 %collective-permute-start.17 = (bf16[592,768]{1,0:T(8,128)(2,1)S(1)}, bf16[592,768]{1,0:T(8,128)(2,1)S(1)}, u32[]{:S(2)}, u32[]{:S(2)}) collective-permute-start(bf16[592,768]{1,0:T(8,128)(2,1)S(1)} %flash.11), channel_id=1, source_target_pairs={{0,16},{1,17},{2,18},{3,19},{4,20},{5,21},{6,22},{7,23},{8,24},{9,... | collective-permute-start | bytes 2727944 | tf_op jit(solution)/shard_map/ppermute | solution.py:382
  85.5 8.3 %copy-start = (s32[384]{0:T(512)S(1)}, s32[384]{0:T(512)}, u32[]{:S(2)}) copy-start(s32[384]{0:T(512)} %clusters_hbm.1) | copy-start | bytes 4612
  85.5 8.3 %copy-start.1 = (s32[32]{0:T(128)S(1)}, s32[32]{0:T(128)}, u32[]{:S(2)}) copy-start(s32[32]{0:T(128)} %owner_hbm.1) | copy-start | bytes 388
  86.3 4.5 %collective-permute-start.18 = (bf16[80,768]{1,0:T(8,128)(2,1)S(1)}, bf16[80,768]{1,0:T(8,128)(2,1)S(1)}, u32[]{:S(2)}, u32[]{:S(2)}) collective-permute-start(bf16[80,768]{1,0:T(8,128)(2,1)S(1)} %get-tuple-element.85), channel_id=1, source_target_pairs={{0,4},{1,5},{2,6},{3,7},{4,0},{5,1},{6,2},{7,3},{8,12},{9,13},{10,... | collective-permute-start | bytes 368648 | tf_op jit(solution)/shard_map/ppermute | solution.py:382
  86.4 5.7 %collective-permute-start.19 = (bf16[80,768]{1,0:T(8,128)(2,1)S(1)}, bf16[80,768]{1,0:T(8,128)(2,1)S(1)}, u32[]{:S(2)}, u32[]{:S(2)}) collective-permute-start(bf16[80,768]{1,0:T(8,128)(2,1)S(1)} %get-tuple-element.86), channel_id=1, source_target_pairs={{0,32},{1,33},{2,34},{3,35},{4,36},{5,37},{6,38},{7,39},{8,40},{9,... | collective-permute-start | bytes 368648 | tf_op jit(solution)/shard_map/ppermute | solution.py:382
  87.5 7.3 %collective-permute-start.20 = (bf16[80,768]{1,0:T(8,128)(2,1)S(1)}, bf16[80,768]{1,0:T(8,128)(2,1)S(1)}, u32[]{:S(2)}, u32[]{:S(2)}) collective-permute-start(bf16[80,768]{1,0:T(8,128)(2,1)S(1)} %get-tuple-element.87), channel_id=1, source_target_pairs={{0,1},{1,0},{2,3},{3,2},{4,5},{5,4},{6,7},{7,6},{8,9},{9,8},{10,11... | collective-permute-start | bytes 368648 | tf_op jit(solution)/shard_map/ppermute | solution.py:382
  88.1 6.7 %collective-permute-start.21 = (bf16[80,768]{1,0:T(8,128)(2,1)S(1)}, bf16[80,768]{1,0:T(8,128)(2,1)S(1)}, u32[]{:S(2)}, u32[]{:S(2)}) collective-permute-start(bf16[80,768]{1,0:T(8,128)(2,1)S(1)} %get-tuple-element.88), channel_id=1, source_target_pairs={{0,36},{1,37},{2,38},{3,39},{4,32},{5,33},{6,34},{7,35},{8,44},{9,... | collective-permute-start | bytes 368648 | tf_op jit(solution)/shard_map/ppermute | solution.py:382
  89.7 6.5 %collective-permute-start.22 = (bf16[80,768]{1,0:T(8,128)(2,1)S(1)}, bf16[80,768]{1,0:T(8,128)(2,1)S(1)}, u32[]{:S(2)}, u32[]{:S(2)}) collective-permute-start(bf16[80,768]{1,0:T(8,128)(2,1)S(1)} %get-tuple-element.89), channel_id=1, source_target_pairs={{0,5},{1,4},{2,7},{3,6},{4,1},{5,0},{6,3},{7,2},{8,13},{9,12},{10,... | collective-permute-start | bytes 368648 | tf_op jit(solution)/shard_map/ppermute | solution.py:382
  90.8 6.0 %collective-permute-start.23 = (bf16[80,768]{1,0:T(8,128)(2,1)S(1)}, bf16[80,768]{1,0:T(8,128)(2,1)S(1)}, u32[]{:S(2)}, u32[]{:S(2)}) collective-permute-start(bf16[80,768]{1,0:T(8,128)(2,1)S(1)} %get-tuple-element.90), channel_id=1, source_target_pairs={{0,33},{1,32},{2,35},{3,34},{4,37},{5,36},{6,39},{7,38},{8,41},{9,... | collective-permute-start | bytes 368648 | tf_op jit(solution)/shard_map/ppermute | solution.py:382
  92.2 7.5 %collective-permute-start.24 = (bf16[80,768]{1,0:T(8,128)(2,1)S(1)}, bf16[80,768]{1,0:T(8,128)(2,1)S(1)}, u32[]{:S(2)}, u32[]{:S(2)}) collective-permute-start(bf16[80,768]{1,0:T(8,128)(2,1)S(1)} %get-tuple-element.91), channel_id=1, source_target_pairs={{0,37},{1,36},{2,39},{3,38},{4,33},{5,32},{6,35},{7,34},{8,45},{9,... | collective-permute-start | bytes 368648 | tf_op jit(solution)/shard_map/ppermute | solution.py:382

commit v7 on v6

--- a/solution.py
+++ b/solution.py
@@ -161,7 +161,8 @@
         for start in range(0, ref.shape[0], step):
             end = start + count * block_keys
             first = len(id_rows) * block_keys
-            store[first : first + count * block_keys, :] = ref[start:end, :]
+            if store is not None:
+                store[first : first + count * block_keys, :] = ref[start:end, :]
             ids = ref[end : end + 8 * count, 0:256].astype(f32)[0:8]
             id_rows += [ids, pltpu.roll(ids, 7, 0)][:count]
     return id_rows
@@ -175,17 +176,20 @@
     return jnp.concatenate(pieces, axis=1)[0:1]
 
 
-def flash_kernel(wides, first, owns, finish, *refs):
+def flash_kernel(wides, first, owns, finish, given, *refs):
     refs = list(refs)
     count = len(owns)
     q_refs = [[refs.pop(0), refs.pop(0)] for _ in range(count)]
     key_refs = [refs.pop(0) for _ in wides]
+    keys = refs.pop(0) if given else None
     states = None if first else [[refs.pop(0) for _ in range(3)] for _ in range(count)]
     outs = [[refs.pop(0)] if finish else [refs.pop(0) for _ in range(3)] for _ in range(count)]
-    keys, queries, labels = refs
+    if not given:
+        keys = refs.pop(0)
+    queries, labels = refs
     width = q_refs[0][0].shape[1]
     scale = score_scale / math.sqrt(width) * log2e
-    key_id = side_by_side(gather_rows(key_refs, wides, keys))
+    key_id = side_by_side(gather_rows(key_refs, wides, None if given else keys))
     other = jnp.where(key_id == 0.0, masked, -penalty * log2e)
     for n in range(count):
         wide_ids = q_refs[n][0][2 * block_keys : big_rows, 0:256].astype(f32)
@@ -245,7 +249,7 @@
             outs[n][0][rows : rows + 16, :] = tails.astype(bf16)
 
 
-def flash(qs, owns, key_arrays, states, finish):
+def flash(qs, owns, key_arrays, states, finish, gathered=None):
     width = qs[0][0].shape[1]
     wides = [wide for _, wide in key_arrays]
     key_arrays = [a for a, _ in key_arrays]
@@ -265,14 +269,15 @@
             jax.ShapeDtypeStruct((rows, width), f32),
         ]
     count = len(qs)
-    args = [a for q in qs for a in q] + key_arrays + ([] if first else [a for state in states for a in state])
+    given = gathered is not None
+    args = [a for q in qs for a in q] + key_arrays + ([gathered] if given else []) + ([] if first else [a for state in states for a in state])
     out = pl.pallas_call(
-        functools.partial(flash_kernel, wides, first, owns, finish),
-        out_shape=each * count,
+        functools.partial(flash_kernel, wides, first, owns, finish, given),
+        out_shape=each * count + ([jax.ShapeDtypeStruct((total, width), bf16)] if finish else []),
         in_specs=vmem_specs(len(args)),
-        out_specs=vmem_specs(len(each) * count),
-        scratch_shapes=[
-            pltpu.VMEM((total, width), bf16),
+        out_specs=vmem_specs(len(each) * count + finish),
+        scratch_shapes=([] if finish or given else [pltpu.VMEM((total, width), bf16)])
+        + [
             pltpu.VMEM((8, 128), bf16),
             pltpu.VMEM((count, rows, 1), f32),
         ],
@@ -425,8 +430,8 @@
     big3, small3 = send(big1, wide[2]), send(small1, narrow[2])
     states = flash(queries, owns, pairs(big1, small1), states, False)
     states = flash(queries, owns, pairs(big2, small2), states, False)
-    (partial,) = flash(queries[:1], owns[:1], pairs(big3, small3), states[:1], True)
-    (mine,) = flash(queries[1:], owns[1:], pairs(big3, small3), states[1:], False)
+    partial, gathered = flash(queries[:1], owns[:1], pairs(big3, small3), states[:1], True)
+    (mine,) = flash(queries[1:], owns[1:], pairs(big3, small3), states[1:], False, gathered)
     theirs = send(partial, swap)
     answers = pl.pallas_call(
         combine_kernel,

time: 103 us -> 103 us (level)
  no operation moved by 1% of the time
where the time goes in v7:
time: 103 us; the launch traced here: 101 us
  starting transfers between devices  38.8 us (38%)
  Pallas kernels  31.3 us (30%)
  waiting for transfers between devices  29.8 us (29%)
    ppermute x25, starting transfers between devices, per_device(): send = lambda a, pairs: lax.ppermute(a, axes, pairs)  38.8 us
    ppermute x25, waiting for transfers between devices, per_device(): send = lambda a, pairs: lax.ppermute(a, axes, pairs)  29.8 us
    pallas_call x6, Pallas kernels, flash(): pl.pallas_call(functools.partial(flash_kernel, wides, first, owns, finish...  25.6 us
    pallas_call x1, Pallas kernels, per_device(): pl.pallas_call(place_kernel, out_shape=[packet] * 8, in_specs=[smem] + [p...  2.46 us
  transfers between devices with their start and end apart: 25, of which 13 were waited for; matrix products, arithmetic and copies ran while one was open for 0% of the time, Pallas kernels for 23%

profile of v7, /device:TPU:1, one launch (start us, length us, event | category | flops | bytes accessed | tf_op | source)
XLA Modules:
  0.0 101.1 jit_solution(16797701998656865421)
XLA Ops:
  0.8 2.5 %place.1 = (bf16[80,768]{1,0:T(8,128)(2,1)S(1)}, bf16[80,768]{1,0:T(8,128)(2,1)S(1)}, bf16[80,768]{1,0:T(8,128)(2,1)S(1)}, bf16[80,768]{1,0:T(8,128)(2,1)S(1)}, ...) custom-call(s32[1]{0:T(128)} %bitcast.me_ref, ...), custom_call_target="tpu_custom_call" | custom-call | tf_op jit(solution)/shard_map/place/pallas_call | solution.py:394
  3.2 3.5 %collective-permute-start.4 = (bf16[80,768]{1,0:T(8,128)(2,1)S(1)}, bf16[80,768]{1,0:T(8,128)(2,1)S(1)}, u32[]{:S(2)}, u32[]{:S(2)}) collective-permute-start(bf16[80,768]{1,0:T(8,128)(2,1)S(1)} %get-tuple-element.57), channel_id=1, source_target_pairs={{0,5},{1,4},{2,7},{3,6},{4,1},{5,0},{6,3},{7,2},{8,13},{9,12},{10,... | collective-permute-start | bytes 368648 | tf_op jit(solution)/shard_map/ppermute | solution.py:387
  7.0 1.3 %collective-permute-start.1 = (bf16[80,768]{1,0:T(8,128)(2,1)S(1)}, bf16[80,768]{1,0:T(8,128)(2,1)S(1)}, u32[]{:S(2)}, u32[]{:S(2)}) collective-permute-start(bf16[80,768]{1,0:T(8,128)(2,1)S(1)} %get-tuple-element.54), channel_id=1, source_target_pairs={{0,32},{1,33},{2,34},{3,35},{4,36},{5,37},{6,38},{7,39},{8,40},{9,... | collective-permute-start | bytes 368648 | tf_op jit(solution)/shard_map/ppermute | solution.py:387
  8.4 1.0 collective-permute-start.3
  9.8 2.6 %collective-permute-done.refs_1_ = bf16[80,768]{1,0:T(8,128)(2,1)S(1)} collective-permute-done((bf16[80,768]{1,0:T(8,128)(2,1)S(1)}, bf16[80,768]{1,0:T(8,128)(2,1)S(1)}, u32[]{:S(2)}, u32[]{:S(2)}) %collective-permute-start) | collective-permute-done | bytes 122912 | tf_op jit(solution)/shard_map/ppermute | solution.py:387
  12.5 3.4 %collective-permute-done.3.refs_4_ = bf16[80,768]{1,0:T(8,128)(2,1)S(1)} collective-permute-done((bf16[80,768]{1,0:T(8,128)(2,1)S(1)}, bf16[80,768]{1,0:T(8,128)(2,1)S(1)}, u32[]{:S(2)}, u32[]{:S(2)}) %collective-permute-start.3) | collective-permute-done | bytes 122912 | tf_op jit(solution)/shard_map/ppermute | solution.py:387
  16.0 2.0 %collective-permute-start.7 = (bf16[400,768]{1,0:T(8,128)(2,1)S(1)}, bf16[400,768]{1,0:T(8,128)(2,1)S(1)}, u32[]{:S(2)}, u32[]{:S(2)}) collective-permute-start(bf16[400,768]{1,0:T(8,128)(2,1)S(1)} %pack.2.refs_0_.refs_2_), channel_id=1, source_target_pairs={{0,12},{1,13},{2,14},{3,15},{4,8},{5,9},{6,10},{7,11},{8,4},{9,5},... | collective-permute-start | bytes 1843208 | tf_op jit(solution)/shard_map/ppermute | solution.py:387
  18.2 3.1 %collective-permute-start.6 = (bf16[80,768]{1,0:T(8,128)(2,1)S(1)}, bf16[80,768]{1,0:T(8,128)(2,1)S(1)}, u32[]{:S(2)}, u32[]{:S(2)}) collective-permute-start(bf16[80,768]{1,0:T(8,128)(2,1)S(1)} %get-tuple-element.59), channel_id=1, source_target_pairs={{0,37},{1,36},{2,39},{3,38},{4,33},{5,32},{6,35},{7,34},{8,45},{9,... | collective-permute-start | bytes 368648 | tf_op jit(solution)/shard_map/ppermute | solution.py:387
  21.3 3.0 %collective-permute-done.5.refs_1_ = bf16[80,768]{1,0:T(8,128)(2,1)S(1)} collective-permute-done((bf16[80,768]{1,0:T(8,128)(2,1)S(1)}, bf16[80,768]{1,0:T(8,128)(2,1)S(1)}, u32[]{:S(2)}, u32[]{:S(2)}) %collective-permute-start.5) | collective-permute-done | bytes 122912 | tf_op jit(solution)/shard_map/ppermute | solution.py:387
  24.3 3.2 %collective-permute-start.10 = (bf16[200,768]{1,0:T(8,128)(2,1)S(1)}, bf16[200,768]{1,0:T(8,128)(2,1)S(1)}, u32[]{:S(2)}, u32[]{:S(2)}) collective-permute-start(bf16[200,768]{1,0:T(8,128)(2,1)S(1)} %pack.3.refs_1_.refs_3_), channel_id=1, source_target_pairs={{0,3},{1,2},{2,1},{3,0},{4,7},{5,6},{6,5},{7,4},{8,11},{9,10},{10,... | collective-permute-start | bytes 921608 | tf_op jit(solution)/shard_map/ppermute | solution.py:387
  27.5 1.5 %collective-permute-start.8 = (bf16[800,768]{1,0:T(8,128)(2,1)S(1)}, bf16[800,768]{1,0:T(8,128)(2,1)S(1)}, u32[]{:S(2)}, u32[]{:S(2)}) collective-permute-start(bf16[800,768]{1,0:T(8,128)(2,1)S(1)} %pad_maximum_fusion), channel_id=1, source_target_pairs={{0,96},{1,97},{2,98},{3,99},{4,100},{5,101},{6,102},{7,103},{8,104... | collective-permute-start | bytes 3686408 | tf_op jit(solution)/shard_map/ppermute | solution.py:387
  29.0 5.4 %collective-permute-start.13 = (bf16[400,768]{1,0:T(8,128)(2,1)S(1)}, bf16[400,768]{1,0:T(8,128)(2,1)S(1)}, u32[]{:S(2)}, u32[]{:S(2)}) collective-permute-start(bf16[400,768]{1,0:T(8,128)(2,1)S(1)} %pack.2.refs_0_.refs_2_), channel_id=1, source_target_pairs={{0,16},{1,17},{2,18},{3,19},{4,20},{5,21},{6,22},{7,23},{8,24},{9,... | collective-permute-start | bytes 1843208 | tf_op jit(solution)/shard_map/ppermute | solution.py:387
  34.5 3.6 %collective-permute-start.11 = (bf16[400,768]{1,0:T(8,128)(2,1)S(1)}, bf16[400,768]{1,0:T(8,128)(2,1)S(1)}, u32[]{:S(2)}, u32[]{:S(2)}) collective-permute-start(bf16[400,768]{1,0:T(8,128)(2,1)S(1)} %pad_maximum_fusion.1), channel_id=1, source_target_pairs={{0,12},{1,13},{2,14},{3,15},{4,8},{5,9},{6,10},{7,11},{8,4},{9,5},... | collective-permute-start | bytes 1843208 | tf_op jit(solution)/shard_map/ppermute | solution.py:387
  38.1 3.2 %flash.6 = (f32[576,1]{1,0:T(8,128)S(1)}, f32[576,1]{1,0:T(8,128)S(1)}, f32[576,768]{1,0:T(8,128)S(1)}) custom-call(bf16[400,768]{1,0:T(8,128)(2,1)S(1)} %pack.2.refs_0_.refs_2_, bf16[200,768]{1,0:T(8,128)(2,1)S(1)} %pack.3.refs_1_.refs_3_, bf16[400,768]{1,0:T(8,128)(2,1)S(1)} %pack.2.refs_0_.refs_2_, bf16[200,768]{1,0:T(8,128)(2,1)S(1)} %pack.3.refs_1_.refs_3_, ...), custom_call_target="tpu_custom_call" | custom-call | flops 4076863488 | bytes 4423680 | tf_op jit(solution)/shard_map/flash/pallas_call | solution.py:274
  41.5 3.1 %flash.7 = (f32[576,1]{1,0:T(8,128)S(1)}, f32[576,1]{1,0:T(8,128)S(1)}, f32[576,768]{1,0:T(8,128)S(1)}) custom-call(bf16[400,768]{1,0:T(8,128)(2,1)S(1)} %collective-permute-done.13.refs_0_, bf16[200,768]{1,0:T(8,128)(2,1)S(1)} %collective-permute-done.14.refs_1_, bf16[400,768]{1,0:T(8,128)(2,1)S(1)} %pack.2.refs_0_.refs_2_, ...), custom_call_target="tpu_custom_call" | custom-call | flops 4076863488 | bytes 4423680 | tf_op jit(solution)/shard_map/flash/pallas_call | solution.py:274
  44.6 3.3 %collective-permute-done.11.refs_5_ = bf16[400,768]{1,0:T(8,128)(2,1)S(1)} collective-permute-done((bf16[400,768]{1,0:T(8,128)(2,1)S(1)}, bf16[400,768]{1,0:T(8,128)(2,1)S(1)}, u32[]{:S(2)}, u32[]{:S(2)}) %collective-permute-start.11) | collective-permute-done | bytes 614432 | tf_op jit(solution)/shard_map/ppermute | solution.py:387
  48.4 6.5 %collective-permute-start.9 = (bf16[800,768]{1,0:T(8,128)(2,1)S(1)}, bf16[800,768]{1,0:T(8,128)(2,1)S(1)}, u32[]{:S(2)}, u32[]{:S(2)}) collective-permute-start(bf16[800,768]{1,0:T(8,128)(2,1)S(1)} %collective-permute-done.8.refs_4_), channel_id=1, source_target_pairs={{0,3},{1,2},{2,1},{3,0},{4,7},{5,6},{6,5},{7,4},{8,11},{9,10},{10,... | collective-permute-start | bytes 3686408 | tf_op jit(solution)/shard_map/ppermute | solution.py:387
  55.0 6.3 %flash.8 = (f32[576,1]{1,0:T(8,128)S(1)}, f32[576,1]{1,0:T(8,128)S(1)}, f32[576,768]{1,0:T(8,128)S(1)}, f32[576,1]{1,0:T(8,128)S(1)}, f32[576,1]{1,0:T(8,128)S(1)}, /*index=5*/f32[576,768]{1,0:T(8,128)S(1)}) custom-call(bf16[400,768]{1,0:T(8,128)(2,1)S(1)} %collective-permute-done.13.refs_0_, bf16[200,768]{1,0:T(8,128)(2,1)S(1)} %collective-permute-done.14.refs_1_, ...), custom_call_target="tpu_custom_call" | custom-call | flops 8153726976 | bytes 7077888 | tf_op jit(solution)/shard_map/flash/pallas_call | solution.py:274
  61.3 4.4 %collective-permute-done.15.refs_4_ = bf16[800,768]{1,0:T(8,128)(2,1)S(1)} collective-permute-done((bf16[800,768]{1,0:T(8,128)(2,1)S(1)}, bf16[800,768]{1,0:T(8,128)(2,1)S(1)}, u32[]{:S(2)}, u32[]{:S(2)}) %collective-permute-start.15) | collective-permute-done | bytes 1228832 | tf_op jit(solution)/shard_map/ppermute | solution.py:387
  65.7 6.2 %flash.9 = (f32[576,1]{1,0:T(8,128)S(1)}, f32[576,1]{1,0:T(8,128)S(1)}, f32[576,768]{1,0:T(8,128)S(1)}, f32[576,1]{1,0:T(8,128)S(1)}, f32[576,1]{1,0:T(8,128)S(1)}, /*index=5*/f32[576,768]{1,0:T(8,128)S(1)}) custom-call(bf16[400,768]{1,0:T(8,128)(2,1)S(1)} %collective-permute-done.13.refs_0_, bf16[200,768]{1,0:T(8,128)(2,1)S(1)} %collective-permute-done.14.refs_1_, ...), custom_call_target="tpu_custom_call" | custom-call | flops 8153726976 | bytes 7077888 | tf_op jit(solution)/shard_map/flash/pallas_call | solution.py:274
  71.9 6.6 %collective-permute-done.9.refs_2_ = bf16[800,768]{1,0:T(8,128)(2,1)S(1)} collective-permute-done((bf16[800,768]{1,0:T(8,128)(2,1)S(1)}, bf16[800,768]{1,0:T(8,128)(2,1)S(1)}, u32[]{:S(2)}, u32[]{:S(2)}) %collective-permute-start.9) | collective-permute-done | bytes 1228832 | tf_op jit(solution)/shard_map/ppermute | solution.py:387
  78.5 3.5 %flash.10 = (bf16[592,768]{1,0:T(8,128)(2,1)S(1)}, bf16[1152,768]{1,0:T(8,128)(2,1)S(1)}) custom-call(bf16[400,768]{1,0:T(8,128)(2,1)S(1)} %collective-permute-done.13.refs_0_, bf16[200,768]{1,0:T(8,128)(2,1)S(1)} %collective-permute-done.14.refs_1_, bf16[800,768]{1,0:T(8,128)(2,1)S(1)} %collective-permute-done.9.refs_2_, ...), custom_call_target="tpu_custom_call" | custom-call | flops 4076863488 | bytes 4423680 | tf_op jit(solution)/shard_map/flash/pallas_call | solution.py:274
  82.1 3.3 %flash.11 = (f32[576,1]{1,0:T(8,128)S(1)}, f32[576,1]{1,0:T(8,128)S(1)}, f32[576,768]{1,0:T(8,128)S(1)}) custom-call(bf16[400,768]{1,0:T(8,128)(2,1)S(1)} %pack.2.refs_0_.refs_2_, bf16[200,768]{1,0:T(8,128)(2,1)S(1)} %pack.3.refs_1_.refs_3_, bf16[800,768]{1,0:T(8,128)(2,1)S(1)} %collective-permute-done.9.refs_2_, ...), custom_call_target="tpu_custom_call" | custom-call | flops 4076863488 | bytes 4423680 | tf_op jit(solution)/shard_map/flash/pallas_call | solution.py:274
  85.5 0.8 combine.1
  86.4 1.1 %collective-permute-start.19 = (bf16[80,768]{1,0:T(8,128)(2,1)S(1)}, bf16[80,768]{1,0:T(8,128)(2,1)S(1)}, u32[]{:S(2)}, u32[]{:S(2)}) collective-permute-start(bf16[80,768]{1,0:T(8,128)(2,1)S(1)} %get-tuple-element.90), channel_id=1, source_target_pairs={{0,32},{1,33},{2,34},{3,35},{4,36},{5,37},{6,38},{7,39},{8,40},{9,... | collective-permute-start | bytes 368648 | tf_op jit(solution)/shard_map/ppermute | solution.py:387
  88.1 1.6 %collective-permute-start.21 = (bf16[80,768]{1,0:T(8,128)(2,1)S(1)}, bf16[80,768]{1,0:T(8,128)(2,1)S(1)}, u32[]{:S(2)}, u32[]{:S(2)}) collective-permute-start(bf16[80,768]{1,0:T(8,128)(2,1)S(1)} %get-tuple-element.92), channel_id=1, source_target_pairs={{0,36},{1,37},{2,38},{3,39},{4,32},{5,33},{6,34},{7,35},{8,44},{9,... | collective-permute-start | bytes 368648 | tf_op jit(solution)/shard_map/ppermute | solution.py:387
  90.7 1.4 %collective-permute-start.23 = (bf16[80,768]{1,0:T(8,128)(2,1)S(1)}, bf16[80,768]{1,0:T(8,128)(2,1)S(1)}, u32[]{:S(2)}, u32[]{:S(2)}) collective-permute-start(bf16[80,768]{1,0:T(8,128)(2,1)S(1)} %get-tuple-element.94), channel_id=1, source_target_pairs={{0,33},{1,32},{2,35},{3,34},{4,37},{5,36},{6,39},{7,38},{8,41},{9,... | collective-permute-start | bytes 368648 | tf_op jit(solution)/shard_map/ppermute | solution.py:387
  92.1 1.6 %collective-permute-start.24 = (bf16[80,768]{1,0:T(8,128)(2,1)S(1)}, bf16[80,768]{1,0:T(8,128)(2,1)S(1)}, u32[]{:S(2)}, u32[]{:S(2)}) collective-permute-start(bf16[80,768]{1,0:T(8,128)(2,1)S(1)} %get-tuple-element.95), channel_id=1, source_target_pairs={{0,37},{1,36},{2,39},{3,38},{4,33},{5,32},{6,35},{7,34},{8,45},{9,... | collective-permute-start | bytes 368648 | tf_op jit(solution)/shard_map/ppermute | solution.py:387
  93.7 1.0 choose.1
  94.7 1.4 %collective-permute-done.22.refs_5_ = bf16[80,768]{1,0:T(8,128)(2,1)S(1)} collective-permute-done((bf16[80,768]{1,0:T(8,128)(2,1)S(1)}, bf16[80,768]{1,0:T(8,128)(2,1)S(1)}, u32[]{:S(2)}, u32[]{:S(2)}) %collective-permute-start.22) | collective-permute-done | bytes 122912 | tf_op jit(solution)/shard_map/ppermute | solution.py:387
  96.8 2.9 %collective-permute-done.24.refs_7_ = bf16[80,768]{1,0:T(8,128)(2,1)S(1)} collective-permute-done((bf16[80,768]{1,0:T(8,128)(2,1)S(1)}, bf16[80,768]{1,0:T(8,128)(2,1)S(1)}, u32[]{:S(2)}, u32[]{:S(2)}) %collective-permute-start.24) | collective-permute-done | bytes 122912 | tf_op jit(solution)/shard_map/ppermute | solution.py:387
  99.6 1.5 %final.1 = (bf16[384,768]{1,0:T(8,128)(2,1)}, f32[384]{0:T(512)}) custom-call(bf16[384,640]{1,0:T(8,128)(2,1)S(1)} %get-tuple-element.49.choice_ref, bf16[256,384]{1,0:T(8,128)(2,1)S(1)} %get-tuple-element.50.lanes_ref, f32[64,384]{1,0:T(8,128)S(1)} %get-tuple-element.51.chosen_ref, bf16[80,768]{1,0:T(8,128)(2,1)S(1)} %get-tuple-element.88.refs_0_, ...), custom_call_target="tpu_custom_call" | custom-call | tf_op jit(solution)/shard_map/final/pallas_call | solution.py:457
  (36 shorter events, 4.6 us)
Async XLA Ops:
  3.2 6.5 %collective-permute-start.4 = (bf16[80,768]{1,0:T(8,128)(2,1)S(1)}, bf16[80,768]{1,0:T(8,128)(2,1)S(1)}, u32[]{:S(2)}, u32[]{:S(2)}) collective-permute-start(bf16[80,768]{1,0:T(8,128)(2,1)S(1)} %get-tuple-element.57), channel_id=1, source_target_pairs={{0,5},{1,4},{2,7},{3,6},{4,1},{5,0},{6,3},{7,2},{8,13},{9,12},{10,... | collective-permute-start | bytes 368648 | tf_op jit(solution)/shard_map/ppermute | solution.py:387
  6.7 5.6 %collective-permute-start = (bf16[80,768]{1,0:T(8,128)(2,1)S(1)}, bf16[80,768]{1,0:T(8,128)(2,1)S(1)}, u32[]{:S(2)}, u32[]{:S(2)}) collective-permute-start(bf16[80,768]{1,0:T(8,128)(2,1)S(1)} %get-tuple-element.53), channel_id=1, source_target_pairs={{0,4},{1,5},{2,6},{3,7},{4,0},{5,1},{6,2},{7,3},{8,12},{9,13},{10,... | collective-permute-start | bytes 368648 | tf_op jit(solution)/shard_map/ppermute | solution.py:387
  7.0 5.4 %collective-permute-start.1 = (bf16[80,768]{1,0:T(8,128)(2,1)S(1)}, bf16[80,768]{1,0:T(8,128)(2,1)S(1)}, u32[]{:S(2)}, u32[]{:S(2)}) collective-permute-start(bf16[80,768]{1,0:T(8,128)(2,1)S(1)} %get-tuple-element.54), channel_id=1, source_target_pairs={{0,32},{1,33},{2,34},{3,35},{4,36},{5,37},{6,38},{7,39},{8,40},{9,... | collective-permute-start | bytes 368648 | tf_op jit(solution)/shard_map/ppermute | solution.py:387
  8.3 4.3 %collective-permute-start.2 = (bf16[80,768]{1,0:T(8,128)(2,1)S(1)}, bf16[80,768]{1,0:T(8,128)(2,1)S(1)}, u32[]{:S(2)}, u32[]{:S(2)}) collective-permute-start(bf16[80,768]{1,0:T(8,128)(2,1)S(1)} %get-tuple-element.55), channel_id=1, source_target_pairs={{0,1},{1,0},{2,3},{3,2},{4,5},{5,4},{6,7},{7,6},{8,9},{9,8},{10,11... | collective-permute-start | bytes 368648 | tf_op jit(solution)/shard_map/ppermute | solution.py:387
  8.4 7.6 %collective-permute-start.3 = (bf16[80,768]{1,0:T(8,128)(2,1)S(1)}, bf16[80,768]{1,0:T(8,128)(2,1)S(1)}, u32[]{:S(2)}, u32[]{:S(2)}) collective-permute-start(bf16[80,768]{1,0:T(8,128)(2,1)S(1)} %get-tuple-element.56), channel_id=1, source_target_pairs={{0,36},{1,37},{2,38},{3,39},{4,32},{5,33},{6,34},{7,35},{8,44},{9,... | collective-permute-start | bytes 368648 | tf_op jit(solution)/shard_map/ppermute | solution.py:387
  16.0 11.4 %collective-permute-start.7 = (bf16[400,768]{1,0:T(8,128)(2,1)S(1)}, bf16[400,768]{1,0:T(8,128)(2,1)S(1)}, u32[]{:S(2)}, u32[]{:S(2)}) collective-permute-start(bf16[400,768]{1,0:T(8,128)(2,1)S(1)} %pack.2.refs_0_.refs_2_), channel_id=1, source_target_pairs={{0,12},{1,13},{2,14},{3,15},{4,8},{5,9},{6,10},{7,11},{8,4},{9,5},... | collective-permute-start | bytes 1843208 | tf_op jit(solution)/shard_map/ppermute | solution.py:387
  18.0 6.2 %collective-permute-start.5 = (bf16[80,768]{1,0:T(8,128)(2,1)S(1)}, bf16[80,768]{1,0:T(8,128)(2,1)S(1)}, u32[]{:S(2)}, u32[]{:S(2)}) collective-permute-start(bf16[80,768]{1,0:T(8,128)(2,1)S(1)} %get-tuple-element.58), channel_id=1, source_target_pairs={{0,33},{1,32},{2,35},{3,34},{4,37},{5,36},{6,39},{7,38},{8,41},{9,... | collective-permute-start | bytes 368648 | tf_op jit(solution)/shard_map/ppermute | solution.py:387
  18.2 6.1 %collective-permute-start.6 = (bf16[80,768]{1,0:T(8,128)(2,1)S(1)}, bf16[80,768]{1,0:T(8,128)(2,1)S(1)}, u32[]{:S(2)}, u32[]{:S(2)}) collective-permute-start(bf16[80,768]{1,0:T(8,128)(2,1)S(1)} %get-tuple-element.59), channel_id=1, source_target_pairs={{0,37},{1,36},{2,39},{3,38},{4,33},{5,32},{6,35},{7,34},{8,45},{9,... | collective-permute-start | bytes 368648 | tf_op jit(solution)/shard_map/ppermute | solution.py:387
  24.3 10.1 %collective-permute-start.10 = (bf16[200,768]{1,0:T(8,128)(2,1)S(1)}, bf16[200,768]{1,0:T(8,128)(2,1)S(1)}, u32[]{:S(2)}, u32[]{:S(2)}) collective-permute-start(bf16[200,768]{1,0:T(8,128)(2,1)S(1)} %pack.3.refs_1_.refs_3_), channel_id=1, source_target_pairs={{0,3},{1,2},{2,1},{3,0},{4,7},{5,6},{6,5},{7,4},{8,11},{9,10},{10,... | collective-permute-start | bytes 921608 | tf_op jit(solution)/shard_map/ppermute | solution.py:387
  27.5 20.9 %collective-permute-start.8 = (bf16[800,768]{1,0:T(8,128)(2,1)S(1)}, bf16[800,768]{1,0:T(8,128)(2,1)S(1)}, u32[]{:S(2)}, u32[]{:S(2)}) collective-permute-start(bf16[800,768]{1,0:T(8,128)(2,1)S(1)} %pad_maximum_fusion), channel_id=1, source_target_pairs={{0,96},{1,97},{2,98},{3,99},{4,100},{5,101},{6,102},{7,103},{8,104... | collective-permute-start | bytes 3686408 | tf_op jit(solution)/shard_map/ppermute | solution.py:387
  29.0 12.4 %collective-permute-start.13 = (bf16[400,768]{1,0:T(8,128)(2,1)S(1)}, bf16[400,768]{1,0:T(8,128)(2,1)S(1)}, u32[]{:S(2)}, u32[]{:S(2)}) collective-permute-start(bf16[400,768]{1,0:T(8,128)(2,1)S(1)} %pack.2.refs_0_.refs_2_), channel_id=1, source_target_pairs={{0,16},{1,17},{2,18},{3,19},{4,20},{5,21},{6,22},{7,23},{8,24},{9,... | collective-permute-start | bytes 1843208 | tf_op jit(solution)/shard_map/ppermute | solution.py:387
  34.4 6.9 %collective-permute-start.14 = (bf16[200,768]{1,0:T(8,128)(2,1)S(1)}, bf16[200,768]{1,0:T(8,128)(2,1)S(1)}, u32[]{:S(2)}, u32[]{:S(2)}) collective-permute-start(bf16[200,768]{1,0:T(8,128)(2,1)S(1)} %pack.3.refs_1_.refs_3_), channel_id=1, source_target_pairs={{0,16},{1,17},{2,18},{3,19},{4,20},{5,21},{6,22},{7,23},{8,24},{9,... | collective-permute-start | bytes 921608 | tf_op jit(solution)/shard_map/ppermute | solution.py:387
  34.5 13.4 %collective-permute-start.11 = (bf16[400,768]{1,0:T(8,128)(2,1)S(1)}, bf16[400,768]{1,0:T(8,128)(2,1)S(1)}, u32[]{:S(2)}, u32[]{:S(2)}) collective-permute-start(bf16[400,768]{1,0:T(8,128)(2,1)S(1)} %pad_maximum_fusion.1), channel_id=1, source_target_pairs={{0,12},{1,13},{2,14},{3,15},{4,8},{5,9},{6,10},{7,11},{8,4},{9,5},... | collective-permute-start | bytes 1843208 | tf_op jit(solution)/shard_map/ppermute | solution.py:387
  41.3 24.4 %collective-permute-start.15 = (bf16[800,768]{1,0:T(8,128)(2,1)S(1)}, bf16[800,768]{1,0:T(8,128)(2,1)S(1)}, u32[]{:S(2)}, u32[]{:S(2)}) collective-permute-start(bf16[800,768]{1,0:T(8,128)(2,1)S(1)} %pad_maximum_fusion), channel_id=1, source_target_pairs={{0,3},{1,2},{2,1},{3,0},{4,7},{5,6},{6,5},{7,4},{8,11},{9,10},{10,... | collective-permute-start | bytes 3686408 | tf_op jit(solution)/shard_map/ppermute | solution.py:387
  41.4 19.9 %collective-permute-start.16 = (bf16[400,768]{1,0:T(8,128)(2,1)S(1)}, bf16[400,768]{1,0:T(8,128)(2,1)S(1)}, u32[]{:S(2)}, u32[]{:S(2)}) collective-permute-start(bf16[400,768]{1,0:T(8,128)(2,1)S(1)} %pad_maximum_fusion.1), channel_id=1, source_target_pairs={{0,96},{1,97},{2,98},{3,99},{4,100},{5,101},{6,102},{7,103},{8,104... | collective-permute-start | bytes 1843208 | tf_op jit(solution)/shard_map/ppermute | solution.py:387
  47.9 24.0 %collective-permute-start.12 = (bf16[400,768]{1,0:T(8,128)(2,1)S(1)}, bf16[400,768]{1,0:T(8,128)(2,1)S(1)}, u32[]{:S(2)}, u32[]{:S(2)}) collective-permute-start(bf16[400,768]{1,0:T(8,128)(2,1)S(1)} %collective-permute-done.11.refs_5_), channel_id=1, source_target_pairs={{0,96},{1,97},{2,98},{3,99},{4,100},{5,101},{6,102},{7,103},{8,104... | collective-permute-start | bytes 1843208 | tf_op jit(solution)/shard_map/ppermute | solution.py:387
  48.4 30.1 %collective-permute-start.9 = (bf16[800,768]{1,0:T(8,128)(2,1)S(1)}, bf16[800,768]{1,0:T(8,128)(2,1)S(1)}, u32[]{:S(2)}, u32[]{:S(2)}) collective-permute-start(bf16[800,768]{1,0:T(8,128)(2,1)S(1)} %collective-permute-done.8.refs_4_), channel_id=1, source_target_pairs={{0,3},{1,2},{2,1},{3,0},{4,7},{5,6},{6,5},{7,4},{8,11},{9,10},{10,... | collective-permute-start | bytes 3686408 | tf_op jit(solution)/shard_map/ppermute | solution.py:387
  82.0 3.4 %collective-permute-start.17 = (bf16[592,768]{1,0:T(8,128)(2,1)S(1)}, bf16[592,768]{1,0:T(8,128)(2,1)S(1)}, u32[]{:S(2)}, u32[]{:S(2)}) collective-permute-start(bf16[592,768]{1,0:T(8,128)(2,1)S(1)} %get-tuple-element.87), channel_id=1, source_target_pairs={{0,16},{1,17},{2,18},{3,19},{4,20},{5,21},{6,22},{7,23},{8,24},{9,... | collective-permute-start | bytes 2727944 | tf_op jit(solution)/shard_map/ppermute | solution.py:387
  85.5 8.3 %copy-start = (s32[384]{0:T(512)S(1)}, s32[384]{0:T(512)}, u32[]{:S(2)}) copy-start(s32[384]{0:T(512)} %clusters_hbm.1) | copy-start | bytes 4612
  85.5 8.3 %copy-start.1 = (s32[32]{0:T(128)S(1)}, s32[32]{0:T(128)}, u32[]{:S(2)}) copy-start(s32[32]{0:T(128)} %owner_hbm.1) | copy-start | bytes 388
  86.3 4.5 %collective-permute-start.18 = (bf16[80,768]{1,0:T(8,128)(2,1)S(1)}, bf16[80,768]{1,0:T(8,128)(2,1)S(1)}, u32[]{:S(2)}, u32[]{:S(2)}) collective-permute-start(bf16[80,768]{1,0:T(8,128)(2,1)S(1)} %get-tuple-element.89), channel_id=1, source_target_pairs={{0,4},{1,5},{2,6},{3,7},{4,0},{5,1},{6,2},{7,3},{8,12},{9,13},{10,... | collective-permute-start | bytes 368648 | tf_op jit(solution)/shard_map/ppermute | solution.py:387
  86.4 5.7 %collective-permute-start.19 = (bf16[80,768]{1,0:T(8,128)(2,1)S(1)}, bf16[80,768]{1,0:T(8,128)(2,1)S(1)}, u32[]{:S(2)}, u32[]{:S(2)}) collective-permute-start(bf16[80,768]{1,0:T(8,128)(2,1)S(1)} %get-tuple-element.90), channel_id=1, source_target_pairs={{0,32},{1,33},{2,34},{3,35},{4,36},{5,37},{6,38},{7,39},{8,40},{9,... | collective-permute-start | bytes 368648 | tf_op jit(solution)/shard_map/ppermute | solution.py:387
  87.5 7.3 %collective-permute-start.20 = (bf16[80,768]{1,0:T(8,128)(2,1)S(1)}, bf16[80,768]{1,0:T(8,128)(2,1)S(1)}, u32[]{:S(2)}, u32[]{:S(2)}) collective-permute-start(bf16[80,768]{1,0:T(8,128)(2,1)S(1)} %get-tuple-element.91), channel_id=1, source_target_pairs={{0,1},{1,0},{2,3},{3,2},{4,5},{5,4},{6,7},{7,6},{8,9},{9,8},{10,11... | collective-permute-start | bytes 368648 | tf_op jit(solution)/shard_map/ppermute | solution.py:387
  88.1 6.7 %collective-permute-start.21 = (bf16[80,768]{1,0:T(8,128)(2,1)S(1)}, bf16[80,768]{1,0:T(8,128)(2,1)S(1)}, u32[]{:S(2)}, u32[]{:S(2)}) collective-permute-start(bf16[80,768]{1,0:T(8,128)(2,1)S(1)} %get-tuple-element.92), channel_id=1, source_target_pairs={{0,36},{1,37},{2,38},{3,39},{4,32},{5,33},{6,34},{7,35},{8,44},{9,... | collective-permute-start | bytes 368648 | tf_op jit(solution)/shard_map/ppermute | solution.py:387
  89.6 6.5 %collective-permute-start.22 = (bf16[80,768]{1,0:T(8,128)(2,1)S(1)}, bf16[80,768]{1,0:T(8,128)(2,1)S(1)}, u32[]{:S(2)}, u32[]{:S(2)}) collective-permute-start(bf16[80,768]{1,0:T(8,128)(2,1)S(1)} %get-tuple-element.93), channel_id=1, source_target_pairs={{0,5},{1,4},{2,7},{3,6},{4,1},{5,0},{6,3},{7,2},{8,13},{9,12},{10,... | collective-permute-start | bytes 368648 | tf_op jit(solution)/shard_map/ppermute | solution.py:387
  90.7 6.0 %collective-permute-start.23 = (bf16[80,768]{1,0:T(8,128)(2,1)S(1)}, bf16[80,768]{1,0:T(8,128)(2,1)S(1)}, u32[]{:S(2)}, u32[]{:S(2)}) collective-permute-start(bf16[80,768]{1,0:T(8,128)(2,1)S(1)} %get-tuple-element.94), channel_id=1, source_target_pairs={{0,33},{1,32},{2,35},{3,34},{4,37},{5,36},{6,39},{7,38},{8,41},{9,... | collective-permute-start | bytes 368648 | tf_op jit(solution)/shard_map/ppermute | solution.py:387
  92.1 7.5 %collective-permute-start.24 = (bf16[80,768]{1,0:T(8,128)(2,1)S(1)}, bf16[80,768]{1,0:T(8,128)(2,1)S(1)}, u32[]{:S(2)}, u32[]{:S(2)}) collective-permute-start(bf16[80,768]{1,0:T(8,128)(2,1)S(1)} %get-tuple-element.95), channel_id=1, source_target_pairs={{0,37},{1,36},{2,39},{3,38},{4,33},{5,32},{6,35},{7,34},{8,45},{9,... | collective-permute-start | bytes 368648 | tf_op jit(solution)/shard_map/ppermute | solution.py:387
